TPU v7x, 32 devices: a whole 2x2x4 slice. The times are simulated.
32 devices in a mesh: batch: 4 (over y, x), seg: 8 (over z, core).
Axes of the slice: x: 2, y: 2, z: 4, core: 2. Of those that a mesh axis runs over, the one named last changes fastest.
Arguments:
- hidden: bfloat16 [2, 4, 4, 8, 128, 768], P(None, 'batch', None, 'seg'), may hold values from -6 to 6
- seg_doc: int32 [2, 4, 32], P(None, 'batch'), may hold values from 0 to 3, as said below
- seg_attn: bfloat16 [768, 3072], P('seg')
- seg_up: bfloat16 [768, 3072], P('seg'), may hold values from -0.21875 to 0.21875
- seg_down: bfloat16 [768, 3072], P('seg'), may hold values from -0.109375 to 0.109375
- seg_vec: bfloat16 [768, 12], P('seg')
- cross_attn: bfloat16 [768, 3072], P('seg')
- cross_up: bfloat16 [768, 3072], P('seg'), may hold values from -0.21875 to 0.21875
- cross_down: bfloat16 [768, 3072], P('seg'), may hold values from -0.109375 to 0.109375
- cross_vec: bfloat16 [768, 12], P('seg')
- tok_cot: bfloat16 [2, 4, 4, 8, 128, 768], P(None, 'batch', None, 'seg'), may hold values from -6 to 6
- cls_cot: bfloat16 [2, 4, 4, 8, 768], P(None, 'batch', None, 'seg'), may hold values from -6 to 6
Outputs:
- tok_out: bfloat16 [2, 4, 4, 8, 128, 768], P(None, 'batch', None, 'seg')
- cls_out: bfloat16 [2, 4, 4, 8, 768], P(None, 'batch', None, 'seg')
- hidden_grad: float32 [2, 4, 4, 8, 128, 768], P(None, 'batch', None, 'seg')
- seg_attn_grad: float32 [768, 3072], P('seg')
- seg_up_grad: float32 [768, 3072], P('seg')
- seg_down_grad: float32 [768, 3072], P('seg')
- seg_vec_grad: float32 [768, 12], P('seg')
- cross_attn_grad: float32 [768, 3072], P('seg')
- cross_up_grad: float32 [768, 3072], P('seg')
- cross_down_grad: float32 [768, 3072], P('seg')
- cross_vec_grad: float32 [768, 12], P('seg')
Inputs may be any that keep to these rules, and one draw needn't show every extreme that they name: `seg_doc`: within one micro-batch and group, document numbers start at 0 and never fall; the segments fall into aligned blocks of 32, each block one document or four documents of 8; both kinds occur in every draw.
All inputs are finite; a program needn't handle non-finite values.
Results may differ from a plain program's by a relative error of at most 0.015.
Values may be sent and summed in bfloat16 or wider, within the bound.
No kernel may reach another device: no remote copies, remote signals or barrier semaphores. Data moves between devices by JAX's collectives and lax.ppermute only.
A program may use at most 256 MiB of HBM per device.

v0:
```python
from functools import partial

import jax
import jax.numpy as jnp
from jax import lax
from jax.sharding import PartitionSpec as P

HEADS = 12
HEAD_DIM = 64
SEG_LEN = 128


NEG_FILL = -1e30
LN_EPS = 1e-05


def layer_norm(rows, gain, shift):
    centred = rows - jnp.mean(rows, -1, keepdims=True)
    spread = jnp.mean(centred * centred, -1, keepdims=True)
    return centred * lax.rsqrt(spread + LN_EPS) * gain + shift


def gelu_exact(value):
    return jax.nn.gelu(value, approximate=False)


def contract_rows(left, right):
    return lax.dot_general(
        left, right, (((0,), (0,)), ((), ())), preferred_element_type=jnp.float32
    )


def contract_cols(left, right):
    return lax.dot_general(
        left, right, (((1,), (1,)), ((), ())), preferred_element_type=jnp.float32
    )


def softmax_rows(scores):
    top = jnp.max(scores, -1, keepdims=True)
    expo = jnp.exp(scores - top)
    total = jnp.sum(expo, -1, keepdims=True)
    return (expo / total, top + jnp.log(total))


def seg_attend(qkv_low):
    parts = qkv_low.reshape(-1, SEG_LEN, 3, HEADS, HEAD_DIM)
    query, keys, values = (parts[:, :, 0], parts[:, :, 1], parts[:, :, 2])
    scores = jnp.einsum(
        "slhe,smhe->shlm", query, keys, preferred_element_type=jnp.float32
    ) * HEAD_DIM ** (-0.5)
    probs, lse = softmax_rows(scores)
    mixed = jnp.einsum(
        "shlm,smhe->slhe", probs.astype(jnp.bfloat16), values, preferred_element_type=jnp.float32
    )
    return (mixed.astype(jnp.bfloat16).reshape(qkv_low.shape[0], -1), lse)


def seg_attend_back(mixed_grad, qkv_low, lse):
    scale = HEAD_DIM ** (-0.5)
    parts = qkv_low.reshape(-1, SEG_LEN, 3, HEADS, HEAD_DIM)
    query, keys, values = (parts[:, :, 0], parts[:, :, 1], parts[:, :, 2])
    scores = jnp.einsum("slhe,smhe->shlm", query, keys, preferred_element_type=jnp.float32) * scale
    probs = jnp.exp(scores - lse)
    out_grad = mixed_grad.reshape(-1, SEG_LEN, HEADS, HEAD_DIM)
    value_grad = jnp.einsum(
        "shlm,slhe->smhe", probs.astype(jnp.bfloat16), out_grad, preferred_element_type=jnp.float32
    )
    prob_grad = jnp.einsum("slhe,smhe->shlm", out_grad, values, preferred_element_type=jnp.float32)
    score_grad = (probs * (prob_grad - jnp.sum(prob_grad * probs, -1, keepdims=True))).astype(
        jnp.bfloat16
    )
    query_grad = (
        jnp.einsum("shlm,smhe->slhe", score_grad, keys, preferred_element_type=jnp.float32) * scale
    )
    key_grad = (
        jnp.einsum("shlm,slhe->smhe", score_grad, query, preferred_element_type=jnp.float32) * scale
    )
    stacked = jnp.stack([query_grad, key_grad, value_grad], 2).astype(jnp.bfloat16)
    return stacked.reshape(qkv_low.shape)


def cross_scores(query, keys, doc_own, doc_all):
    same = doc_own[:, None] == doc_all[None, :]
    raw = jnp.einsum(
        "lhe,mhe->hlm", query, keys, preferred_element_type=jnp.float32
    ) * HEAD_DIM ** (-0.5)
    return jnp.where(same[None], raw, NEG_FILL)


def cross_attend(qkv_low, doc_own, doc_all):
    rows = qkv_low.shape[0]
    width = qkv_low.shape[1] // 3
    query = qkv_low[:, :width].reshape(rows, HEADS, HEAD_DIM)
    pair = qkv_low[:, width:].reshape(rows, 1, 2 * width)
    shared = lax.all_gather(pair, "seg", axis=1, tiled=True).reshape(-1, 2 * width)
    keys = shared[:, :width].reshape(-1, HEADS, HEAD_DIM)
    values = shared[:, width:].reshape(-1, HEADS, HEAD_DIM)
    probs, lse = softmax_rows(cross_scores(query, keys, doc_own, doc_all))
    mixed = jnp.einsum(
        "hlm,mhe->lhe", probs.astype(jnp.bfloat16), values, preferred_element_type=jnp.float32
    )
    return (mixed.astype(jnp.bfloat16).reshape(rows, width), (shared, lse))


def cross_attend_back(mixed_grad, qkv_low, kept, doc_own, doc_all):
    shared, lse = kept
    scale = HEAD_DIM ** (-0.5)
    rows = qkv_low.shape[0]
    width = qkv_low.shape[1] // 3
    query = qkv_low[:, :width].reshape(rows, HEADS, HEAD_DIM)
    keys = shared[:, :width].reshape(-1, HEADS, HEAD_DIM)
    values = shared[:, width:].reshape(-1, HEADS, HEAD_DIM)
    probs = jnp.exp(cross_scores(query, keys, doc_own, doc_all) - lse)
    out_grad = mixed_grad.reshape(rows, HEADS, HEAD_DIM)
    value_grad = jnp.einsum(
        "hlm,lhe->mhe", probs.astype(jnp.bfloat16), out_grad, preferred_element_type=jnp.float32
    )
    prob_grad = jnp.einsum("lhe,mhe->hlm", out_grad, values, preferred_element_type=jnp.float32)
    score_grad = (probs * (prob_grad - jnp.sum(prob_grad * probs, -1, keepdims=True))).astype(
        jnp.bfloat16
    )
    query_grad = (
        jnp.einsum("hlm,mhe->lhe", score_grad, keys, preferred_element_type=jnp.float32) * scale
    )
    key_grad = (
        jnp.einsum("hlm,lhe->mhe", score_grad, query, preferred_element_type=jnp.float32) * scale
    )
    partial_sums = jnp.concatenate([key_grad.reshape(-1, width), value_grad.reshape(-1, width)], 1)
    partial_sums = partial_sums.reshape(rows, -1, 2 * width)
    own_sums = lax.psum_scatter(partial_sums, "seg", scatter_dimension=1, tiled=True)
    return jnp.concatenate(
        [query_grad.reshape(rows, width), own_sums.reshape(rows, 2 * width)], 1
    ).astype(jnp.bfloat16)


def vec_columns(
    bias_grad, out_bias, gain_one, shift_one, down_bias, gain_two, shift_two, up_bias, width
):
    columns = jnp.stack(
        [
            bias_grad[:width],
            bias_grad[2 * width :],
            out_bias,
            gain_one,
            shift_one,
            down_bias,
            gain_two,
            shift_two,
        ],
        1,
    )
    return jnp.concatenate([columns, up_bias], 1)


def block_forward(flat, full, attend):
    attn, up_proj, down_proj, vec = full
    vecf = vec.astype(jnp.float32)
    width = attn.shape[0]
    low_in = flat.astype(jnp.bfloat16)
    qkv = jnp.dot(low_in, attn[:, : 3 * width], preferred_element_type=jnp.float32)
    bias = jnp.concatenate([vecf[:, 0], jnp.zeros_like(vecf[:, 0]), vecf[:, 1]])
    qkv_low = (qkv + bias).astype(jnp.bfloat16)
    mixed, kept = attend(qkv_low)
    first_sum = (
        flat + jnp.dot(mixed, attn[:, 3 * width :], preferred_element_type=jnp.float32) + vecf[:, 2]
    )
    normed = layer_norm(first_sum, vecf[:, 3], vecf[:, 4])
    normed_low = normed.astype(jnp.bfloat16)
    inner = jnp.dot(normed_low, up_proj, preferred_element_type=jnp.float32) + vecf[
        :, 8:
    ].T.reshape(-1)
    act_low = gelu_exact(inner).astype(jnp.bfloat16)
    second_sum = normed + contract_cols(act_low, down_proj) + vecf[:, 5]
    result = layer_norm(second_sum, vecf[:, 6], vecf[:, 7])
    return (
        result,
        (low_in, qkv_low, kept, mixed, first_sum, normed_low, inner, act_low, second_sum),
    )


def block_backward(out_grad, full, saved, attend_back):
    attn, up_proj, down_proj, vec = full
    vecf = vec.astype(jnp.float32)
    width = attn.shape[0]
    low_in, qkv_low, kept, mixed, first_sum, normed_low, inner, act_low, second_sum = saved
    norm_out, second_back = jax.vjp(layer_norm, second_sum, vecf[:, 6], vecf[:, 7])
    second_grad, gain_two, shift_two = second_back(out_grad)
    branch_low = second_grad.astype(jnp.bfloat16)
    down_bias = jnp.sum(branch_low.astype(jnp.float32), 0)
    down_grad = contract_rows(branch_low, act_low)
    act_grad = jnp.dot(branch_low, down_proj, preferred_element_type=jnp.float32)
    inner_out, gelu_back = jax.vjp(gelu_exact, inner)
    inner_low = gelu_back(act_grad)[0].astype(jnp.bfloat16)
    up_bias = jnp.sum(inner_low.astype(jnp.float32), 0).reshape(-1, width).T
    up_grad = contract_rows(normed_low, inner_low)
    normed_grad = second_grad + contract_cols(inner_low, up_proj)
    norm_first, first_back = jax.vjp(layer_norm, first_sum, vecf[:, 3], vecf[:, 4])
    first_grad, gain_one, shift_one = first_back(normed_grad)
    attn_low = first_grad.astype(jnp.bfloat16)
    out_bias = jnp.sum(attn_low.astype(jnp.float32), 0)
    out_weight = contract_rows(mixed, attn_low)
    mixed_low = contract_cols(attn_low, attn[:, 3 * width :]).astype(jnp.bfloat16)
    qkv_grad = attend_back(mixed_low, qkv_low, kept)
    qkv_weight = contract_rows(low_in, qkv_grad)
    bias_grad = jnp.sum(qkv_grad.astype(jnp.float32), 0)
    flat_grad = first_grad + contract_cols(qkv_grad, attn[:, : 3 * width])
    vec_grad = vec_columns(
        bias_grad, out_bias, gain_one, shift_one, down_bias, gain_two, shift_two, up_bias, width
    )
    attn_grad = jnp.concatenate([qkv_weight, out_weight], 1)
    return (flat_grad, (attn_grad, up_grad, down_grad, vec_grad))


def add_sets(stored, fresh):
    if stored is None:
        return fresh
    return jax.tree.map(jnp.add, stored, fresh)


def local(
    hidden,
    seg_doc,
    seg_attn,
    seg_up,
    seg_down,
    seg_vec,
    cross_attn,
    cross_up,
    cross_down,
    cross_vec,
    tok_cot,
    cls_cot,
):
    got = (
        lax.all_gather(seg_attn, "seg", axis=0, tiled=True),
        lax.all_gather(seg_up, "seg", axis=0, tiled=True),
        lax.all_gather(seg_down, "seg", axis=0, tiled=True),
        lax.all_gather(seg_vec, "seg", axis=0, tiled=True),
        lax.all_gather(cross_attn, "seg", axis=0, tiled=True),
        lax.all_gather(cross_up, "seg", axis=0, tiled=True),
        lax.all_gather(cross_down, "seg", axis=0, tiled=True),
        lax.all_gather(cross_vec, "seg", axis=0, tiled=True),
    )
    seg_full = got[:4]
    cross_full = got[4:]
    micro = hidden.shape[0]
    segments = hidden.shape[2]
    width = hidden.shape[5]
    parts = lax.axis_size("seg")
    place = lax.axis_index("seg")
    tok_list, cls_list, grad_list = ([], [], [])
    seg_store = None
    cross_store = None
    for step in range(micro):
        doc_all = seg_doc[step, 0]
        doc_own = lax.dynamic_slice_in_dim(doc_all.reshape(-1, parts), place, 1, 1)[:, 0]
        flat = hidden[step, 0, :, 0].reshape(segments * SEG_LEN, width)
        seg_result, seg_saved = block_forward(flat, seg_full, seg_attend)
        cls_rows = seg_result.reshape(segments, SEG_LEN, width)[:, 0, :]
        cls_top = cls_cot[step, 0, :, 0].astype(jnp.float32)
        tok_list.append(seg_result.reshape(segments, SEG_LEN, width).astype(jnp.bfloat16))
        cross_fwd = partial(cross_attend, doc_own=doc_own, doc_all=doc_all)
        cross_bwd = partial(cross_attend_back, doc_own=doc_own, doc_all=doc_all)
        cross_result, cross_saved = block_forward(cls_rows, cross_full, cross_fwd)
        cls_grad, cross_grads = block_backward(cls_top, cross_full, cross_saved, cross_bwd)
        cls_list.append(cross_result.astype(jnp.bfloat16))
        top_grad = tok_cot[step, 0, :, 0].astype(jnp.float32)
        top_grad = jnp.concatenate([top_grad[:, :1] + cls_grad[:, None, :], top_grad[:, 1:]], 1)
        flat_grad, seg_grads = block_backward(
            top_grad.reshape(-1, width), seg_full, seg_saved, seg_attend_back
        )
        grad_list.append(flat_grad.reshape(segments, SEG_LEN, width))
        seg_store = add_sets(seg_store, tuple(seg_grads))
        cross_store = add_sets(cross_store, tuple(cross_grads))
    both = (
        lax.psum_scatter(seg_store[0], "seg", scatter_dimension=0, tiled=True),
        lax.psum_scatter(seg_store[1], "seg", scatter_dimension=0, tiled=True),
        lax.psum_scatter(seg_store[2], "seg", scatter_dimension=0, tiled=True),
        lax.psum_scatter(seg_store[3], "seg", scatter_dimension=0, tiled=True),
        lax.psum_scatter(cross_store[0], "seg", scatter_dimension=0, tiled=True),
        lax.psum_scatter(cross_store[1], "seg", scatter_dimension=0, tiled=True),
        lax.psum_scatter(cross_store[2], "seg", scatter_dimension=0, tiled=True),
        lax.psum_scatter(cross_store[3], "seg", scatter_dimension=0, tiled=True),
    )
    seg_store = both[:4]
    cross_store = both[4:]
    summed = (
        lax.psum(seg_store[0].astype(jnp.bfloat16), "batch").astype(jnp.float32),
        lax.psum(seg_store[1].astype(jnp.bfloat16), "batch").astype(jnp.float32),
        lax.psum(seg_store[2].astype(jnp.bfloat16), "batch").astype(jnp.float32),
        lax.psum(seg_store[3].astype(jnp.bfloat16), "batch").astype(jnp.float32),
        lax.psum(cross_store[0].astype(jnp.bfloat16), "batch").astype(jnp.float32),
        lax.psum(cross_store[1].astype(jnp.bfloat16), "batch").astype(jnp.float32),
        lax.psum(cross_store[2].astype(jnp.bfloat16), "batch").astype(jnp.float32),
        lax.psum(cross_store[3].astype(jnp.bfloat16), "batch").astype(jnp.float32),
    )
    tok_out = jnp.stack(tok_list)[:, None, :, None]
    cls_out = jnp.stack(cls_list)[:, None, :, None]
    hidden_grad = jnp.stack(grad_list)[:, None, :, None]
    return (
        tok_out,
        cls_out,
        hidden_grad,
        summed[0],
        summed[1],
        summed[2],
        summed[3],
        summed[4],
        summed[5],
        summed[6],
        summed[7],
    )


def solution(mesh):
    in_specs = (
        P(None, "batch", None, "seg", None, None),
        P(None, "batch", None),
        P("seg", None),
        P("seg", None),
        P("seg", None),
        P("seg", None),
        P("seg", None),
        P("seg", None),
        P("seg", None),
        P("seg", None),
        P(None, "batch", None, "seg", None, None),
        P(None, "batch", None, "seg", None),
    )
    out_specs = (
        P(None, "batch", None, "seg", None, None),
        P(None, "batch", None, "seg", None),
        P(None, "batch", None, "seg", None, None),
        P("seg", None),
        P("seg", None),
        P("seg", None),
        P("seg", None),
        P("seg", None),
        P("seg", None),
        P("seg", None),
        P("seg", None),
    )
    return jax.shard_map(local, mesh=mesh, in_specs=in_specs, out_specs=out_specs, check_vma=False)
```

profile of v0, /device:TPU:0, one launch (start us, length us, event | category | flops | bytes accessed | tf_op | source)
XLA Modules:
  0.0 1151.2 jit_solution(10574348013985345337)
XLA Ops:
  11.2 15.7 %all-gather.2 = bf16[8,96,12]{1,2,0:T(8,128)(2,1)S(1)} all-gather(bf16[1,96,12]{1,2,0:T(8,128)(2,1)S(1)} %bitcast.360), channel_id=1, replica_groups=mesh['batch'=4,'seg'=8] {'seg'}, dimensions={0}, use_global_device_ids=true | all-gather | bytes 20736 | tf_op jit(solution)/shard_map/all_gather | solution.py:239
  27.2 14.2 %all-gather.3 = bf16[8,96,12]{1,2,0:T(8,128)(2,1)S(1)} all-gather(bf16[1,96,12]{1,2,0:T(8,128)(2,1)S(1)} %bitcast.361), channel_id=1, replica_groups=mesh['batch'=4,'seg'=8] {'seg'}, dimensions={0}, use_global_device_ids=true | all-gather | bytes 20736 | tf_op jit(solution)/shard_map/all_gather | solution.py:243
  44.3 20.1 %all-gather.11.cloned.1.call-done = bf16[768,3072]{1,0:T(8,128)(2,1)} async-done(((bf16[96,3072]{1,0:T(8,128)(2,1)}), bf16[768,3072]{1,0:T(8,128)(2,1)}) %all-gather.11.cloned.1.call-update) | async-done | bytes 4718608 | tf_op jit(solution)/shard_map/all_gather | solution.py:236
  99.8 16.8 %all-gather.13.cloned.1.call-done = bf16[768,3072]{1,0:T(8,128)(2,1)} async-done(((bf16[96,3072]{1,0:T(8,128)(2,1)}), bf16[768,3072]{1,0:T(8,128)(2,1)}) %all-gather.13.cloned.1.call-update) | async-done | bytes 4718608 | tf_op jit(solution)/shard_map/all_gather | solution.py:237
  124.1 34.8 %multiply_convert_fusion.1 = (bf16[512,3072]{1,0:T(8,128)(2,1)}, f32[512,3072]{1,0:T(8,128)}, bf16[512,3072]{1,0:T(8,128)(2,1)}, f32[512,3072]{1,0:T(8,128)}, f32[512,3072]{1,0:T(8,128)}) fusion(f32[3072]{0:T(1024)S(1)} %add.436, f32[512,3072]{1,0:T(8,128)S(1)} %fusion.218, bf16[768,3072]{1,0:T(8,128)(2,1)S(1)} %copy-done.183, ...), kind=kOutput, calls=%fused_computation.23 | convolution fusion | flops 2625503232 | bytes 37771264 | tf_op jit(solution)/shard_map/dot_general | solution.py:170
  158.9 9.8 all-gather.15.cloned.1.call-done
  168.8 6.2 fusion.251
  180.9 39.9 %all-gather.17.cloned.1.call-done = bf16[768,3072]{1,0:T(8,128)(2,1)} async-done(((bf16[96,3072]{1,0:T(8,128)(2,1)}), bf16[768,3072]{1,0:T(8,128)(2,1)}) %all-gather.17.cloned.1.call-update) | async-done | bytes 4718608 | tf_op jit(solution)/shard_map/all_gather | solution.py:240
  227.6 14.3 %all-gather.1 = bf16[4,12288]{1,0:T(4,128)(2,1)S(1)} all-gather(bf16[4,1536]{1,0:T(4,128)(2,1)S(1)} %slice.320), channel_id=3, replica_groups=mesh['batch'=4,'seg'=8] {'seg'}, dimensions={1}, use_global_device_ids=true | all-gather | bytes 110592 | tf_op jit(solution)/shard_map/all_gather | solution.py:96
  246.6 26.8 %all-gather.19.cloned.1.call-done = bf16[768,3072]{1,0:T(8,128)(2,1)} async-done(((bf16[96,3072]{1,0:T(8,128)(2,1)}), bf16[768,3072]{1,0:T(8,128)(2,1)}) %all-gather.19.cloned.1.call-update) | async-done | bytes 4718608 | tf_op jit(solution)/shard_map/all_gather | solution.py:241
  276.7 48.8 %all-gather.21.cloned.1.call-done = bf16[768,3072]{1,0:T(8,128)(2,1)} async-done(((bf16[96,3072]{1,0:T(8,128)(2,1)}), bf16[768,3072]{1,0:T(8,128)(2,1)}) %all-gather.21.cloned.1.call-update) | async-done | bytes 4718608 | tf_op jit(solution)/shard_map/all_gather | solution.py:242
  330.0 14.1 %all-gather = bf16[4,12288]{1,0:T(4,128)(2,1)S(1)} all-gather(bf16[4,1536]{1,0:T(4,128)(2,1)S(1)} %slice-done.2), channel_id=2, replica_groups=mesh['batch'=4,'seg'=8] {'seg'}, dimensions={1}, use_global_device_ids=true | all-gather | bytes 110592 | tf_op jit(solution)/shard_map/all_gather | solution.py:96
  411.8 41.1 %all-reduce.9 = (bf16[4,8,1536]{2,0,1:T(4,128)(2,1)S(1)}, bf16[4,8,1536]{2,0,1:T(4,128)(2,1)}) all-reduce(f32[4,8,1536]{2,0,1:T(4,128)S(1)} %copy.218, f32[4,8,1536]{2,0,1:T(4,128)} %copy.236), channel_id=4, replica_groups=mesh['batch'=4,'seg'=8] {'seg'}, use_global_device_ids=true, to_apply=%region_29.30.clone | all-reduce | flops 98304 | bytes 589824
  489.4 16.2 %convert_reduce_fusion.1 = (f32[3072]{0:T(1024)S(1)}, bf16[512,3072]{1,0:T(8,128)(2,1)}, f32[3072]{0:T(1024)S(1)}, bf16[512,3072]{1,0:T(8,128)(2,1)}) fusion(f32[512,3072]{1,0:T(8,128)} %get-tuple-element.158, f32[512,3072]{1,0:T(8,128)} %get-tuple-element.228, f32[3072]{0:T(1024)S(1)} %copy-done.163, f32[512,3072]{1,0:T(8,128)S(1)} %fusion.260, ...), kind=kOutput, calls=%fused_computation.7 | convolution fusion | flops 2469390336 | bytes 43290624 | tf_op jit(solution)/shard_map/dot_general | solution.py:192
  516.9 6.6 add_add_fusion.9
  576.0 9.7 copy.259
  594.3 76.9 %reduce-scatter.19.cloned.1.call-done = f32[96,3072]{1,0:T(8,128)} async-done(((f32[768,3072]{1,0:T(8,128)}), f32[96,3072]{1,0:T(8,128)}) %reduce-scatter.19.cloned.1.call-update) | async-done | bytes 1179664 | tf_op jit(solution)/shard_map/reduce_scatter | solution.py:281
  673.4 97.9 %reduce-scatter.17.cloned.1.call-done = f32[96,3072]{1,0:T(8,128)} async-done(((f32[768,3072]{1,0:T(8,128)}), f32[96,3072]{1,0:T(8,128)}) %reduce-scatter.17.cloned.1.call-update) | async-done | bytes 1179664 | tf_op jit(solution)/shard_map/reduce_scatter | solution.py:279
  773.5 98.1 %reduce-scatter.15.cloned.1.call-done = f32[96,3072]{1,0:T(8,128)} async-done(((f32[768,3072]{1,0:T(8,128)}), f32[96,3072]{1,0:T(8,128)}) %reduce-scatter.15.cloned.1.call-update) | async-done | bytes 1179664 | tf_op jit(solution)/shard_map/reduce_scatter | solution.py:278
  873.7 97.9 %reduce-scatter.25.cloned.1.call-done = f32[96,3072]{1,0:T(8,128)} async-done(((f32[768,3072]{1,0:T(8,128)}), f32[96,3072]{1,0:T(8,128)}) %reduce-scatter.25.cloned.1.call-update) | async-done | bytes 1179664
  987.0 15.9 %reduce-scatter.29.cloned.1.call-done = f32[96,12]{1,0:T(8,128)} async-done(((f32[768,12]{1,0:T(8,128)}), f32[96,12]{1,0:T(8,128)}) %reduce-scatter.29.cloned.1.call-update) | async-done | bytes 4624
  1003.8 30.2 %reduce-scatter.27.cloned.1.call-done = f32[96,12]{1,0:T(8,128)} async-done(((f32[768,12]{1,0:T(8,128)}), f32[96,12]{1,0:T(8,128)}) %reduce-scatter.27.cloned.1.call-update) | async-done | bytes 4624
  1034.9 10.1 all-reduce.3
  1046.2 88.8 %all-reduce.8.cloned.1.call-done = (bf16[96,3072]{0,1:T(8,128)(2,1)}, bf16[96,3072]{1,0:T(8,128)(2,1)}, bf16[96,3072]{1,0:T(8,128)(2,1)}, bf16[96,3072]{1,0:T(8,...) async-done(((bf16[96,3072]{0,1:T(8,128)(2,1)}, bf16[96,3072]{1,0:T(8,128)(2,1)}, bf16[96,3072]{1,0:T(8,128)(2,1)}, bf16[96,3072]{1,0:T(8,128)(2,1)}, ...) | async-done | bytes 3538960 | tf_op jit(solution)/shard_map/psum | solution.py:289
  (710 shorter events, 282.5 us)
Async XLA Ops:
  7.2 57.2 %all-gather.11.cloned.1.call-start = ((), (), s32[]{:S(2)}) async-start(), calls=%async_computation.8 | async-start | bytes 5308416 | tf_op jit(solution)/shard_map/all_gather | solution.py:236
  7.9 108.6 %all-gather.13.cloned.1.call-start = ((), (), s32[]{:S(2)}) async-start(), calls=%async_computation.9 | async-start | bytes 5308416 | tf_op jit(solution)/shard_map/all_gather | solution.py:237
  8.7 160.1 %all-gather.15.cloned.1.call-start = ((), (), s32[]{:S(2)}) async-start(), calls=%async_computation.10 | async-start | bytes 5308416 | tf_op jit(solution)/shard_map/all_gather | solution.py:238
  9.4 211.4 %all-gather.17.cloned.1.call-start = ((), (), s32[]{:S(2)}) async-start(), calls=%async_computation.11 | async-start | bytes 5308416 | tf_op jit(solution)/shard_map/all_gather | solution.py:240
  10.0 263.4 %all-gather.19.cloned.1.call-start = ((), (), s32[]{:S(2)}) async-start(), calls=%async_computation.12 | async-start | bytes 5308416 | tf_op jit(solution)/shard_map/all_gather | solution.py:241
  10.6 314.8 %all-gather.21.cloned.1.call-start = ((), (), s32[]{:S(2)}) async-start(), calls=%async_computation.13 | async-start | bytes 5308416 | tf_op jit(solution)/shard_map/all_gather | solution.py:242
  11.2 578.8 %reduce-scatter.23.cloned.1.call-start = ((), (), s32[]{:S(2)}) async-start(), calls=%async_computation.18 | async-start | bytes 10616832 | tf_op jit(solution)/shard_map/reduce_scatter | solution.py:283
  27.1 148.2 %copy-start.66 = (f32[768]{0:T(1024)}, f32[768]{0:T(1024)S(1)}, u32[]{:S(2)}) copy-start(f32[768]{0:T(1024)S(1)} %get-tuple-element.77) | copy-start | bytes 9220
  27.1 148.2 %copy-start.87 = (f32[768]{0:T(1024)}, f32[768]{0:T(1024)S(1)}, u32[]{:S(2)}) copy-start(f32[768]{0:T(1024)S(1)} %get-tuple-element.76) | copy-start | bytes 9220
  27.1 151.5 %copy-start.92 = (f32[768]{0:T(1024)}, f32[768]{0:T(1024)S(1)}, u32[]{:S(2)}) copy-start(f32[768]{0:T(1024)S(1)} %get-tuple-element.73) | copy-start | bytes 9220
  42.1 202.5 %copy-start.117 = (f32[768]{0:T(1024)}, f32[768]{0:T(1024)S(1)}, u32[]{:S(2)}) copy-start(f32[768]{0:T(1024)S(1)} %get-tuple-element.70) | copy-start | bytes 9220
  42.1 283.3 %copy-start.115 = (f32[768]{0:T(1024)}, f32[768]{0:T(1024)S(1)}, u32[]{:S(2)}) copy-start(f32[768]{0:T(1024)S(1)} %get-tuple-element.67) | copy-start | bytes 9220
  43.7 229.7 %copy-start.86 = (f32[3072]{0:T(1024)}, f32[3072]{0:T(1024)S(1)}, u32[]{:S(2)}) copy-start(f32[3072]{0:T(1024)S(1)} %add.468) | copy-start | bytes 36868
  365.1 227.1 %reduce-scatter.21.cloned.1.call-start = ((), (), s32[]{:S(2)}) async-start(), calls=%async_computation.17 | async-start | bytes 10616832 | tf_op jit(solution)/shard_map/reduce_scatter | solution.py:282
  380.1 291.1 %reduce-scatter.19.cloned.1.call-start = ((), (), s32[]{:S(2)}) async-start(), calls=%async_computation.16 | async-start | bytes 10616832 | tf_op jit(solution)/shard_map/reduce_scatter | solution.py:281
  462.9 308.4 %reduce-scatter.17.cloned.1.call-start = ((), (), s32[]{:S(2)}) async-start(), calls=%async_computation.15 | async-start | bytes 10616832 | tf_op jit(solution)/shard_map/reduce_scatter | solution.py:279
  484.5 387.0 %reduce-scatter.15.cloned.1.call-start = ((), (), s32[]{:S(2)}) async-start(), calls=%async_computation.14 | async-start | bytes 10616832 | tf_op jit(solution)/shard_map/reduce_scatter | solution.py:278
  516.4 455.2 %reduce-scatter.25.cloned.1.call-start = ((), (), s32[]{:S(2)}) async-start(), calls=%async_computation.19 | async-start | bytes 10616832
  585.8 417.1 %reduce-scatter.29.cloned.1.call-start = ((), (), s32[]{:S(2)}) async-start(), calls=%async_computation.21 | async-start | bytes 442368
  588.0 446.0 %reduce-scatter.27.cloned.1.call-start = ((), (), s32[]{:S(2)}) async-start(), calls=%async_computation.20 | async-start | bytes 442368
  589.6 545.4 %all-reduce.8.cloned.1.call-start = ((), (), s32[]{:S(2)}) async-start(), calls=%async_computation.22 | async-start | bytes 7471104 | tf_op jit(solution)/shard_map/psum | solution.py:289
  873.7 100.4 %copy-start.132 = (bf16[1,4,768]{2,1,0:T(4,128)(2,1)S(1)}, bf16[1,4,768]{2,1,0:T(4,128)(2,1)}, u32[]{:S(2)}) copy-start(bf16[1,4,768]{2,1,0:T(4,128)(2,1)} %get-tuple-element.187) | copy-start | bytes 18436
  873.7 101.0 %copy-start.44 = (bf16[512,768]{1,0:T(8,128)(2,1)S(1)}, bf16[512,768]{1,0:T(8,128)(2,1)}, u32[]{:S(2)}) copy-start(bf16[512,768]{1,0:T(8,128)(2,1)} %get-tuple-element.155) | copy-start | bytes 2359300
  873.7 101.0 %copy-start.45 = (bf16[512,768]{1,0:T(8,128)(2,1)S(1)}, bf16[512,768]{1,0:T(8,128)(2,1)}, u32[]{:S(2)}) copy-start(bf16[512,768]{1,0:T(8,128)(2,1)} %get-tuple-element.198) | copy-start | bytes 2359300
  (184 other events, 2229.8 us)
Sparse Core Ops, SparseCore 0:
  9.7 54.6 all-gather.10
  66.0 50.5 all-gather.12
  118.2 50.5 all-gather.14
  170.3 50.5 all-gather.16
  222.3 51.0 all-gather.18
  274.9 50.4 all-gather.20
  365.2 105.6 reduce-scatter.22
  473.2 97.8 reduce-scatter.20
  573.4 97.8 reduce-scatter.18
  673.4 97.8 reduce-scatter.16
  773.6 97.8 reduce-scatter.14
  873.7 97.8 reduce-scatter.24
  973.8 29.0 reduce-scatter.28
  1005.1 28.8 reduce-scatter.26
  1038.8 96.1 all-reduce.7
where the time goes:
time: 1160 us; the launch traced here: 1150 us
  waiting for transfers between devices  672 us (58%)
  matrix products  211 us (18%)
  blocking collectives  110 us (9%)
  local copies, waits for them, and re-layouts  77.8 us (7%)
  other arithmetic  61.7 us (5%)
  between operations  17.6 us (2%)
    unnamed x18, waiting for transfers between devices  148 us
    reduce_scatter x1, waiting for transfers between devices, local(): lax.psum_scatter(seg_store[1], 'seg', scatter_dimension=0, tiled=True)  98.1 us
    reduce_scatter x1, waiting for transfers between devices, local(): lax.psum_scatter(seg_store[2], 'seg', scatter_dimension=0, tiled=True)  97.9 us
    psum x1, waiting for transfers between devices, local(): lax.psum(seg_store[0].astype(jnp.bfloat16), 'batch').astype(jnp.float32)  88.8 us
    reduce_scatter x1, waiting for transfers between devices, local(): lax.psum_scatter(cross_store[0], 'seg', scatter_dimension=0, tiled=True)  76.9 us
    dot_general x16, matrix products, contract_cols(): lax.dot_general(left, right, (((1,), (1,)), ((), ())), preferred_element_...  53.9 us
    all_gather x1, waiting for transfers between devices, local(): lax.all_gather(cross_down, 'seg', axis=0, tiled=True)  48.8 us
    dot_general x4, matrix products, block_forward(): jnp.dot(normed_low, up_proj, preferred_element_type=jnp.float32)  46.1 us
  transfers between devices with their start and end apart: 15, of which 13 were waited for; matrix products, arithmetic and copies ran while one was open for 26% of the time, Pallas kernels for 0%

commit v1 on v0

v1 whole, which is shorter than its diff:
```python
from functools import partial

import jax
import jax.numpy as jnp
from jax import lax
from jax.experimental import pallas as pl
from jax.experimental.pallas import tpu as pltpu
from jax.sharding import PartitionSpec as P

HEADS = 12
HEAD_DIM = 64
SEG_LEN = 128
PAIRS = HEADS // 2
PAIR = 2 * HEAD_DIM

NEG_FILL = -1e30
LN_EPS = 1e-05
SCALE = HEAD_DIM ** (-0.5)
ROOT_HALF = 0.7071067811865476
PDF_AT_ZERO = 0.3989422804014327
BLOCK = 256
VMEM_LIMIT = 60 * 1024 * 1024

f32 = jnp.float32
bf16 = jnp.bfloat16


def dot_nn(left, right):
    return lax.dot_general(left, right, (((1,), (0,)), ((), ())), preferred_element_type=f32)


def dot_nt(left, right):
    return lax.dot_general(left, right, (((1,), (1,)), ((), ())), preferred_element_type=f32)


def dot_tn(left, right):
    return lax.dot_general(left, right, (((0,), (0,)), ((), ())), preferred_element_type=f32)


def normalise(rows):
    centred = rows - jnp.mean(rows, -1, keepdims=True)
    spread = jnp.mean(centred * centred, -1, keepdims=True)
    inverse = lax.rsqrt(spread + LN_EPS)
    return centred * inverse, inverse


def norm_back(grad, unit, inverse, gain):
    scaled = grad * gain
    return inverse * (
        scaled
        - jnp.mean(scaled, -1, keepdims=True)
        - unit * jnp.mean(scaled * unit, -1, keepdims=True)
    )


def column_sum(rows):
    return jnp.sum(rows, 0, keepdims=True)


def gelu_parts(value):
    cdf = 0.5 * (1.0 + lax.erf(value * ROOT_HALF))
    pdf = PDF_AT_ZERO * jnp.exp(-0.5 * value * value)
    return value * cdf, cdf + value * pdf


def first_half(rows):
    return lax.broadcasted_iota(jnp.int32, (rows, PAIR), 1) < HEAD_DIM


def split_heads(rows, first):
    zero = jnp.zeros_like(rows)
    return jnp.concatenate([jnp.where(first, rows, zero), jnp.where(first, zero, rows)], 0)


def join_heads(stacked, first):
    rows = stacked.shape[0] // 2
    return jnp.where(first, stacked[:rows], stacked[rows:])


def pair_probs(query, keys, mask):
    scores = dot_nt(query, keys) * SCALE
    if mask is not None:
        scores = jnp.where(mask, scores, NEG_FILL)
    top = jnp.max(scores, -1, keepdims=True)
    expo = jnp.exp(scores - top)
    return expo * (1.0 / jnp.sum(expo, -1, keepdims=True))


def pair_forward(qkv_ref, out_ref, rows, pair, width, mask):
    first = first_half(rows.size)
    at = pair * PAIR
    query = split_heads(qkv_ref[rows, at : at + PAIR], first)
    keys = qkv_ref[rows, width + at : width + at + PAIR]
    values = qkv_ref[rows, 2 * width + at : 2 * width + at + PAIR]
    probs = pair_probs(query, keys, mask)
    mixed = join_heads(dot_nn(probs.astype(bf16), values), first)
    out_ref[rows, at : at + PAIR] = mixed.astype(bf16)


def pair_backward(qkv_ref, grad_ref, out_ref, rows, pair, width, mask):
    first = first_half(rows.size)
    at = pair * PAIR
    query = split_heads(qkv_ref[rows, at : at + PAIR], first)
    keys = qkv_ref[rows, width + at : width + at + PAIR]
    values = qkv_ref[rows, 2 * width + at : 2 * width + at + PAIR]
    out_grad = split_heads(grad_ref[rows, at : at + PAIR], first)
    probs = pair_probs(query, keys, mask)
    value_grad = dot_tn(probs.astype(bf16), out_grad)
    prob_grad = dot_nt(out_grad, values)
    score_grad = probs * (prob_grad - jnp.sum(prob_grad * probs, -1, keepdims=True))
    score_grad = score_grad.astype(bf16)
    query_grad = join_heads(dot_nn(score_grad, keys), first) * SCALE
    key_grad = dot_tn(score_grad, query) * SCALE
    out_ref[rows, at : at + PAIR] = query_grad.astype(bf16)
    out_ref[rows, width + at : width + at + PAIR] = key_grad.astype(bf16)
    out_ref[rows, 2 * width + at : 2 * width + at + PAIR] = value_grad.astype(bf16)


def qkv_bias(vec_ref):
    query = vec_ref[0:1, :]
    return jnp.concatenate([query, jnp.zeros_like(query), vec_ref[1:2, :]], 1)


def attn_fwd_kernel(x_ref, w_ref, vec_ref, qkv_ref, mixed_ref, sum_ref):
    width = x_ref.shape[1]
    rows = x_ref[...]
    qkv = dot_nn(rows, w_ref[:, : 3 * width]) + qkv_bias(vec_ref)
    qkv_ref[...] = qkv.astype(bf16)
    for start in range(0, x_ref.shape[0], SEG_LEN):
        for pair in range(PAIRS):
            pair_forward(qkv_ref, mixed_ref, pl.ds(start, SEG_LEN), pair, width, None)
    branch = dot_nn(mixed_ref[...], w_ref[:, 3 * width :])
    sum_ref[...] = rows.astype(f32) + branch + vec_ref[2:3, :]


def ffn_fwd_kernel(sum_ref, up_ref, down_ref, vec_ref, norm_ref, act_ref, slope_ref, second_ref, tok_ref, cls_ref):
    width = sum_ref.shape[1]
    unit, _ = normalise(sum_ref[...])
    normed = unit * vec_ref[3:4, :] + vec_ref[4:5, :]
    low = normed.astype(bf16)
    norm_ref[...] = low
    total = normed + vec_ref[5:6, :]
    for part in range(4):
        cols = pl.ds(part * width, width)
        inner = dot_nn(low, up_ref[:, cols]) + vec_ref[8 + part : 9 + part, :]
        act, slope = gelu_parts(inner)
        act = act.astype(bf16)
        act_ref[:, cols] = act
        slope_ref[:, cols] = slope.astype(bf16)
        total = total + dot_nt(act, down_ref[:, cols])
    second_ref[...] = total
    unit, _ = normalise(total)
    result = unit * vec_ref[6:7, :] + vec_ref[7:8, :]
    tok_ref[...] = result.astype(bf16)
    for index in range(sum_ref.shape[0] // SEG_LEN):
        cls_ref[0, index : index + 1, :] = result[index * SEG_LEN : index * SEG_LEN + 1, :]


def ffn_bwd_kernel(cot_ref, cls_ref, second_ref, sum_ref, slope_ref, up_ref, down_ref, vec_ref, branch_ref, inner_ref, first_ref, sums_ref):
    width = sum_ref.shape[1]

    @pl.when(pl.program_id(0) == 0)
    def _():
        sums_ref[...] = jnp.zeros_like(sums_ref)

    place = lax.broadcasted_iota(jnp.int32, (SEG_LEN, 1), 0) == 0
    parts = []
    for index in range(sum_ref.shape[0] // SEG_LEN):
        rows = cot_ref[index * SEG_LEN : (index + 1) * SEG_LEN, :].astype(f32)
        parts.append(rows + jnp.where(place, cls_ref[0, index : index + 1, :], 0.0))
    grad = jnp.concatenate(parts, 0)
    unit, inverse = normalise(second_ref[...])
    sums_ref[6:7, :] += column_sum(grad * unit)
    sums_ref[7:8, :] += column_sum(grad)
    second_grad = norm_back(grad, unit, inverse, vec_ref[6:7, :])
    branch = second_grad.astype(bf16)
    branch_ref[...] = branch
    sums_ref[5:6, :] += column_sum(branch.astype(f32))
    total = second_grad
    for part in range(4):
        cols = pl.ds(part * width, width)
        act_grad = dot_nn(branch, down_ref[:, cols])
        inner = (act_grad * slope_ref[:, cols].astype(f32)).astype(bf16)
        inner_ref[:, cols] = inner
        sums_ref[8 + part : 9 + part, :] += column_sum(inner.astype(f32))
        total = total + dot_nt(inner, up_ref[:, cols])
    unit, inverse = normalise(sum_ref[...])
    sums_ref[3:4, :] += column_sum(total * unit)
    sums_ref[4:5, :] += column_sum(total)
    first = norm_back(total, unit, inverse, vec_ref[3:4, :])
    first_ref[...] = first
    sums_ref[2:3, :] += column_sum(first.astype(bf16).astype(f32))


def attn_bwd_kernel(first_ref, qkv_ref, w_ref, low_ref, qkv_grad_ref, x_grad_ref, sums_ref, mixed_grad):
    width = first_ref.shape[1]

    @pl.when(pl.program_id(0) == 0)
    def _():
        sums_ref[...] = jnp.zeros_like(sums_ref)

    first = first_ref[...]
    low = first.astype(bf16)
    low_ref[...] = low
    mixed_grad[...] = dot_nt(low, w_ref[:, 3 * width :]).astype(bf16)
    for start in range(0, first_ref.shape[0], SEG_LEN):
        for pair in range(PAIRS):
            pair_backward(qkv_ref, mixed_grad, qkv_grad_ref, pl.ds(start, SEG_LEN), pair, width, None)
    qkv_grad = qkv_grad_ref[...]
    x_grad_ref[...] = first + dot_nt(qkv_grad, w_ref[:, : 3 * width])
    sums_ref[0:1, :] += column_sum(qkv_grad[:, :width].astype(f32))
    sums_ref[1:2, :] += column_sum(qkv_grad[:, 2 * width :].astype(f32))


def cross_kernel(
    x_ref, cot_ref, key_own_ref, key_all_ref, attn_ref, up_ref, down_ref, vec_ref,
    out_ref, x_grad_ref, low_in_ref, qkv_grad_ref, mixed_ref, attn_low_ref,
    norm_ref, inner_ref, branch_ref, act_ref, sums_ref,
    qkv_ref, mixed_grad, slope,
):
    width = x_ref.shape[1]
    count = x_ref.shape[0]
    rows = pl.ds(0, count)

    @pl.when(pl.program_id(0) == 0)
    def _():
        sums_ref[...] = jnp.zeros_like(sums_ref)

    same = key_own_ref[...] == key_all_ref[0]
    mask = jnp.concatenate([same, same], 0)
    entry = x_ref[...]
    low_in = entry.astype(bf16)
    low_in_ref[...] = low_in
    qkv = dot_nn(low_in, attn_ref[:, : 3 * width]) + qkv_bias(vec_ref)
    qkv_ref[...] = qkv.astype(bf16)
    for pair in range(PAIRS):
        pair_forward(qkv_ref, mixed_ref, rows, pair, width, mask)
    first_sum = entry + dot_nn(mixed_ref[...], attn_ref[:, 3 * width :]) + vec_ref[2:3, :]
    unit_one, inverse_one = normalise(first_sum)
    normed = unit_one * vec_ref[3:4, :] + vec_ref[4:5, :]
    low = normed.astype(bf16)
    norm_ref[...] = low
    total = normed + vec_ref[5:6, :]
    for part in range(4):
        cols = pl.ds(part * width, width)
        inner = dot_nn(low, up_ref[:, cols]) + vec_ref[8 + part : 9 + part, :]
        act, rate = gelu_parts(inner)
        act = act.astype(bf16)
        act_ref[:, cols] = act
        slope[:, cols] = rate
        total = total + dot_nt(act, down_ref[:, cols])
    unit_two, inverse_two = normalise(total)
    out_ref[...] = (unit_two * vec_ref[6:7, :] + vec_ref[7:8, :]).astype(bf16)

    grad = cot_ref[...].astype(f32)
    sums_ref[6:7, :] += column_sum(grad * unit_two)
    sums_ref[7:8, :] += column_sum(grad)
    second_grad = norm_back(grad, unit_two, inverse_two, vec_ref[6:7, :])
    branch = second_grad.astype(bf16)
    branch_ref[...] = branch
    sums_ref[5:6, :] += column_sum(branch.astype(f32))
    total = second_grad
    for part in range(4):
        cols = pl.ds(part * width, width)
        inner = (dot_nn(branch, down_ref[:, cols]) * slope[:, cols]).astype(bf16)
        inner_ref[:, cols] = inner
        sums_ref[8 + part : 9 + part, :] += column_sum(inner.astype(f32))
        total = total + dot_nt(inner, up_ref[:, cols])
    sums_ref[3:4, :] += column_sum(total * unit_one)
    sums_ref[4:5, :] += column_sum(total)
    first = norm_back(total, unit_one, inverse_one, vec_ref[3:4, :])
    attn_low = first.astype(bf16)
    attn_low_ref[...] = attn_low
    sums_ref[2:3, :] += column_sum(attn_low.astype(f32))
    mixed_grad[...] = dot_nt(attn_low, attn_ref[:, 3 * width :]).astype(bf16)
    for pair in range(PAIRS):
        pair_backward(qkv_ref, mixed_grad, qkv_grad_ref, rows, pair, width, mask)
    qkv_grad = qkv_grad_ref[...]
    x_grad_ref[...] = first + dot_nt(qkv_grad, attn_ref[:, : 3 * width])
    sums_ref[0:1, :] += column_sum(qkv_grad[:, :width].astype(f32))
    sums_ref[1:2, :] += column_sum(qkv_grad[:, 2 * width :].astype(f32))


def row_spec(width, block=BLOCK):
    return pl.BlockSpec((block, width), lambda i: (i, 0))


def whole_spec(shape):
    return pl.BlockSpec(shape, lambda i: (0,) * len(shape), pipeline_mode=pl.Buffered(1))


def fixed_spec(shape):
    return pl.BlockSpec(shape, lambda i: (0,) * len(shape))


def params():
    return pltpu.CompilerParams(dimension_semantics=("arbitrary",), vmem_limit_bytes=VMEM_LIMIT)


def shaped(*dims, dtype=bf16):
    return jax.ShapeDtypeStruct(dims, dtype)


def cost(flops, nbytes, trans=0):
    return pl.CostEstimate(flops=int(flops), bytes_accessed=int(nbytes), transcendentals=int(trans))


def attn_forward(flat, attn, vec):
    rows, width = flat.shape
    return pl.pallas_call(
        attn_fwd_kernel,
        grid=(rows // BLOCK,),
        in_specs=[row_spec(width), whole_spec(attn.shape), whole_spec(vec.shape)],
        out_specs=[row_spec(3 * width), row_spec(width), row_spec(width)],
        out_shape=[shaped(rows, 3 * width), shaped(rows, width), shaped(rows, width, dtype=f32)],
        compiler_params=params(),
        cost_estimate=cost(2 * rows * width * (4 * width + 2 * SEG_LEN), rows * width * 14 + attn.size * 2),
        name="seg_attn_fwd",
    )(flat, attn, vec)


def ffn_forward(first_sum, up_proj, down_proj, vec):
    rows, width = first_sum.shape
    inner = up_proj.shape[1]
    per = BLOCK // SEG_LEN
    cls_spec = pl.BlockSpec((1, per, width), lambda i: (i, 0, 0))
    return pl.pallas_call(
        ffn_fwd_kernel,
        grid=(rows // BLOCK,),
        in_specs=[row_spec(width), whole_spec(up_proj.shape), whole_spec(down_proj.shape), whole_spec(vec.shape)],
        out_specs=[row_spec(width), row_spec(inner), row_spec(inner), row_spec(width), row_spec(width), cls_spec],
        out_shape=[
            shaped(rows, width), shaped(rows, inner), shaped(rows, inner), shaped(rows, width, dtype=f32),
            shaped(rows, width), shaped(rows // BLOCK, per, width, dtype=f32),
        ],
        compiler_params=params(),
        cost_estimate=cost(4 * rows * width * inner, rows * (width * 12 + inner * 4) + up_proj.size * 4, 2 * rows * inner),
        name="seg_ffn_fwd",
    )(first_sum, up_proj, down_proj, vec)


def ffn_backward(cot, cls_grad, second_sum, first_sum, slope, up_proj, down_proj, vec):
    rows, width = first_sum.shape
    inner = up_proj.shape[1]
    per = BLOCK // SEG_LEN
    cls_spec = pl.BlockSpec((1, per, width), lambda i: (i, 0, 0))
    return pl.pallas_call(
        ffn_bwd_kernel,
        grid=(rows // BLOCK,),
        in_specs=[
            row_spec(width), cls_spec, row_spec(width), row_spec(width), row_spec(inner),
            whole_spec(up_proj.shape), whole_spec(down_proj.shape), whole_spec(vec.shape),
        ],
        out_specs=[row_spec(width), row_spec(inner), row_spec(width), fixed_spec(vec.shape)],
        out_shape=[
            shaped(rows, width), shaped(rows, inner), shaped(rows, width, dtype=f32), shaped(*vec.shape, dtype=f32),
        ],
        compiler_params=params(),
        cost_estimate=cost(4 * rows * width * inner, rows * (width * 16 + inner * 4) + up_proj.size * 4),
        name="seg_ffn_bwd",
    )(cot, cls_grad, second_sum, first_sum, slope, up_proj, down_proj, vec)


def attn_backward(first_grad, qkv, attn):
    rows, width = first_grad.shape
    return pl.pallas_call(
        attn_bwd_kernel,
        grid=(rows // BLOCK,),
        in_specs=[row_spec(width), row_spec(3 * width), whole_spec(attn.shape)],
        out_specs=[row_spec(width), row_spec(3 * width), row_spec(width), fixed_spec((8, width))],
        out_shape=[
            shaped(rows, width), shaped(rows, 3 * width), shaped(rows, width, dtype=f32), shaped(8, width, dtype=f32),
        ],
        scratch_shapes=[pltpu.VMEM((BLOCK, width), bf16)],
        compiler_params=params(),
        cost_estimate=cost(2 * rows * width * (4 * width + 5 * SEG_LEN), rows * width * 22 + attn.size * 2),
        name="seg_attn_bwd",
    )(first_grad, qkv, attn)


def cross_layer(entry, cot, row_key, blocks, attn, up_proj, down_proj, vec):
    rows, width = entry.shape
    inner = up_proj.shape[1]
    block = rows // blocks
    spec = partial(row_spec, block=block)
    return pl.pallas_call(
        cross_kernel,
        grid=(blocks,),
        in_specs=[
            spec(width), spec(width), spec(1), pl.BlockSpec((1, 1, block), lambda i: (i, 0, 0)),
            whole_spec(attn.shape), whole_spec(up_proj.shape), whole_spec(down_proj.shape), whole_spec(vec.shape),
        ],
        out_specs=[
            spec(width), spec(width), spec(width), spec(3 * width), spec(width), spec(width),
            spec(width), spec(inner), spec(width), spec(inner), fixed_spec(vec.shape),
        ],
        out_shape=[
            shaped(rows, width), shaped(rows, width, dtype=f32), shaped(rows, width), shaped(rows, 3 * width),
            shaped(rows, width), shaped(rows, width), shaped(rows, width), shaped(rows, inner),
            shaped(rows, width), shaped(rows, inner), shaped(*vec.shape, dtype=f32),
        ],
        scratch_shapes=[
            pltpu.VMEM((block, 3 * width), bf16), pltpu.VMEM((block, width), bf16), pltpu.VMEM((block, inner), f32),
        ],
        compiler_params=params(),
        cost_estimate=cost(24 * rows * width * 4 * width, rows * width * 40 + attn.size * 6),
        name="cross_layer",
    )(entry, cot, row_key.reshape(rows, 1), row_key.reshape(blocks, 1, block), attn, up_proj, down_proj, vec)


def spread_vec(columns):
    return jnp.concatenate([columns.astype(f32), jnp.zeros((4, columns.shape[1]), f32)], 0)


def gather_rows(matrix):
    return lax.all_gather(matrix, "seg", axis=0, tiled=True)


def scatter_sum(matrix):
    return lax.psum_scatter(matrix, "seg", scatter_dimension=0, tiled=True)


def local(
    hidden, seg_doc, seg_attn, seg_up, seg_down, seg_vec,
    cross_attn, cross_up, cross_down, cross_vec, tok_cot, cls_cot,
):
    micro, _, segments, _, length, width = hidden.shape
    own = seg_attn.shape[0]
    parts = lax.axis_size("seg")
    place = lax.axis_index("seg")
    count = micro * segments
    total = parts * count

    small = jnp.concatenate([cls_cot.reshape(count * width), seg_vec.T.reshape(-1), cross_vec.T.reshape(-1)])
    small = lax.all_gather(small, "seg", axis=0, tiled=False)
    cot_all = small[:, : count * width].reshape(total, width)
    vecs = small[:, count * width :].reshape(parts, 24, own).transpose(1, 0, 2).reshape(24, width)
    seg_vec_full = spread_vec(vecs[:12])
    cross_vec_full = spread_vec(vecs[12:])

    attn_full = gather_rows(seg_attn)
    up_full = gather_rows(seg_up)
    down_full = gather_rows(seg_down)
    cross_attn_full = gather_rows(cross_attn)
    cross_up_full = gather_rows(cross_up)
    cross_down_full = gather_rows(cross_down)

    flat = hidden.reshape(count * length, width)
    qkv, mixed, first_sum = attn_forward(flat, attn_full, seg_vec_full)
    normed, act, slope, second_sum, tok, cls = ffn_forward(first_sum, up_full, down_full, seg_vec_full)

    entry = lax.all_gather(cls.reshape(count, width), "seg", axis=0, tiled=True)
    docs = seg_doc[:, 0].reshape(micro, segments, parts) + (1 << 16) * jnp.arange(micro, dtype=jnp.int32)[:, None, None]
    blocks = micro if total > 256 else 1
    if blocks > 1:
        order = lambda rows: rows.reshape(parts, micro, segments, -1).transpose(1, 0, 2, 3).reshape(total, -1)
        back = lambda rows: rows.reshape(micro, parts, segments, -1).transpose(1, 0, 2, 3).reshape(total, -1)
        row_key = docs.transpose(0, 2, 1).reshape(total)
    else:
        order = back = lambda rows: rows
        row_key = docs.transpose(2, 0, 1).reshape(total)
    (
        cls_out, cls_grad, x_low, x_qkv_grad, x_mixed, x_attn_low, x_norm, x_inner, x_branch, x_act, x_sums,
    ) = cross_layer(
        order(entry), order(cot_all), row_key, blocks,
        cross_attn_full, cross_up_full, cross_down_full, cross_vec_full,
    )
    own_rows = lambda rows: lax.dynamic_slice_in_dim(back(rows), place * count, count, 0)
    own_cols = lambda rows: lax.dynamic_slice_in_dim(rows, place * own, own, 1)
    cls_out = own_rows(cls_out)
    cls_grad = own_rows(cls_grad)

    branch, inner, first_grad, ffn_sums = ffn_backward(
        tok_cot.reshape(count * length, width),
        cls_grad.reshape(cls.shape), second_sum, first_sum, slope, up_full, down_full, seg_vec_full,
    )
    down_grad = dot_tn(branch, act).astype(bf16)
    up_grad = dot_tn(normed, inner).astype(bf16)
    attn_low, qkv_grad, hidden_grad, attn_sums = attn_backward(first_grad, qkv, attn_full)
    attn_grad = jnp.concatenate([dot_tn(flat, qkv_grad), dot_tn(mixed, attn_low)], 1).astype(bf16)

    x_attn_grad = jnp.concatenate(
        [dot_tn(own_cols(x_low), x_qkv_grad), dot_tn(own_cols(x_mixed), x_attn_low)], 1
    )
    x_up_grad = dot_tn(own_cols(x_norm), x_inner)
    x_down_grad = dot_tn(own_cols(x_branch), x_act)

    sums = jnp.concatenate([attn_sums[:2], ffn_sums[2:12]], 0)
    vec_sums = scatter_sum(jnp.stack(jnp.split(sums, parts, 1)).astype(bf16))[0]
    vec_all = jnp.concatenate([vec_sums.astype(f32), own_cols(x_sums[:12])], 0)

    seg_parts = [scatter_sum(down_grad), scatter_sum(up_grad), scatter_sum(attn_grad)]
    down_sum, up_sum, attn_sum, x_down_sum, x_up_sum, x_attn_sum, vec_all = lax.psum(
        (
            seg_parts[0], seg_parts[1], seg_parts[2],
            x_down_grad.astype(bf16), x_up_grad.astype(bf16), x_attn_grad.astype(bf16), vec_all.astype(bf16),
        ),
        "batch",
    )
    vec_all = vec_all.astype(f32)
    return (
        tok.reshape(hidden.shape),
        cls_out.reshape(cls_cot.shape),
        hidden_grad.reshape(hidden.shape),
        attn_sum.astype(f32), up_sum.astype(f32), down_sum.astype(f32), vec_all[:12].T,
        x_attn_sum.astype(f32), x_up_sum.astype(f32), x_down_sum.astype(f32), vec_all[12:].T,
    )


def solution(mesh):
    wide = P(None, "batch", None, "seg", None, None)
    rows = P("seg", None)
    cls = P(None, "batch", None, "seg", None)
    in_specs = (wide, P(None, "batch", None)) + (rows,) * 8 + (wide, cls)
    out_specs = (wide, cls, wide) + (rows,) * 8
    return jax.shard_map(local, mesh=mesh, in_specs=in_specs, out_specs=out_specs, check_vma=False)
```

time: 1160 us -> 733 us (0.63)
  matrix products: 211 us -> 33.7 us
  waiting for transfers between devices: 672 us -> 497 us
  Pallas kernels: 0 us -> 108 us
  blocking collectives: 110 us -> 42.3 us
  local copies, waits for them, and re-layouts: 77.8 us -> 22.2 us
  other arithmetic: 61.7 us -> 13.9 us
    dot_general x72 -> x8, matrix products: 211 us -> 33.7 us  [dot_tn(): lax.dot_general(left, right, (((0,), (0,)), ((), ())), preferred_element_...]
    reduce_scatter x5 -> x3, waiting for transfers between devices: 273 us -> 139 us  [scatter_sum(): return lax.psum_scatter(matrix, 'seg', scatter_dimension=0, tiled=True)]
    unnamed x18 -> x12, waiting for transfers between devices: 148 us -> 26.4 us
    pallas_call x0 -> x5, Pallas kernels: none -> 108 us  [the longest x1 34.3 us: attn_backward(): pl.pallas_call(attn_bwd_kernel, grid=(rows // BLOCK,), in_specs=[row_spec...]
    all_gather x6, waiting for transfers between devices: 162 us -> 242 us  [gather_rows(): return lax.all_gather(matrix, 'seg', axis=0, tiled=True)]
    unnamed x1 -> x0, blocking collectives: 41.1 us -> none
    all_gather x4 -> x2, blocking collectives: 58.4 us -> 32.3 us  [the longest x1 16.2 us: local(): small = lax.all_gather(small, 'seg', axis=0, tiled=False)]
    unnamed x390 -> x53, local copies, waits for them, and re-layouts: 34.4 us -> 14.5 us
  transfers between devices with their start and end apart: 15 -> 11, of which waited for: 13 -> 11; matrix products, arithmetic and copies ran while one was open for 26% -> 5% of each run, Pallas kernels for 0% -> 5%
where the time goes in v1:
time: 733 us; the launch traced here: 732 us
  waiting for transfers between devices  497 us (68%)
  Pallas kernels  108 us (15%)
  blocking collectives  42.3 us (6%)
  matrix products  33.7 us (5%)
  local copies, waits for them, and re-layouts  22.2 us (3%)
  between operations  14.2 us (2%)
  other arithmetic  13.9 us (2%)
    all_gather x6, waiting for transfers between devices, gather_rows(): return lax.all_gather(matrix, 'seg', axis=0, tiled=True)  242 us
    reduce_scatter x3, waiting for transfers between devices, scatter_sum(): return lax.psum_scatter(matrix, 'seg', scatter_dimension=0, tiled=True)  139 us
    psum x1, waiting for transfers between devices, local(): lax.psum((seg_parts[0], seg_parts[1], seg_parts[2], x_down_grad.astype(bf...  90.3 us
    pallas_call x1, Pallas kernels, attn_backward(): pl.pallas_call(attn_bwd_kernel, grid=(rows // BLOCK,), in_specs=[row_spec...  34.3 us
    dot_general x8, matrix products, dot_tn(): lax.dot_general(left, right, (((0,), (0,)), ((), ())), preferred_element_...  33.7 us
    unnamed x12, waiting for transfers between devices  26.4 us
    pallas_call x1, Pallas kernels, ffn_forward(): pl.pallas_call(ffn_fwd_kernel, grid=(rows // BLOCK,), in_specs=[row_spec(...  20.8 us
    pallas_call x1, Pallas kernels, ffn_backward(): pl.pallas_call(ffn_bwd_kernel, grid=(rows // BLOCK,), in_specs=[row_spec(...  20.5 us
  transfers between devices with their start and end apart: 11, of which 11 were waited for; matrix products, arithmetic and copies ran while one was open for 5% of the time, Pallas kernels for 5%

profile of v1, /device:TPU:0, one launch (start us, length us, event | category | flops | bytes accessed | tf_op | source)
XLA Modules:
  0.0 731.9 jit_solution(5500449880878392777)
XLA Ops:
  11.5 16.2 %all-gather.1 = bf16[8,1,8448]{2,1,0:T(2,128)(2,1)S(1)} all-gather(bf16[1,1,8448]{2,1,0:T(2,128)(2,1)S(1)} %reshape.85), channel_id=2, replica_groups=mesh['batch'=4,'seg'=8] {'seg'}, dimensions={0}, use_global_device_ids=true | all-gather | bytes 152064 | tf_op jit(solution)/shard_map/all_gather | solution.py:435
  32.8 32.0 %all-gather.9.cloned.1.call-done.w_ref = bf16[768,3072]{1,0:T(8,128)(2,1)} async-done(((bf16[96,3072]{1,0:T(8,128)(2,1)}), bf16[768,3072]{1,0:T(8,128)(2,1)}) %all-gather.9.cloned.1.call-update) | async-done | bytes 4718608 | tf_op jit(solution)/shard_map/all_gather | solution.py:416
  64.8 14.9 %seg_attn_fwd.1 = (bf16[1024,2304]{1,0:T(8,128)(2,1)}, bf16[1024,768]{1,0:T(8,128)(2,1)}, f32[1024,768]{1,0:T(8,128)}) custom-call(bf16[1024,768]{1,0:T(8,128)(2,1)} %bitcast.77, bf16[768,3072]{1,0:T(8,128)(2,1)} %all-gather.9.cloned.1.call-done.w_ref, f32[16,768]{1,0:T(8,128)} %pad_convert_fusion.1.vec_ref), custom_call_target="tpu_custom_call" | custom-call | flops 5234491392 | bytes 15728640 | tf_op jit(solution)/shard_map/seg_attn_fwd/pallas_call | solution.py:310
  79.7 37.3 %all-gather.11.cloned.1.call-done.up_ref = bf16[768,3072]{1,0:T(8,128)(2,1)} async-done(((bf16[96,3072]{1,0:T(8,128)(2,1)}), bf16[768,3072]{1,0:T(8,128)(2,1)}) %all-gather.11.cloned.1.call-update) | async-done | bytes 4718608 | tf_op jit(solution)/shard_map/all_gather | solution.py:416
  117.0 52.2 %all-gather.13.cloned.1.call-done.down_ref = bf16[768,3072]{1,0:T(8,128)(2,1)} async-done(((bf16[96,3072]{1,0:T(8,128)(2,1)}), bf16[768,3072]{1,0:T(8,128)(2,1)}) %all-gather.13.cloned.1.call-update) | async-done | bytes 4718608 | tf_op jit(solution)/shard_map/all_gather | solution.py:416
  169.2 20.8 %seg_ffn_fwd.1 = (bf16[1024,768]{1,0:T(8,128)(2,1)}, bf16[1024,3072]{1,0:T(8,128)(2,1)}, bf16[1024,3072]{1,0:T(8,128)(2,1)}, f32[1024,768]{1,0:T(8,128)}, bf16[1...) custom-call(f32[1024,768]{1,0:T(8,128)} %get-tuple-element.39.sum_ref, bf16[768,3072]{1,0:T(8,128)(2,1)} %all-gather.11.cloned.1.call-done.up_ref, ...), custom_call_target="tpu_custom_call" | custom-call | flops 9663676416 | bytes 31457280 | tf_op jit(solution)/shard_map/seg_ffn_fwd/pallas_call | solution.py:327
  190.7 16.1 %all_gather.32.x_ref = f32[64,768]{1,0:T(8,128)} all-gather(f32[8,768]{1,0:T(8,128)S(1)} %reshape.78), channel_id=1, replica_groups=mesh['batch'=4,'seg'=8] {'seg'}, dimensions={0}, use_global_device_ids=true | all-gather | bytes 221184 | tf_op jit(solution)/shard_map/all_gather | solution.py:452
  206.8 15.9 %all-gather.15.cloned.1.call-done.attn_ref = bf16[768,3072]{1,0:T(8,128)(2,1)} async-done(((bf16[96,3072]{1,0:T(8,128)(2,1)}), bf16[768,3072]{1,0:T(8,128)(2,1)}) %all-gather.15.cloned.1.call-update) | async-done | bytes 4718608 | tf_op jit(solution)/shard_map/all_gather | solution.py:416
  222.7 52.1 %all-gather.17.cloned.1.call-done.up_ref = bf16[768,3072]{1,0:T(8,128)(2,1)} async-done(((bf16[96,3072]{1,0:T(8,128)(2,1)}), bf16[768,3072]{1,0:T(8,128)(2,1)}) %all-gather.17.cloned.1.call-update) | async-done | bytes 4718608 | tf_op jit(solution)/shard_map/all_gather | solution.py:416
  274.7 52.0 %all-gather.19.cloned.1.call-done.down_ref = bf16[768,3072]{1,0:T(8,128)(2,1)} async-done(((bf16[96,3072]{1,0:T(8,128)(2,1)}), bf16[768,3072]{1,0:T(8,128)(2,1)}) %all-gather.19.cloned.1.call-update) | async-done | bytes 4718608 | tf_op jit(solution)/shard_map/all_gather | solution.py:416
  326.8 17.8 %cross_layer.1 = (bf16[64,768]{1,0:T(8,128)(2,1)}, f32[64,768]{1,0:T(8,128)}, bf16[64,768]{1,0:T(8,128)(2,1)}, bf16[64,2304]{1,0:T(8,128)(2,1)}, bf16[64,768]{1,...) custom-call(f32[64,768]{1,0:T(8,128)} %all_gather.32.x_ref, ...), custom_call_target="tpu_custom_call" | custom-call | flops 3623878656 | bytes 16121856 | tf_op jit(solution)/shard_map/cross_layer/pallas_call | solution.py:386
  345.9 20.5 %seg_ffn_bwd.1 = (bf16[1024,768]{1,0:T(8,128)(2,1)}, bf16[1024,3072]{1,0:T(8,128)(2,1)}, f32[1024,768]{1,0:T(8,128)}, f32[16,768]{1,0:T(8,128)}) custom-call(bf16[1024,768]{1,0:T(8,128)(2,1)} %bitcast.76, f32[4,2,768]{2,1,0:T(2,128)} %reshape.82.cls_ref, f32[1024,768]{1,0:T(8,128)} %get-tuple-element.44.second_ref, f32[1024,768]{1,0:T(8,128)} %get-tuple-element.39.sum_ref, ...), custom_call_target="tpu_custom_call" | custom-call | flops 9663676416 | bytes 34603008 | tf_op jit(solution)/shard_map/seg_ffn_bwd/pallas_call | solution.py:347
  366.4 34.3 %seg_attn_bwd.1 = (bf16[1024,768]{1,0:T(8,128)(2,1)}, bf16[1024,2304]{1,0:T(8,128)(2,1)}, f32[1024,768]{1,0:T(8,128)}, f32[8,768]{1,0:T(8,128)}) custom-call(f32[1024,768]{1,0:T(8,128)} %get-tuple-element.46.first_ref, bf16[1024,2304]{1,0:T(8,128)(2,1)} %get-tuple-element.47.qkv_ref, bf16[768,3072]{1,0:T(8,128)(2,1)} %all-gather.9.cloned.1.call-done.w_ref), custom_call_target="tpu_custom_call" | custom-call | flops 5838471168 | bytes 22020096 | tf_op jit(solution)/shard_map/seg_attn_bwd/pallas_call | solution.py:366
  400.7 6.9 fusion
  409.1 2.5 pad_maximum_fusion
  411.6 6.6 copy.53
  419.6 9.5 %convolution_convert_fusion = bf16[768,3072]{1,0:T(8,128)(2,1)} fusion(bf16[1024,768]{1,0:T(8,128)(2,1)S(1)} %copy-done.19, bf16[1024,3072]{1,0:T(8,128)(2,1)} %get-tuple-element.55), kind=kOutput, calls=%fused_computation | convolution fusion | flops 4834197504 | bytes 12582912 | tf_op jit(solution)/shard_map/dot_general | solution.py:37
  430.6 9.6 %convolution_convert_fusion.1 = bf16[768,3072]{1,0:T(8,128)(2,1)} fusion(bf16[1024,768]{1,0:T(8,128)(2,1)S(1)} %copy-done.18, bf16[1024,3072]{1,0:T(8,128)(2,1)} %get-tuple-element.53), kind=kOutput, calls=%fused_computation.1 | convolution fusion | flops 4834197504 | bytes 12582912 | tf_op jit(solution)/shard_map/dot_general | solution.py:37
  449.4 22.7 %reduce-scatter.13.cloned.1.call-done = bf16[96,3072]{1,0:T(8,128)(2,1)} async-done(((bf16[768,3072]{1,0:T(8,128)(2,1)}), bf16[96,3072]{1,0:T(8,128)(2,1)}) %reduce-scatter.13.cloned.1.call-update) | async-done | bytes 589840
  474.3 53.4 %reduce-scatter.9.cloned.1.call-done = bf16[96,3072]{1,0:T(8,128)(2,1)} async-done(((bf16[768,3072]{1,0:T(8,128)(2,1)}), bf16[96,3072]{1,0:T(8,128)(2,1)}) %reduce-scatter.9.cloned.1.call-update) | async-done | bytes 589840 | tf_op jit(solution)/shard_map/reduce_scatter | solution.py:420
  527.8 55.7 %reduce-scatter.7.cloned.1.call-done = bf16[96,3072]{1,0:T(8,128)(2,1)} async-done(((bf16[768,3072]{1,0:T(8,128)(2,1)}), bf16[96,3072]{1,0:T(8,128)(2,1)}) %reduce-scatter.7.cloned.1.call-update) | async-done | bytes 589840 | tf_op jit(solution)/shard_map/reduce_scatter | solution.py:420
  584.9 29.6 %reduce-scatter.11.cloned.1.call-done = bf16[1,12,96]{2,1,0:T(8,128)(2,1)} async-done(((bf16[8,12,96]{2,1,0:T(8,128)(2,1)}), bf16[1,12,96]{2,1,0:T(8,128)(2,1)}) %reduce-scatter.11.cloned.1.call-update) | async-done | bytes 2320 | tf_op jit(solution)/shard_map/reduce_scatter | solution.py:420
  615.2 10.1 %psum.52 = bf16[24,96]{1,0:T(8,128)(2,1)S(1)} all-reduce(bf16[24,96]{1,0:T(8,128)(2,1)S(1)} %pad_maximum_fusion.3), channel_id=1, replica_groups=mesh['batch'=4,'seg'=8] {'batch'}, use_global_device_ids=true, to_apply=%region_7.0 | all-reduce | flops 2304 | bytes 9216 | tf_op jit(solution)/shard_map/psum | solution.py:493
  625.9 90.3 %all-reduce.5.cloned.1.call-done = (bf16[96,3072]{0,1:T(8,128)(2,1)}, bf16[96,3072]{1,0:T(8,128)(2,1)}, bf16[96,3072]{1,0:T(8,128)(2,1)}, bf16[96,3072]{1,0:T(8,...) async-done(((bf16[96,3072]{0,1:T(8,128)(2,1)}, bf16[96,3072]{1,0:T(8,128)(2,1)}, bf16[96,3072]{1,0:T(8,128)(2,1)}, bf16[96,3072]{1,0:T(8,128)(2,1)}, ...) | async-done | bytes 3538960 | tf_op jit(solution)/shard_map/psum | solution.py:493
  (121 shorter events, 38.9 us)
Async XLA Ops:
  7.2 4.1 copy-start.12
  7.2 4.2 copy-start.13
  7.2 21.0 %copy-start.14 = (s32[2,1,32]{2,1,0:T(1,128)S(1)}, s32[2,1,32]{2,1,0:T(1,128)}, u32[]{:S(2)}) copy-start(s32[2,1,32]{2,1,0:T(1,128)} %param.13) | copy-start | bytes 772
  7.2 57.6 %all-gather.9.cloned.1.call-start = ((), (), s32[]{:S(2)}) async-start(), calls=%async_computation.4 | async-start | bytes 5308416 | tf_op jit(solution)/shard_map/all_gather | solution.py:416
  8.0 109.0 %all-gather.11.cloned.1.call-start = ((), (), s32[]{:S(2)}) async-start(), calls=%async_computation.5 | async-start | bytes 5308416 | tf_op jit(solution)/shard_map/all_gather | solution.py:416
  8.7 160.5 %all-gather.13.cloned.1.call-start = ((), (), s32[]{:S(2)}) async-start(), calls=%async_computation.6 | async-start | bytes 5308416 | tf_op jit(solution)/shard_map/all_gather | solution.py:416
  9.4 213.2 %all-gather.15.cloned.1.call-start = ((), (), s32[]{:S(2)}) async-start(), calls=%async_computation.7 | async-start | bytes 5308416 | tf_op jit(solution)/shard_map/all_gather | solution.py:416
  10.0 264.7 %all-gather.17.cloned.1.call-start = ((), (), s32[]{:S(2)}) async-start(), calls=%async_computation.8 | async-start | bytes 5308416 | tf_op jit(solution)/shard_map/all_gather | solution.py:416
  10.6 316.2 %all-gather.19.cloned.1.call-start = ((), (), s32[]{:S(2)}) async-start(), calls=%async_computation.9 | async-start | bytes 5308416 | tf_op jit(solution)/shard_map/all_gather | solution.py:416
  11.2 460.9 %reduce-scatter.13.cloned.1.call-start = ((), (), s32[]{:S(2)}) async-start(), calls=%async_computation.13 | async-start | bytes 5308416
  366.4 34.3 %copy-start.15 = (bf16[2,1,4,1,128,768]{5,4,3,2,1,0:T(8,128)(2,1)S(1)}, bf16[2,1,4,1,128,768]{5,4,3,2,1,0:T(8,128)(2,1)}, u32[]{:S(2)}) copy-start(bf16[2,1,4,1,128,768]{5,4,3,2,1,0:T(8,128)(2,1)} %param.12) | copy-start | bytes 4718596
  400.7 6.9 copy-start.16
  400.7 6.9 copy-start.17
  418.2 109.6 %reduce-scatter.9.cloned.1.call-start = ((), (), s32[]{:S(2)}) async-start(), calls=%async_computation.11 | async-start | bytes 5308416 | tf_op jit(solution)/shard_map/reduce_scatter | solution.py:420
  429.2 154.3 %reduce-scatter.7.cloned.1.call-start = ((), (), s32[]{:S(2)}) async-start(), calls=%async_computation.10 | async-start | bytes 5308416 | tf_op jit(solution)/shard_map/reduce_scatter | solution.py:420
  440.2 5.3 copy-start.5
  440.2 7.3 copy-start.4
  440.2 174.3 %reduce-scatter.11.cloned.1.call-start = ((), (), s32[]{:S(2)}) async-start(), calls=%async_computation.12 | async-start | bytes 36864 | tf_op jit(solution)/shard_map/reduce_scatter | solution.py:420
  442.3 273.9 %all-reduce.5.cloned.1.call-start = ((), (), s32[]{:S(2)}) async-start(), calls=%async_computation.14 | async-start | bytes 7471104 | tf_op jit(solution)/shard_map/psum | solution.py:493
  447.5 136.0 %copy-start.9 = (f32[16,768]{1,0:T(8,128)S(1)}, f32[16,768]{1,0:T(8,128)}, u32[]{:S(2)}) copy-start(f32[16,768]{1,0:T(8,128)} %get-tuple-element.58) | copy-start | bytes 147460
  716.2 4.6 copy-start.3
  716.2 5.7 copy-start.2
  716.2 6.8 copy-start.1
  718.5 5.6 copy-start
  (7 other events, 14.0 us)
Sparse Core Ops, SparseCore 0:
  9.7 55.0 all-gather.8
  66.5 50.4 all-gather.10
  118.6 50.5 all-gather.12
  170.7 51.9 all-gather.14
  224.1 50.5 all-gather.16
  276.2 50.5 all-gather.18
  418.3 53.7 reduce-scatter.12
  474.4 53.3 reduce-scatter.8
  530.1 53.3 reduce-scatter.6
  586.1 28.3 reduce-scatter.10
  619.9 96.2 all-reduce.4

commit v2 on v1

--- a/solution.py
+++ b/solution.py
@@ -116,13 +116,83 @@
     out_ref[rows, 2 * width + at : 2 * width + at + PAIR] = value_grad.astype(bf16)
 
 
+class Pieces:
+    def __init__(self, shape, arrays, blocks):
+        self.shape, self.arrays, self.blocks = shape, arrays, blocks
+
+    def specs(self):
+        return [pl.BlockSpec(memory_space=pl.ANY)] * len(self.arrays)
+
+    def scratch(self):
+        return [pltpu.VMEM(self.shape, bf16), pltpu.SemaphoreType.DMA((len(self.blocks),))]
+
+    def copies(self, refs, place_ref, full_ref, sems):
+        out = []
+        for at, (index, source, size, target) in enumerate(self.blocks):
+            row, col = target(place_ref[0], place_ref[1], place_ref[2])
+            if not isinstance(row, int):
+                row = pl.multiple_of(row, size[0])
+            if not isinstance(col, int):
+                col = pl.multiple_of(col, size[1])
+            view = full_ref.at[pl.ds(row, size[0]), pl.ds(col, size[1])]
+            out.append(pltpu.make_async_copy(refs[index].at[source], view, sems.at[at]))
+        return out
+
+
+class Weights:
+    def __init__(self, *matrices):
+        self.matrices = matrices
+
+    def arrays(self, place):
+        return [place] + [array for matrix in self.matrices for array in matrix.arrays]
+
+    def specs(self):
+        return [pl.BlockSpec(memory_space=pltpu.SMEM)] + [spec for matrix in self.matrices for spec in matrix.specs()]
+
+    def scratch(self):
+        return [item for matrix in self.matrices for item in matrix.scratch()]
+
+    def wrap(self, body, step_axis=0):
+        many = sum(len(matrix.arrays) for matrix in self.matrices)
+
+        def kernel(place_ref, *refs):
+            given, rest = refs[:many], refs[many:]
+            cut = len(rest) - 2 * len(self.matrices)
+            rest, own = rest[:cut], rest[cut:]
+            first = pl.program_id(step_axis) == 0
+            views, copies = [], []
+            for at, matrix in enumerate(self.matrices):
+                views.append(own[2 * at])
+                copies.append(partial(matrix.copies, given[: len(matrix.arrays)], place_ref, own[2 * at], own[2 * at + 1]))
+                given = given[len(matrix.arrays) :]
+
+            @pl.when(first)
+            def _():
+                for group in copies:
+                    for copy in group():
+                        copy.start()
+
+            def ready(at):
+                @pl.when(first)
+                def _():
+                    for copy in copies[at]():
+                        copy.wait()
+
+                return views[at]
+
+            body(ready, *rest)
+
+        return kernel
+
+
 def qkv_bias(vec_ref):
     query = vec_ref[0:1, :]
     return jnp.concatenate([query, jnp.zeros_like(query), vec_ref[1:2, :]], 1)
 
 
-def attn_fwd_kernel(x_ref, w_ref, vec_ref, qkv_ref, mixed_ref, sum_ref):
+def attn_fwd_kernel(ready, x_ref, vec_ref, qkv_ref, mixed_ref, sum_ref):
     width = x_ref.shape[1]
+    w_ref = ready(0)
     rows = x_ref[...]
     qkv = dot_nn(rows, w_ref[:, : 3 * width]) + qkv_bias(vec_ref)
     qkv_ref[...] = qkv.astype(bf16)
@@ -133,8 +203,10 @@
     sum_ref[...] = rows.astype(f32) + branch + vec_ref[2:3, :]
 
 
-def ffn_fwd_kernel(sum_ref, up_ref, down_ref, vec_ref, norm_ref, act_ref, slope_ref, second_ref, tok_ref, cls_ref):
+def ffn_fwd_kernel(ready, sum_ref, vec_ref, norm_ref, act_ref, slope_ref, second_ref, tok_ref, cls_ref):
     width = sum_ref.shape[1]
+    up_ref = ready(0)
+    down_ref = ready(1)
     unit, _ = normalise(sum_ref[...])
     normed = unit * vec_ref[3:4, :] + vec_ref[4:5, :]
     low = normed.astype(bf16)
@@ -156,7 +228,7 @@
         cls_ref[0, index : index + 1, :] = result[index * SEG_LEN : index * SEG_LEN + 1, :]
 
 
-def ffn_bwd_kernel(cot_ref, cls_ref, second_ref, sum_ref, slope_ref, up_ref, down_ref, vec_ref, branch_ref, inner_ref, first_ref, sums_ref):
+def ffn_bwd_kernel(ready, cot_ref, cls_ref, second_ref, sum_ref, slope_ref, vec_ref, branch_ref, inner_ref, first_ref, low_ref, sums_ref):
     width = sum_ref.shape[1]
 
     @pl.when(pl.program_id(0) == 0)
@@ -176,6 +248,8 @@
     branch = second_grad.astype(bf16)
     branch_ref[...] = branch
     sums_ref[5:6, :] += column_sum(branch.astype(f32))
+    up_ref = ready(0)
+    down_ref = ready(1)
     total = second_grad
     for part in range(4):
         cols = pl.ds(part * width, width)
@@ -189,31 +263,31 @@
     sums_ref[4:5, :] += column_sum(total)
     first = norm_back(total, unit, inverse, vec_ref[3:4, :])
     first_ref[...] = first
-    sums_ref[2:3, :] += column_sum(first.astype(bf16).astype(f32))
-
-
-def attn_bwd_kernel(first_ref, qkv_ref, w_ref, low_ref, qkv_grad_ref, x_grad_ref, sums_ref, mixed_grad):
+    low = first.astype(bf16)
+    low_ref[...] = low
+    sums_ref[2:3, :] += column_sum(low.astype(f32))
+
+
+def attn_bwd_kernel(ready, first_ref, low_ref, qkv_ref, qkv_grad_ref, x_grad_ref, sums_ref, mixed_grad):
     width = first_ref.shape[1]
 
     @pl.when(pl.program_id(0) == 0)
     def _():
         sums_ref[...] = jnp.zeros_like(sums_ref)
 
-    first = first_ref[...]
-    low = first.astype(bf16)
-    low_ref[...] = low
-    mixed_grad[...] = dot_nt(low, w_ref[:, 3 * width :]).astype(bf16)
+    w_ref = ready(0)
+    mixed_grad[...] = dot_nt(low_ref[...], w_ref[:, 3 * width :]).astype(bf16)
     for start in range(0, first_ref.shape[0], SEG_LEN):
         for pair in range(PAIRS):
             pair_backward(qkv_ref, mixed_grad, qkv_grad_ref, pl.ds(start, SEG_LEN), pair, width, None)
     qkv_grad = qkv_grad_ref[...]
-    x_grad_ref[...] = first + dot_nt(qkv_grad, w_ref[:, : 3 * width])
+    x_grad_ref[...] = first_ref[...] + dot_nt(qkv_grad, w_ref[:, : 3 * width])
     sums_ref[0:1, :] += column_sum(qkv_grad[:, :width].astype(f32))
     sums_ref[1:2, :] += column_sum(qkv_grad[:, 2 * width :].astype(f32))
 
 
 def cross_kernel(
-    x_ref, cot_ref, key_own_ref, key_all_ref, attn_ref, up_ref, down_ref, vec_ref,
+    ready, x_ref, cot_ref, key_own_ref, key_all_ref, vec_ref,
     out_ref, x_grad_ref, low_in_ref, qkv_grad_ref, mixed_ref, attn_low_ref,
     norm_ref, inner_ref, branch_ref, act_ref, sums_ref,
     qkv_ref, mixed_grad, slope,
@@ -226,6 +300,7 @@
     def _():
         sums_ref[...] = jnp.zeros_like(sums_ref)
 
+    attn_ref = ready(0)
     same = key_own_ref[...] == key_all_ref[0]
     mask = jnp.concatenate([same, same], 0)
     entry = x_ref[...]
@@ -240,6 +315,8 @@
     normed = unit_one * vec_ref[3:4, :] + vec_ref[4:5, :]
     low = normed.astype(bf16)
     norm_ref[...] = low
+    up_ref = ready(1)
+    down_ref = ready(2)
     total = normed + vec_ref[5:6, :]
     for part in range(4):
         cols = pl.ds(part * width, width)
@@ -305,90 +382,95 @@
     return pl.CostEstimate(flops=int(flops), bytes_accessed=int(nbytes), transcendentals=int(trans))
 
 
-def attn_forward(flat, attn, vec):
+def attn_forward(flat, place, attn, vec):
     rows, width = flat.shape
+    weights = Weights(attn)
     return pl.pallas_call(
-        attn_fwd_kernel,
+        weights.wrap(attn_fwd_kernel),
         grid=(rows // BLOCK,),
-        in_specs=[row_spec(width), whole_spec(attn.shape), whole_spec(vec.shape)],
+        in_specs=weights.specs() + [row_spec(width), whole_spec(vec.shape)],
         out_specs=[row_spec(3 * width), row_spec(width), row_spec(width)],
         out_shape=[shaped(rows, 3 * width), shaped(rows, width), shaped(rows, width, dtype=f32)],
+        scratch_shapes=weights.scratch(),
         compiler_params=params(),
-        cost_estimate=cost(2 * rows * width * (4 * width + 2 * SEG_LEN), rows * width * 14 + attn.size * 2),
+        cost_estimate=cost(2 * rows * width * (4 * width + 2 * SEG_LEN), rows * width * 14 + width * width * 8),
         name="seg_attn_fwd",
-    )(flat, attn, vec)
-
-
-def ffn_forward(first_sum, up_proj, down_proj, vec):
+    )(*weights.arrays(place), flat, vec)
+
+
+def ffn_forward(first_sum, place, up_proj, down_proj, vec):
     rows, width = first_sum.shape
     inner = up_proj.shape[1]
     per = BLOCK // SEG_LEN
+    weights = Weights(up_proj, down_proj)
     cls_spec = pl.BlockSpec((1, per, width), lambda i: (i, 0, 0))
     return pl.pallas_call(
-        ffn_fwd_kernel,
+        weights.wrap(ffn_fwd_kernel),
         grid=(rows // BLOCK,),
-        in_specs=[row_spec(width), whole_spec(up_proj.shape), whole_spec(down_proj.shape), whole_spec(vec.shape)],
+        in_specs=weights.specs() + [row_spec(width), whole_spec(vec.shape)],
         out_specs=[row_spec(width), row_spec(inner), row_spec(inner), row_spec(width), row_spec(width), cls_spec],
         out_shape=[
             shaped(rows, width), shaped(rows, inner), shaped(rows, inner), shaped(rows, width, dtype=f32),
             shaped(rows, width), shaped(rows // BLOCK, per, width, dtype=f32),
         ],
+        scratch_shapes=weights.scratch(),
         compiler_params=params(),
-        cost_estimate=cost(4 * rows * width * inner, rows * (width * 12 + inner * 4) + up_proj.size * 4, 2 * rows * inner),
+        cost_estimate=cost(4 * rows * width * inner, rows * (width * 12 + inner * 4) + width * inner * 4, 2 * rows * inner),
         name="seg_ffn_fwd",
-    )(first_sum, up_proj, down_proj, vec)
-
-
-def ffn_backward(cot, cls_grad, second_sum, first_sum, slope, up_proj, down_proj, vec):
+    )(*weights.arrays(place), first_sum, vec)
+
+
+def ffn_backward(cot, cls_grad, second_sum, first_sum, slope, place, up_proj, down_proj, vec):
     rows, width = first_sum.shape
     inner = up_proj.shape[1]
     per = BLOCK // SEG_LEN
+    weights = Weights(up_proj, down_proj)
     cls_spec = pl.BlockSpec((1, per, width), lambda i: (i, 0, 0))
     return pl.pallas_call(
-        ffn_bwd_kernel,
+        weights.wrap(ffn_bwd_kernel),
         grid=(rows // BLOCK,),
-        in_specs=[
-            row_spec(width), cls_spec, row_spec(width), row_spec(width), row_spec(inner),
-            whole_spec(up_proj.shape), whole_spec(down_proj.shape), whole_spec(vec.shape),
+        in_specs=weights.specs() + [
+            row_spec(width), cls_spec, row_spec(width), row_spec(width), row_spec(inner), whole_spec(vec.shape),
         ],
-        out_specs=[row_spec(width), row_spec(inner), row_spec(width), fixed_spec(vec.shape)],
+        out_specs=[row_spec(width), row_spec(inner), row_spec(width), row_spec(width), fixed_spec(vec.shape)],
         out_shape=[
-            shaped(rows, width), shaped(rows, inner), shaped(rows, width, dtype=f32), shaped(*vec.shape, dtype=f32),
+            shaped(rows, width), shaped(rows, inner), shaped(rows, width, dtype=f32), shaped(rows, width),
+            shaped(*vec.shape, dtype=f32),
         ],
+        scratch_shapes=weights.scratch(),
         compiler_params=params(),
-        cost_estimate=cost(4 * rows * width * inner, rows * (width * 16 + inner * 4) + up_proj.size * 4),
+        cost_estimate=cost(4 * rows * width * inner, rows * (width * 16 + inner * 4) + width * inner * 4),
         name="seg_ffn_bwd",
-    )(cot, cls_grad, second_sum, first_sum, slope, up_proj, down_proj, vec)
-
-
-def attn_backward(first_grad, qkv, attn):
+    )(*weights.arrays(place), cot, cls_grad, second_sum, first_sum, slope, vec)
+
+
+def attn_backward(first_grad, attn_low, qkv, place, attn):
     rows, width = first_grad.shape
+    weights = Weights(attn)
     return pl.pallas_call(
-        attn_bwd_kernel,
+        weights.wrap(attn_bwd_kernel),
         grid=(rows // BLOCK,),
-        in_specs=[row_spec(width), row_spec(3 * width), whole_spec(attn.shape)],
-        out_specs=[row_spec(width), row_spec(3 * width), row_spec(width), fixed_spec((8, width))],
-        out_shape=[
-            shaped(rows, width), shaped(rows, 3 * width), shaped(rows, width, dtype=f32), shaped(8, width, dtype=f32),
-        ],
-        scratch_shapes=[pltpu.VMEM((BLOCK, width), bf16)],
+        in_specs=weights.specs() + [row_spec(width), row_spec(width), row_spec(3 * width)],
+        out_specs=[row_spec(3 * width), row_spec(width), fixed_spec((8, width))],
+        out_shape=[shaped(rows, 3 * width), shaped(rows, width, dtype=f32), shaped(8, width, dtype=f32)],
+        scratch_shapes=[pltpu.VMEM((BLOCK, width), bf16)] + weights.scratch(),
         compiler_params=params(),
-        cost_estimate=cost(2 * rows * width * (4 * width + 5 * SEG_LEN), rows * width * 22 + attn.size * 2),
+        cost_estimate=cost(2 * rows * width * (4 * width + 5 * SEG_LEN), rows * width * 22 + width * width * 8),
         name="seg_attn_bwd",
-    )(first_grad, qkv, attn)
-
-
-def cross_layer(entry, cot, row_key, blocks, attn, up_proj, down_proj, vec):
+    )(*weights.arrays(place), first_grad, attn_low, qkv)
+
+
+def cross_layer(entry, cot, row_key, blocks, place, attn, up_proj, down_proj, vec):
     rows, width = entry.shape
     inner = up_proj.shape[1]
     block = rows // blocks
     spec = partial(row_spec, block=block)
+    weights = Weights(attn, up_proj, down_proj)
     return pl.pallas_call(
-        cross_kernel,
+        weights.wrap(cross_kernel),
         grid=(blocks,),
-        in_specs=[
-            spec(width), spec(width), spec(1), pl.BlockSpec((1, 1, block), lambda i: (i, 0, 0)),
-            whole_spec(attn.shape), whole_spec(up_proj.shape), whole_spec(down_proj.shape), whole_spec(vec.shape),
+        in_specs=weights.specs() + [
+            spec(width), spec(width), spec(1), pl.BlockSpec((1, 1, block), lambda i: (i, 0, 0)), whole_spec(vec.shape),
         ],
         out_specs=[
             spec(width), spec(width), spec(width), spec(3 * width), spec(width), spec(width),
@@ -401,23 +483,240 @@
         ],
         scratch_shapes=[
             pltpu.VMEM((block, 3 * width), bf16), pltpu.VMEM((block, width), bf16), pltpu.VMEM((block, inner), f32),
-        ],
+        ] + weights.scratch(),
         compiler_params=params(),
-        cost_estimate=cost(24 * rows * width * 4 * width, rows * width * 40 + attn.size * 6),
+        cost_estimate=cost(24 * rows * width * 4 * width, rows * width * 40 + width * inner * 6),
         name="cross_layer",
-    )(entry, cot, row_key.reshape(rows, 1), row_key.reshape(blocks, 1, block), attn, up_proj, down_proj, vec)
+    )(*weights.arrays(place), entry, cot, row_key.reshape(rows, 1), row_key.reshape(blocks, 1, block), vec)
 
 
 def spread_vec(columns):
     return jnp.concatenate([columns.astype(f32), jnp.zeros((4, columns.shape[1]), f32)], 0)
 
 
-def gather_rows(matrix):
-    return lax.all_gather(matrix, "seg", axis=0, tiled=True)
+def hop_seg(value, hops):
+    size = lax.axis_size("seg")
+    return lax.ppermute(value, "seg", [(at, (at + 2 * hops) % size) for at in range(size)])
+
+
+def swap_core(value):
+    return lax.ppermute(value, "seg", [(at, at ^ 1) for at in range(lax.axis_size("seg"))])
+
+
+def swap_batch(value, flip):
+    return lax.ppermute(value, "batch", [(at, at ^ flip) for at in range(lax.axis_size("batch"))])
+
+
+def fence(*values):
+    return lax.optimization_barrier(values)
+
+
+def by_links():
+    return lax.axis_size("batch") == 4 and lax.axis_size("seg") == 8
+
+
+class Gather:
+    def __init__(self, *shards):
+        self.many = len(shards)
+        self.own, self.cols = shards[0].shape
+        self.quarter = self.cols // 4
+        self.mine = jnp.concatenate(shards, 0) if self.many > 1 else shards[0]
+        self.part = lax.dynamic_slice_in_dim(self.mine, lax.axis_index("batch") * self.quarter, self.quarter, 1)
+
+    def run_seg(self, direct):
+        if direct:
+            self.along = jnp.stack([hop_seg(self.part, hops) for hops in (3, 2, 1)])
+        else:
+            full = chips_exchange(jnp.broadcast_to(self.part, (4,) + self.part.shape))
+            self.along = lax.dynamic_slice_in_dim(jnp.concatenate([full, full[:3]], 0), lax.axis_index("seg") // 2 + 1, 3)
+        self.mine_too = swap_core(self.mine)
+
+    def run_batch(self):
+        self.over = [swap_batch(self.along, flip) for flip in (1, 2, 3)]
+
+    def run_core(self):
+        self.over = jnp.stack([self.along] + self.over)
+        self.over_too = swap_core(self.over)
+
+    def pieces(self):
+        own, cols, quarter = self.own, self.cols, self.quarter
+        arrays = [self.mine, self.over, self.mine_too, self.over_too]
+        matrices = []
+        for at in range(self.many):
+            lines = slice(at * own, (at + 1) * own)
+            blocks = []
+            for core in (0, 1):
+                target = lambda z, c, q, core=core: ((z * 2 + (c ^ core)) * own, 0)
+                blocks.append((2 * core, (lines, slice(None)), (own, cols), target))
+                for flip in range(4):
+                    for later in range(3):
+                        target = lambda z, c, q, core=core, flip=flip, later=later: (
+                            (((z + 1 + later) & 3) * 2 + (c ^ core)) * own, (q ^ flip) * quarter
+                        )
+                        blocks.append((2 * core + 1, (flip, later, lines, slice(None)), (own, quarter), target))
+            matrices.append(Pieces((own * lax.axis_size("seg"), cols), arrays, blocks))
+        return matrices
+
+
+def gather_plain(shard):
+    full = lax.all_gather(shard, "seg", axis=0, tiled=True)
+    block = (0, (slice(None), slice(None)), full.shape, lambda z, c, q: (0, 0))
+    return Pieces(full.shape, [full], [block])
+
+
+def swap_seg(value, flip):
+    return lax.ppermute(value, "seg", [(at, at ^ flip) for at in range(lax.axis_size("seg"))])
+
+
+def chips_exchange(value):
+    groups = [[0, 2, 4, 6], [1, 3, 5, 7]]
+    return lax.all_to_all(value, "seg", 0, 0, axis_index_groups=groups, tiled=True)
+
+
+def gather_seg(value):
+    if not by_links():
+        return lax.all_gather(value, "seg", axis=0, tiled=False)
+    copies = jnp.broadcast_to(value, (lax.axis_size("seg"),) + value.shape)
+    return lax.all_to_all(copies, "seg", 0, 0, tiled=True)
+
+
+def weight_grad_kernel(steps, place_ref, *refs):
+    pairs, (keep_ref, send_ref, acc_ref) = refs[: 2 * len(steps)], refs[2 * len(steps) :]
+    step = pl.program_id(0)
+    begin = 0
+    for at, many in enumerate(steps):
+
+        @pl.when((step >= begin) & (step < begin + many))
+        def _(at=at):
+            acc_ref[...] = dot_tn(pairs[2 * at][...], pairs[2 * at + 1][...])
+
+        begin += many
+    c, q = place_ref[1], place_ref[2]
+    size = keep_ref.shape[2]
+    for flip in range(4):
+        for chip in range(4):
+            for core, out_ref in ((0, keep_ref), (1, send_ref)):
+                row = (chip * 2 + (c ^ core)) * (4 * size) + (q ^ flip) * size
+                rows = pl.ds(pl.multiple_of(row, size), size)
+                out_ref[flip, chip] = acc_ref[rows, :].astype(bf16)
+
+
+def weight_grads(place, *pairs):
+    rows, width = pairs[0][0].shape
+    steps = tuple(right.shape[1] // width for _, right in pairs)
+    size = width // 32
+    in_specs = [pl.BlockSpec(memory_space=pltpu.SMEM)]
+    begin = 0
+    for many in steps:
+        in_specs.append(whole_spec((rows, width)))
+        in_specs.append(pl.BlockSpec((rows, width), lambda i, begin=begin, many=many: (0, jnp.clip(i - begin, 0, many - 1))))
+        begin += many
+    out_spec = pl.BlockSpec((4, 4, size, width), lambda i: (0, 0, 0, i))
+    out = shaped(4, 4, size, begin * width)
+    return pl.pallas_call(
+        partial(weight_grad_kernel, steps),
+        grid=(begin,),
+        in_specs=in_specs,
+        out_specs=[out_spec, out_spec],
+        out_shape=[out, out],
+        scratch_shapes=[pltpu.VMEM((width, width), f32)],
+        compiler_params=params(),
+        cost_estimate=cost(2 * rows * width * width * begin, 2 * (rows + width) * width * begin),
+        name="weight_grads",
+    )(place, *[array for pair in pairs for array in pair])
+
+
+def cross_grad_kernel(*refs):
+    pairs, (out_ref,) = refs[:8], refs[8:]
+    size = out_ref.shape[1]
+    start = 0
+    for at in range(4):
+        cols = pairs[2 * at + 1].shape[1]
+        grad = dot_tn(pairs[2 * at][...], pairs[2 * at + 1][...]).astype(bf16)
+        for part in range(4):
+            out_ref[part, :, start : start + cols] = grad[part * size : (part + 1) * size]
+        start += cols
+
+
+def cross_grads(*pairs):
+    own = pairs[0][0].shape[1]
+    cols = sum(right.shape[1] for _, right in pairs)
+    vmem = pl.BlockSpec(memory_space=pltpu.VMEM)
+    return pl.pallas_call(
+        cross_grad_kernel,
+        in_specs=[vmem] * 8,
+        out_specs=vmem,
+        out_shape=shaped(4, own // 4, cols),
+        compiler_params=pltpu.CompilerParams(vmem_limit_bytes=VMEM_LIMIT),
+        cost_estimate=cost(2 * pairs[0][0].size * cols, own * cols * 2),
+        name="cross_weight_grads",
+    )(*[array for pair in pairs for array in pair])
+
+
+def wide_sum(first, *others):
+    total = first.astype(f32)
+    for other in others:
+        total = total + other.astype(f32)
+    return total
+
+
+def batch_spread(value):
+    value = value.astype(bf16)
+    return [value] + [swap_batch(value, flip) for flip in (1, 2, 3)]
+
+
+def core_sums(keep, got):
+    sums = [wide_sum(keep[flip], got[flip]) for flip in range(4)]
+    return sums[0], [part.astype(bf16) for part in sums[1:]]
+
+
+def batch_swaps(parts):
+    return [swap_batch(part, flip) for flip, part in zip((1, 2, 3), parts)]
+
+
+def chip_sum(value):
+    return jnp.sum(chips_exchange(value.astype(bf16)).astype(f32), 0)
+
+
+def place_kernel(plan, place_ref, *refs):
+    count = 4 * len(plan)
+    blocks, outs = refs[:count], refs[count:]
+    q = place_ref[2]
+    for at, targets in enumerate(plan):
+        for flip in range(4):
+            block = blocks[4 * at + flip]
+            size = block.shape[0]
+            rows = pl.ds(pl.multiple_of((q ^ flip) * size, size), size)
+            for source, index, target, cols in targets:
+                outs[index][rows, target : target + cols] = block[:, source : source + cols].astype(f32)
+
+
+def place_outputs(place, plan, groups, own, shape):
+    vmem = pl.BlockSpec(memory_space=pltpu.VMEM)
+    return pl.pallas_call(
+        partial(place_kernel, plan),
+        in_specs=[pl.BlockSpec(memory_space=pltpu.SMEM)] + [vmem] * (4 * len(groups)),
+        out_specs=[vmem] * own,
+        out_shape=[jax.ShapeDtypeStruct(shape, f32)] * own,
+        compiler_params=pltpu.CompilerParams(vmem_limit_bytes=VMEM_LIMIT),
+        cost_estimate=cost(0, own * shape[0] * shape[1] * 6),
+        name="place_outputs",
+    )(place, *[block for group in groups for block in group])
 
 
 def scatter_sum(matrix):
-    return lax.psum_scatter(matrix, "seg", scatter_dimension=0, tiled=True)
+    return lax.psum_scatter(matrix.astype(bf16), "seg", scatter_dimension=0, tiled=True)
+
+
+def sum_everywhere(seg_sums, cross_sums):
+    if not by_links():
+        return lax.psum(seg_sums, ("batch", "seg")), lax.psum(cross_sums, "batch")
+    for flip in (1, 2, 4):
+        seg_sums = seg_sums + swap_seg(seg_sums, flip)
+    both = jnp.concatenate([seg_sums, cross_sums], 0)
+    for flip in (1, 2):
+        both = both + swap_batch(both, flip)
+    return both[: seg_sums.shape[0]], both[seg_sums.shape[0] :]
 
 
 def local(
@@ -425,85 +724,130 @@
     cross_attn, cross_up, cross_down, cross_vec, tok_cot, cls_cot,
 ):
     micro, _, segments, _, length, width = hidden.shape
-    own = seg_attn.shape[0]
+    own, cols = seg_attn.shape
     parts = lax.axis_size("seg")
     place = lax.axis_index("seg")
     count = micro * segments
     total = parts * count
-
+    spot = jnp.stack([place // 2, place % 2, lax.axis_index("batch")]).astype(jnp.int32)
+
+    flat = hidden.reshape(count * length, width)
     small = jnp.concatenate([cls_cot.reshape(count * width), seg_vec.T.reshape(-1), cross_vec.T.reshape(-1)])
-    small = lax.all_gather(small, "seg", axis=0, tiled=False)
-    cot_all = small[:, : count * width].reshape(total, width)
-    vecs = small[:, count * width :].reshape(parts, 24, own).transpose(1, 0, 2).reshape(24, width)
-    seg_vec_full = spread_vec(vecs[:12])
-    cross_vec_full = spread_vec(vecs[12:])
-
-    attn_full = gather_rows(seg_attn)
-    up_full = gather_rows(seg_up)
-    down_full = gather_rows(seg_down)
-    cross_attn_full = gather_rows(cross_attn)
-    cross_up_full = gather_rows(cross_up)
-    cross_down_full = gather_rows(cross_down)
-
-    flat = hidden.reshape(count * length, width)
-    qkv, mixed, first_sum = attn_forward(flat, attn_full, seg_vec_full)
-    normed, act, slope, second_sum, tok, cls = ffn_forward(first_sum, up_full, down_full, seg_vec_full)
-
-    entry = lax.all_gather(cls.reshape(count, width), "seg", axis=0, tiled=True)
+
+    def spread_small(small):
+        cot_all = small[:, : count * width].reshape(total, width)
+        vecs = small[:, count * width :].reshape(parts, 24, own).transpose(1, 0, 2).reshape(24, width)
+        return cot_all, spread_vec(vecs[:12]), spread_vec(vecs[12:])
+
+    if by_links():
+        one, two, three, four = Gather(seg_attn), Gather(seg_up, seg_down), Gather(cross_attn, cross_up), Gather(cross_down)
+        one.run_seg(True)
+        small = gather_seg(small)
+        one.along, small, two.part, two.mine = fence(one.along, small, two.part, two.mine)
+        cot_all, seg_vec_full, cross_vec_full = spread_small(small)
+        one.run_batch()
+        two.run_seg(False)
+        one.over, two.along, three.part, three.mine = fence(one.over, two.along, three.part, three.mine)
+        one.run_core()
+        two.run_batch()
+        three.run_seg(False)
+        (attn_full,) = one.pieces()
+        outs = attn_forward(flat, spot, attn_full, seg_vec_full)
+        (qkv, mixed, first_sum), two.over, three.along, four.part, four.mine = fence(
+            outs, two.over, three.along, four.part, four.mine
+        )
+        two.run_core()
+        three.run_batch()
+        four.run_seg(False)
+        up_full, down_full = two.pieces()
+        outs = ffn_forward(first_sum, spot, up_full, down_full, seg_vec_full)
+        (normed, act, slope, second_sum, tok, cls), three.over, four.along = fence(outs, three.over, four.along)
+        three.run_core()
+        four.run_batch()
+        entry = gather_seg(cls.reshape(count, width)).reshape(total, width)
+        entry, four.over = fence(entry, four.over)
+        four.run_core()
+        cross_attn_full, cross_up_full = three.pieces()
+        (cross_down_full,) = four.pieces()
+    else:
+        attn_full, up_full, down_full = [gather_plain(shard) for shard in (seg_attn, seg_up, seg_down)]
+        cross_attn_full, cross_up_full, cross_down_full = [
+            gather_plain(shard) for shard in (cross_attn, cross_up, cross_down)
+        ]
+        cot_all, seg_vec_full, cross_vec_full = spread_small(gather_seg(small))
+        qkv, mixed, first_sum = attn_forward(flat, spot, attn_full, seg_vec_full)
+        normed, act, slope, second_sum, tok, cls = ffn_forward(first_sum, spot, up_full, down_full, seg_vec_full)
+        entry = gather_seg(cls.reshape(count, width)).reshape(total, width)
+
     docs = seg_doc[:, 0].reshape(micro, segments, parts) + (1 << 16) * jnp.arange(micro, dtype=jnp.int32)[:, None, None]
+    docs = docs.transpose(2, 0, 1)
     blocks = micro if total > 256 else 1
     if blocks > 1:
         order = lambda rows: rows.reshape(parts, micro, segments, -1).transpose(1, 0, 2, 3).reshape(total, -1)
         back = lambda rows: rows.reshape(micro, parts, segments, -1).transpose(1, 0, 2, 3).reshape(total, -1)
-        row_key = docs.transpose(0, 2, 1).reshape(total)
+        row_key = docs.transpose(1, 0, 2).reshape(total)
     else:
         order = back = lambda rows: rows
-        row_key = docs.transpose(2, 0, 1).reshape(total)
+        row_key = docs.reshape(total)
     (
         cls_out, cls_grad, x_low, x_qkv_grad, x_mixed, x_attn_low, x_norm, x_inner, x_branch, x_act, x_sums,
     ) = cross_layer(
-        order(entry), order(cot_all), row_key, blocks,
+        order(entry), order(cot_all), row_key, blocks, spot,
         cross_attn_full, cross_up_full, cross_down_full, cross_vec_full,
     )
+    own_cols = lambda rows: lax.dynamic_slice_in_dim(rows, place * own, own, 1)
     own_rows = lambda rows: lax.dynamic_slice_in_dim(back(rows), place * count, count, 0)
-    own_cols = lambda rows: lax.dynamic_slice_in_dim(rows, place * own, own, 1)
     cls_out = own_rows(cls_out)
     cls_grad = own_rows(cls_grad)
 
-    branch, inner, first_grad, ffn_sums = ffn_backward(
+    branch, inner, first_grad, attn_low, ffn_sums = ffn_backward(
         tok_cot.reshape(count * length, width),
-        cls_grad.reshape(cls.shape), second_sum, first_sum, slope, up_full, down_full, seg_vec_full,
+        cls_grad.reshape(cls.shape), second_sum, first_sum, slope, spot, up_full, down_full, seg_vec_full,
     )
-    down_grad = dot_tn(branch, act).astype(bf16)
-    up_grad = dot_tn(normed, inner).astype(bf16)
-    attn_low, qkv_grad, hidden_grad, attn_sums = attn_backward(first_grad, qkv, attn_full)
-    attn_grad = jnp.concatenate([dot_tn(flat, qkv_grad), dot_tn(mixed, attn_low)], 1).astype(bf16)
-
-    x_attn_grad = jnp.concatenate(
-        [dot_tn(own_cols(x_low), x_qkv_grad), dot_tn(own_cols(x_mixed), x_attn_low)], 1
+    cross_pairs = (
+        (own_cols(x_low), x_qkv_grad), (own_cols(x_mixed), x_attn_low),
+        (own_cols(x_norm), x_inner), (own_cols(x_branch), x_act),
     )
-    x_up_grad = dot_tn(own_cols(x_norm), x_inner)
-    x_down_grad = dot_tn(own_cols(x_branch), x_act)
-
+
+    if by_links():
+        keep, send = weight_grads(spot, (branch, act), (normed, inner), (mixed, attn_low))
+        got = swap_core(send)
+        x_grads = cross_grads(*cross_pairs)
+        got, x_grads = fence(got, x_grads)
+        stay, leave = core_sums(keep, got)
+        stay, leave, attn_low = fence(stay, leave, attn_low)
+        came = batch_swaps(leave)
+        x_came = lax.all_to_all(x_grads, "batch", 0, 0, tiled=True)
+        outs = attn_backward(first_grad, attn_low, qkv, spot, attn_full)
+        (qkv_grad, hidden_grad, attn_sums), came, x_came = fence(outs, came, x_came)
+        total_one = wide_sum(stay, *came)
+        keep, send = weight_grads(spot, (flat, qkv_grad))
+        set_one = batch_spread(chip_sum(total_one))
+        set_cross = batch_spread(jnp.sum(x_came.astype(f32), 0))
+        stay, leave = core_sums(keep, swap_core(send))
+        set_two = batch_spread(chip_sum(wide_sum(stay, *batch_swaps(leave))))
+        plan = (
+            ((0, 2, 0, cols), (cols, 1, 0, cols), (2 * cols, 0, 3 * width, width)),
+            ((0, 0, 0, 3 * width),),
+            ((0, 3, 0, cols), (cols, 4, 0, cols), (2 * cols, 5, 0, cols)),
+        )
+        grads = place_outputs(spot, plan, (set_one, set_two, set_cross), 6, (own, cols))
+    else:
+        qkv_grad, hidden_grad, attn_sums = attn_backward(first_grad, attn_low, qkv, spot, attn_full)
+        wide = [dot_tn(left, right) for left, right in cross_pairs]
+        grads = [
+            scatter_sum(jnp.concatenate([dot_tn(flat, qkv_grad), dot_tn(mixed, attn_low)], 1)),
+            scatter_sum(dot_tn(normed, inner)), scatter_sum(dot_tn(branch, act)),
+            jnp.concatenate(wide[:2], 1).astype(bf16), wide[2].astype(bf16), wide[3].astype(bf16),
+        ]
+        grads = [grad.astype(f32) for grad in lax.psum(tuple(grads), "batch")]
     sums = jnp.concatenate([attn_sums[:2], ffn_sums[2:12]], 0)
-    vec_sums = scatter_sum(jnp.stack(jnp.split(sums, parts, 1)).astype(bf16))[0]
-    vec_all = jnp.concatenate([vec_sums.astype(f32), own_cols(x_sums[:12])], 0)
-
-    seg_parts = [scatter_sum(down_grad), scatter_sum(up_grad), scatter_sum(attn_grad)]
-    down_sum, up_sum, attn_sum, x_down_sum, x_up_sum, x_attn_sum, vec_all = lax.psum(
-        (
-            seg_parts[0], seg_parts[1], seg_parts[2],
-            x_down_grad.astype(bf16), x_up_grad.astype(bf16), x_attn_grad.astype(bf16), vec_all.astype(bf16),
-        ),
-        "batch",
-    )
-    vec_all = vec_all.astype(f32)
+    seg_sums, x_sums = sum_everywhere(sums, x_sums[:12])
+    seg_vec_grad = own_cols(seg_sums).T
+    cross_vec_grad = own_cols(x_sums).T
     return (
-        tok.reshape(hidden.shape),
-        cls_out.reshape(cls_cot.shape),
-        hidden_grad.reshape(hidden.shape),
-        attn_sum.astype(f32), up_sum.astype(f32), down_sum.astype(f32), vec_all[:12].T,
-        x_attn_sum.astype(f32), x_up_sum.astype(f32), x_down_sum.astype(f32), vec_all[12:].T,
+        tok.reshape(hidden.shape), cls_out.reshape(cls_cot.shape), hidden_grad.reshape(hidden.shape),
+        grads[0], grads[1], grads[2], seg_vec_grad, grads[3], grads[4], grads[5], cross_vec_grad,
     )
 
 

time: 733 us -> 473 us (0.65)
  waiting for transfers between devices: 497 us -> 145 us
  starting transfers between devices: 0.43 us -> 79.8 us
  Pallas kernels: 108 us -> 152 us
  matrix products: 33.7 us -> 0 us
  blocking collectives: 42.3 us -> 13.2 us
  other arithmetic: 13.9 us -> 38.8 us
  local copies, waits for them, and re-layouts: 22.2 us -> 35.1 us
  between operations: 14.2 us -> 1.71 us
    all_gather x6 -> x0, waiting for transfers between devices: 242 us -> none  [gather_rows(): return lax.all_gather(matrix, 'seg', axis=0, tiled=True)]
    reduce_scatter x3 -> x0, waiting for transfers between devices: 139 us -> none  [scatter_sum(): return lax.psum_scatter(matrix, 'seg', scatter_dimension=0, tiled=True)]
    psum x1 -> x0, waiting for transfers between devices: 90.3 us -> none  [local(): lax.psum((seg_parts[0], seg_parts[1], seg_parts[2], x_down_grad.astype(bf...]
    ppermute x0 -> x45, waiting for transfers between devices: none -> 77.5 us  [the longest x29 64.2 us: swap_batch(): lax.ppermute(value, 'batch', [(at, at ^ flip) for at in range(lax.axis_si...]
    all_to_all x0 -> x7, waiting for transfers between devices: none -> 67.5 us  [the longest x5 54.9 us: chips_exchange(): lax.all_to_all(value, 'seg', 0, 0, axis_index_groups=groups, tiled=True)]
    ppermute x0 -> x45, starting transfers between devices: none -> 49.9 us  [the longest x29 35 us: swap_batch(): lax.ppermute(value, 'batch', [(at, at ^ flip) for at in range(lax.axis_si...]
    pallas_call x5 -> x9, Pallas kernels: 108 us -> 152 us  [the longest x1 35.6 us: attn_backward(): pl.pallas_call(weights.wrap(attn_bwd_kernel), grid=(rows // BLOCK,), in_s...]
    dot_general x8 -> x0, matrix products: 33.7 us -> none  [dot_tn(): lax.dot_general(left, right, (((0,), (0,)), ((), ())), preferred_element_...]
  transfers between devices with their start and end apart: 11 -> 52, of which waited for: 11 -> 19; matrix products, arithmetic and copies ran while one was open for 5% -> 12% of each run, Pallas kernels for 5% -> 17%
where the time goes in v2:
time: 473 us; the launch traced here: 465 us
  Pallas kernels  152 us (32%)
  waiting for transfers between devices  145 us (31%)
  starting transfers between devices  79.8 us (17%)
  other arithmetic  38.8 us (8%)
  local copies, waits for them, and re-layouts  35.1 us (7%)
  blocking collectives  13.2 us (3%)
    ppermute x29, waiting for transfers between devices, swap_batch(): lax.ppermute(value, 'batch', [(at, at ^ flip) for at in range(lax.axis_si...  64.2 us
    all_to_all x5, waiting for transfers between devices, chips_exchange(): lax.all_to_all(value, 'seg', 0, 0, axis_index_groups=groups, tiled=True)  54.9 us
    pallas_call x1, Pallas kernels, attn_backward(): pl.pallas_call(weights.wrap(attn_bwd_kernel), grid=(rows // BLOCK,), in_s...  35.6 us
    ppermute x29, starting transfers between devices, swap_batch(): lax.ppermute(value, 'batch', [(at, at ^ flip) for at in range(lax.axis_si...  35 us
    pallas_call x2, Pallas kernels, weight_grads(): pl.pallas_call(partial(weight_grad_kernel, steps), grid=(begin,), in_spec...  28 us
    pallas_call x1, Pallas kernels, ffn_backward(): pl.pallas_call(weights.wrap(ffn_bwd_kernel), grid=(rows // BLOCK,), in_sp...  22.3 us
    pallas_call x1, Pallas kernels, ffn_forward(): pl.pallas_call(weights.wrap(ffn_fwd_kernel), grid=(rows // BLOCK,), in_sp...  22 us
    all_to_all x5, starting transfers between devices, chips_exchange(): lax.all_to_all(value, 'seg', 0, 0, axis_index_groups=groups, tiled=True)  21.2 us
  transfers between devices with their start and end apart: 52, of which 19 were waited for; matrix products, arithmetic and copies ran while one was open for 12% of the time, Pallas kernels for 17%

profile of v2, /device:TPU:0, one launch (start us, length us, event | category | flops | bytes accessed | tf_op | source)
XLA Modules:
  0.0 465.3 jit_solution(5189530017766618851)
XLA Ops:
  1.7 5.1 %collective-permute-start = (bf16[96,768]{1,0:T(8,128)(2,1)S(1)}, bf16[96,768]{1,0:T(8,128)(2,1)S(1)}, u32[]{:S(2)}, u32[]{:S(2)}) collective-permute-start(bf16[96,768]{1,0:T(8,128)(2,1)S(1)} %constant_dynamic-slice_fusion.9), channel_id=1, source_target_pairs={{0,6},{1,7},{2,0},{3,1},{4,2},{5,3},{6,4},{7,5},{8,14},{9,15},{10,... | collective-permute-start | bytes 442376 | tf_op jit(solution)/shard_map/ppermute | solution.py:499
  34.9 22.2 %all-to-all-done.1 = bf16[4,192,768]{2,1,0:T(8,128)(2,1)S(1)} async-done(((bf16[4,192,768]{2,1,0:T(8,128)(2,1)}), bf16[4,192,768]{2,1,0:T(8,128)(2,1)S(1)}, u32[]{:S(2)}, u32[]{:S(2)}) %all-to-all-start.1) | async-done | bytes 1179680 | tf_op jit(solution)/shard_map/all_to_all | solution.py:573
  72.1 18.1 %all-to-all-done.2 = bf16[4,192,768]{2,1,0:T(8,128)(2,1)S(1)} async-done(((bf16[4,192,768]{2,1,0:T(8,128)(2,1)}), bf16[4,192,768]{2,1,0:T(8,128)(2,1)S(1)}, u32[]{:S(2)}, u32[]{:S(2)}) %all-to-all-start.2) | async-done | bytes 1179680 | tf_op jit(solution)/shard_map/all_to_all | solution.py:573
  90.6 16.1 %seg_attn_fwd.1 = (bf16[1024,2304]{1,0:T(8,128)(2,1)}, bf16[1024,768]{1,0:T(8,128)(2,1)}, f32[1024,768]{1,0:T(8,128)}) custom-call(s32[3]{0:T(128)} %pad_add_fusion.place_ref, bf16[96,3072]{1,0:T(8,128)(2,1)} %refs_0_.3, bf16[4,3,96,768]{3,2,1,0:T(8,128)(2,1)} %pad_maximum_fusion.2.refs_1_, bf16[96,3072]{1,0:T(8,128)(2,1)} %collective-permute-done.6.refs_2_, ...), custom_call_target="tpu_custom_call" | custom-call | flops 5234491392 | bytes 15728640 | tf_op jit(solution)/shard_map/seg_attn_fwd/pallas_call | solution.py:388
  113.6 5.6 %all-to-all-start.3 = ((bf16[4,96,768]{2,1,0:T(8,128)(2,1)}), bf16[4,96,768]{2,1,0:T(8,128)(2,1)S(1)}, u32[]{:S(2)}, u32[]{:S(2)}) async-start(bf16[4,96,768]{2,1,0:T(8,128)(2,1)} %broadcast_in_dim.19), calls=%async_computation.3 | async-start | bytes 1179648 | tf_op jit(solution)/shard_map/all_to_all | solution.py:573
  122.7 12.5 %all-to-all-done.3 = bf16[4,96,768]{2,1,0:T(8,128)(2,1)S(1)} async-done(((bf16[4,96,768]{2,1,0:T(8,128)(2,1)}), bf16[4,96,768]{2,1,0:T(8,128)(2,1)S(1)}, u32[]{:S(2)}, u32[]{:S(2)}) %all-to-all-start.3) | async-done | bytes 589856 | tf_op jit(solution)/shard_map/all_to_all | solution.py:573
  136.2 22.0 %seg_ffn_fwd.1 = (bf16[1024,768]{1,0:T(8,128)(2,1)}, bf16[1024,3072]{1,0:T(8,128)(2,1)}, bf16[1024,3072]{1,0:T(8,128)(2,1)}, f32[1024,768]{1,0:T(8,128)}, bf16[1...) custom-call(s32[3]{0:T(128)} %pad_add_fusion.place_ref, bf16[192,3072]{1,0:T(8,128)(2,1)} %constant_dynamic-update-slice_fusion.refs_0_.refs_4_, ...), custom_call_target="tpu_custom_call" | custom-call | flops 9663676416 | bytes 31457280 | tf_op jit(solution)/shard_map/seg_ffn_fwd/pallas_call | solution.py:407
  169.6 13.2 %all_to_all.44 = f32[8,8,768]{2,1,0:T(8,128)} all-to-all(f32[8,8,768]{2,1,0:T(8,128)S(1)} %broadcast_in_dim.20), channel_id=1, replica_groups=mesh['batch'=4,'seg'=8] {'seg'}, dimensions={0} | all-to-all | bytes 393216 | tf_op jit(solution)/shard_map/all_to_all | solution.py:580
  182.8 4.3 collective-permute-done.20
  200.6 19.3 %cross_layer.1 = (bf16[64,768]{1,0:T(8,128)(2,1)}, f32[64,768]{1,0:T(8,128)}, bf16[64,768]{1,0:T(8,128)(2,1)}, bf16[64,2304]{1,0:T(8,128)(2,1)}, bf16[64,768]{1,...) custom-call(s32[3]{0:T(128)} %pad_add_fusion.place_ref, ...), custom_call_target="tpu_custom_call" | custom-call | flops 3623878656 | bytes 16121856 | tf_op jit(solution)/shard_map/cross_layer/pallas_call | solution.py:469
  221.2 22.3 %seg_ffn_bwd.1 = (bf16[1024,768]{1,0:T(8,128)(2,1)}, bf16[1024,3072]{1,0:T(8,128)(2,1)}, f32[1024,768]{1,0:T(8,128)}, bf16[1024,768]{1,0:T(8,128)(2,1)}, f32[16,768]{1,0:T(8,128)}) custom-call(s32[3]{0:T(128)} %pad_add_fusion.place_ref, bf16[192,3072]{1,0:T(8,128)(2,1)} %constant_dynamic-update-slice_fusion.refs_0_.refs_4_, ...), custom_call_target="tpu_custom_call" | custom-call | flops 9663676416 | bytes 34603008 | tf_op jit(solution)/shard_map/seg_ffn_bwd/pallas_call | solution.py:429
  243.5 20.0 %weight_grads.2 = (bf16[4,4,24,6912]{3,2,1,0:T(8,128)(2,1)}, bf16[4,4,24,6912]{3,2,1,0:T(8,128)(2,1)}) custom-call(s32[3]{0:T(128)} %pad_add_fusion.place_ref, bf16[1024,768]{1,0:T(8,128)(2,1)} %get-tuple-element.137.refs_0_, bf16[1024,3072]{1,0:T(8,128)(2,1)} %get-tuple-element.138.refs_1_, bf16[1024,768]{1,0:T(8,128)(2,1)} %get-tuple-element.139.refs_2_, ...), custom_call_target="tpu_custom_call" | custom-call | flops 10871635968 | bytes 24772608 | tf_op jit(solution)/shard_map/weight_grads/pallas_call | solution.py:616
  272.8 6.4 %fusion.2 = (bf16[4,24,6912]{2,1,0:T(8,128)(2,1)}, bf16[4,24,6912]{2,1,0:T(8,128)(2,1)}, bf16[4,24,6912]{2,1,0:T(8,128)(2,1)}, f32[4,24,6912]{2,1,0:T(8,128)S(1)}) fusion(bf16[4,4,24,6912]{3,2,1,0:T(8,128)(2,1)} %collective-permute-done.23, bf16[4,4,24,6912]{3,2,1,0:T(8,128)(2,1)} %get-tuple-element.143), kind=kLoop, calls=%fused_computation.15 | loop fusion | flops 9953280 | bytes 17252352 | tf_op jit(solution)/shard_map/convert_element_type | solution.py:670
  282.7 4.7 %all-to-all-start.5 = ((bf16[4,24,9216]{2,1,0:T(8,128)(2,1)}), bf16[4,24,9216]{2,1,0:T(8,128)(2,1)}, u32[]{:S(2)}, u32[]{:S(2)}) async-start(bf16[4,24,9216]{2,1,0:T(8,128)(2,1)} %cross_weight_grads.1), calls=%async_computation.5 | async-start | bytes 3538944 | tf_op jit(solution)/shard_map/all_to_all | solution.py:820
  287.4 35.6 %seg_attn_bwd.1 = (bf16[1024,2304]{1,0:T(8,128)(2,1)}, f32[1024,768]{1,0:T(8,128)}, f32[8,768]{1,0:T(8,128)}) custom-call(s32[3]{0:T(128)} %pad_add_fusion.place_ref, bf16[96,3072]{1,0:T(8,128)(2,1)} %refs_0_.3, bf16[4,3,96,768]{3,2,1,0:T(8,128)(2,1)} %pad_maximum_fusion.2.refs_1_, bf16[96,3072]{1,0:T(8,128)(2,1)} %collective-permute-done.6.refs_2_, ...), custom_call_target="tpu_custom_call" | custom-call | flops 5838471168 | bytes 22020096 | tf_op jit(solution)/shard_map/seg_attn_bwd/pallas_call | solution.py:450
  323.0 27.4 %collective-permute-done.25 = bf16[4,24,6912]{2,1,0:T(8,128)(2,1)} collective-permute-done((bf16[4,24,6912]{2,1,0:T(8,128)(2,1)}, bf16[4,24,6912]{2,1,0:T(8,128)(2,1)}, u32[]{:S(2)}, u32[]{:S(2)}) %collective-permute-start.25) | collective-permute-done | bytes 1327136 | tf_op jit(solution)/shard_map/ppermute | solution.py:507
  350.4 8.6 %all-to-all-done.5 = bf16[4,24,9216]{2,1,0:T(8,128)(2,1)} async-done(((bf16[4,24,9216]{2,1,0:T(8,128)(2,1)}), bf16[4,24,9216]{2,1,0:T(8,128)(2,1)}, u32[]{:S(2)}, u32[]{:S(2)}) %all-to-all-start.5) | async-done | bytes 1769504 | tf_op jit(solution)/shard_map/all_to_all | solution.py:820
  359.0 7.9 %weight_grads.3 = (bf16[4,4,24,2304]{3,2,1,0:T(8,128)(2,1)}, bf16[4,4,24,2304]{3,2,1,0:T(8,128)(2,1)}) custom-call(s32[3]{0:T(128)} %pad_add_fusion.place_ref, bf16[1024,768]{1,0:T(8,128)(2,1)} %bitcast.85, bf16[1024,2304]{1,0:T(8,128)(2,1)} %get-tuple-element.168.refs_1_), custom_call_target="tpu_custom_call" | custom-call | flops 3623878656 | bytes 8257536 | tf_op jit(solution)/shard_map/weight_grads/pallas_call | solution.py:616
  370.7 4.9 %all-to-all-start.6 = ((bf16[4,24,6912]{2,1,0:T(8,128)(2,1)}), bf16[4,24,6912]{2,1,0:T(8,128)(2,1)S(1)}, u32[]{:S(2)}, u32[]{:S(2)}) async-start(bf16[4,24,6912]{2,1,0:T(8,128)(2,1)} %add_convert_fusion), calls=%async_computation.6 | async-start | bytes 2654208 | tf_op jit(solution)/shard_map/all_to_all | solution.py:573
  389.5 9.5 %collective-permute-done.41 = f32[12,768]{1,0:T(8,128)} collective-permute-done((f32[12,768]{1,0:T(8,128)}, f32[12,768]{1,0:T(8,128)}, u32[]{:S(2)}, u32[]{:S(2)}) %collective-permute-start.41) | collective-permute-done | bytes 36896 | tf_op jit(solution)/shard_map/ppermute | solution.py:568
  400.5 4.6 collective-permute-start.42
  422.7 15.0 %collective-permute-done.44 = f32[24,768]{1,0:T(8,128)S(1)} collective-permute-done((f32[24,768]{1,0:T(8,128)S(1)}, f32[24,768]{1,0:T(8,128)S(1)}, u32[]{:S(2)}, u32[]{:S(2)}) %collective-permute-start.44) | collective-permute-done | bytes 73760 | tf_op jit(solution)/shard_map/ppermute | solution.py:507
  451.3 4.7 %collective-permute-done.28.refs_2_ = bf16[24,6912]{1,0:T(8,128)(2,1)S(1)} collective-permute-done((bf16[24,6912]{1,0:T(8,128)(2,1)S(1)}, bf16[24,6912]{1,0:T(8,128)(2,1)S(1)}, u32[]{:S(2)}, u32[]{:S(2)}) %collective-permute-start.28) | collective-permute-done | bytes 331808 | tf_op jit(solution)/shard_map/ppermute | solution.py:507
  459.6 5.2 %place_outputs.1 = (f32[96,3072]{1,0:T(8,128)}, f32[96,3072]{1,0:T(8,128)}, f32[96,3072]{1,0:T(8,128)}, f32[96,3072]{1,0:T(8,128)}, f32[96,3072]{1,0:T(8,128)}, /*index=5*/f32[96,3072]{1,0:T(8,128)}) custom-call(s32[3]{0:T(128)} %pad_add_fusion.place_ref, bf16[24,6912]{1,0:T(8,128)(2,1)} %copy-done.4, bf16[24,6912]{1,0:T(8,128)(2,1)} %copy-done.15, ...), custom_call_target="tpu_custom_call" | custom-call | bytes 10616832 | tf_op jit(solution)/shard_map/place_outputs/pallas_call | solution.py:696
  (215 shorter events, 148.3 us)
Async XLA Ops:
  25.0 32.1 %all-to-all-start.1 = ((bf16[4,192,768]{2,1,0:T(8,128)(2,1)}), bf16[4,192,768]{2,1,0:T(8,128)(2,1)S(1)}, u32[]{:S(2)}, u32[]{:S(2)}) async-start(bf16[4,192,768]{2,1,0:T(8,128)(2,1)} %broadcast_in_dim.17), calls=%async_computation.1 | async-start | bytes 2359296 | tf_op jit(solution)/shard_map/all_to_all | solution.py:573
  29.6 28.0 %collective-permute-start.3 = (bf16[3,96,768]{2,1,0:T(8,128)(2,1)S(1)}, bf16[3,96,768]{2,1,0:T(8,128)(2,1)}, u32[]{:S(2)}, u32[]{:S(2)}) collective-permute-start(bf16[3,96,768]{2,1,0:T(8,128)(2,1)S(1)} %pad_maximum_fusion.4), channel_id=1, source_target_pairs={{0,8},{8,0},{16,24},{24,16},{1,9},{9,1},{17,25},{25,17},{2,10},{10... | collective-permute-start | bytes 1327112 | tf_op jit(solution)/shard_map/ppermute | solution.py:507
  31.1 26.5 %collective-permute-start.4 = (bf16[3,96,768]{2,1,0:T(8,128)(2,1)S(1)}, bf16[3,96,768]{2,1,0:T(8,128)(2,1)}, u32[]{:S(2)}, u32[]{:S(2)}) collective-permute-start(bf16[3,96,768]{2,1,0:T(8,128)(2,1)S(1)} %pad_maximum_fusion.4), channel_id=1, source_target_pairs={{0,16},{8,24},{16,0},{24,8},{1,17},{9,25},{17,1},{25,9},{2,18},{10... | collective-permute-start | bytes 1327112 | tf_op jit(solution)/shard_map/ppermute | solution.py:507
  58.7 31.5 %all-to-all-start.2 = ((bf16[4,192,768]{2,1,0:T(8,128)(2,1)}), bf16[4,192,768]{2,1,0:T(8,128)(2,1)S(1)}, u32[]{:S(2)}, u32[]{:S(2)}) async-start(bf16[4,192,768]{2,1,0:T(8,128)(2,1)} %broadcast_in_dim.18), calls=%async_computation.2 | async-start | bytes 2359296 | tf_op jit(solution)/shard_map/all_to_all | solution.py:573
  65.0 25.7 %collective-permute-start.7 = (bf16[4,3,96,768]{3,2,1,0:T(8,128)(2,1)}, bf16[4,3,96,768]{3,2,1,0:T(8,128)(2,1)}, u32[]{:S(2)}, u32[]{:S(2)}) collective-permute-start(bf16[4,3,96,768]{3,2,1,0:T(8,128)(2,1)} %pad_maximum_fusion.2.refs_1_), channel_id=1, source_target_pairs={{0,1},{1,0},{2,3},{3,2},{4,5},{5,4},{6,7},{7,6},{8,9},{9,8},{10,11... | collective-permute-start | bytes 5308424 | tf_op jit(solution)/shard_map/ppermute | solution.py:503
  65.0 25.7 %collective-permute-start.6 = (bf16[96,3072]{1,0:T(8,128)(2,1)}, bf16[96,3072]{1,0:T(8,128)(2,1)}, u32[]{:S(2)}, u32[]{:S(2)}) collective-permute-start(bf16[96,3072]{1,0:T(8,128)(2,1)} %refs_0_.3), channel_id=1, source_target_pairs={{0,1},{1,0},{2,3},{3,2},{4,5},{5,4},{6,7},{7,6},{8,9},{9,8},{10,11... | collective-permute-start | bytes 1769480 | tf_op jit(solution)/shard_map/ppermute | solution.py:503
  67.2 39.5 %collective-permute-start.10 = (bf16[3,192,768]{2,1,0:T(8,128)(2,1)S(1)}, bf16[3,192,768]{2,1,0:T(8,128)(2,1)}, u32[]{:S(2)}, u32[]{:S(2)}) collective-permute-start(bf16[3,192,768]{2,1,0:T(8,128)(2,1)S(1)} %fusion.4), channel_id=1, source_target_pairs={{0,24},{8,16},{16,8},{24,0},{1,25},{9,17},{17,9},{25,1},{2,26},{10... | collective-permute-start | bytes 2654216 | tf_op jit(solution)/shard_map/ppermute | solution.py:507
  69.7 39.2 %collective-permute-start.8 = (bf16[3,192,768]{2,1,0:T(8,128)(2,1)S(1)}, bf16[3,192,768]{2,1,0:T(8,128)(2,1)}, u32[]{:S(2)}, u32[]{:S(2)}) collective-permute-start(bf16[3,192,768]{2,1,0:T(8,128)(2,1)S(1)} %fusion.4), channel_id=1, source_target_pairs={{0,8},{8,0},{16,24},{24,16},{1,9},{9,1},{17,25},{25,17},{2,10},{10... | collective-permute-start | bytes 2654216 | tf_op jit(solution)/shard_map/ppermute | solution.py:507
  70.2 38.6 %collective-permute-start.9 = (bf16[3,192,768]{2,1,0:T(8,128)(2,1)S(1)}, bf16[3,192,768]{2,1,0:T(8,128)(2,1)}, u32[]{:S(2)}, u32[]{:S(2)}) collective-permute-start(bf16[3,192,768]{2,1,0:T(8,128)(2,1)S(1)} %fusion.4), channel_id=1, source_target_pairs={{0,16},{8,24},{16,0},{24,8},{1,17},{9,25},{17,1},{25,9},{2,18},{10... | collective-permute-start | bytes 2654216 | tf_op jit(solution)/shard_map/ppermute | solution.py:507
  119.2 39.0 %collective-permute-start.13 = (bf16[3,192,768]{2,1,0:T(8,128)(2,1)S(1)}, bf16[3,192,768]{2,1,0:T(8,128)(2,1)S(1)}, u32[]{:S(2)}, u32[]{:S(2)}) collective-permute-start(bf16[3,192,768]{2,1,0:T(8,128)(2,1)S(1)} %fusion.3), channel_id=1, source_target_pairs={{0,8},{8,0},{16,24},{24,16},{1,9},{9,1},{17,25},{25,17},{2,10},{10... | collective-permute-start | bytes 2654216 | tf_op jit(solution)/shard_map/ppermute | solution.py:507
  120.7 40.0 %collective-permute-start.14 = (bf16[3,192,768]{2,1,0:T(8,128)(2,1)S(1)}, bf16[3,192,768]{2,1,0:T(8,128)(2,1)S(1)}, u32[]{:S(2)}, u32[]{:S(2)}) collective-permute-start(bf16[3,192,768]{2,1,0:T(8,128)(2,1)S(1)} %fusion.3), channel_id=1, source_target_pairs={{0,16},{8,24},{16,0},{24,8},{1,17},{9,25},{17,1},{25,9},{2,18},{10... | collective-permute-start | bytes 2654216 | tf_op jit(solution)/shard_map/ppermute | solution.py:507
  122.1 38.5 %collective-permute-start.15 = (bf16[3,192,768]{2,1,0:T(8,128)(2,1)S(1)}, bf16[3,192,768]{2,1,0:T(8,128)(2,1)}, u32[]{:S(2)}, u32[]{:S(2)}) collective-permute-start(bf16[3,192,768]{2,1,0:T(8,128)(2,1)S(1)} %fusion.3), channel_id=1, source_target_pairs={{0,24},{8,16},{16,8},{24,0},{1,25},{9,17},{17,9},{25,1},{2,26},{10... | collective-permute-start | bytes 2654216 | tf_op jit(solution)/shard_map/ppermute | solution.py:507
  163.8 36.8 %collective-permute-start.17 = (bf16[4,3,192,768]{3,2,1,0:T(8,128)(2,1)S(1)}, bf16[4,3,192,768]{3,2,1,0:T(8,128)(2,1)}, u32[]{:S(2)}, u32[]{:S(2)}) collective-permute-start(bf16[4,3,192,768]{3,2,1,0:T(8,128)(2,1)S(1)} %pad_maximum_fusion.1.refs_1_.refs_5_), channel_id=1, source_target_pairs={{0,1},{1,0},{2,3},{3,2},{4,5},{5,4},{6,7},{7,6},{8,9},{9,8},{10,11... | collective-permute-start | bytes 10616840 | tf_op jit(solution)/shard_map/ppermute | solution.py:503
  279.2 43.7 %collective-permute-start.24 = (bf16[4,24,6912]{2,1,0:T(8,128)(2,1)}, bf16[4,24,6912]{2,1,0:T(8,128)(2,1)}, u32[]{:S(2)}, u32[]{:S(2)}) collective-permute-start(bf16[4,24,6912]{2,1,0:T(8,128)(2,1)} %get-tuple-element.159), channel_id=1, source_target_pairs={{0,8},{8,0},{16,24},{24,16},{1,9},{9,1},{17,25},{25,17},{2,10},{10... | collective-permute-start | bytes 3981320 | tf_op jit(solution)/shard_map/ppermute | solution.py:507
  280.1 70.2 %collective-permute-start.25 = (bf16[4,24,6912]{2,1,0:T(8,128)(2,1)}, bf16[4,24,6912]{2,1,0:T(8,128)(2,1)}, u32[]{:S(2)}, u32[]{:S(2)}) collective-permute-start(bf16[4,24,6912]{2,1,0:T(8,128)(2,1)} %get-tuple-element.160), channel_id=1, source_target_pairs={{0,16},{8,24},{16,0},{24,8},{1,17},{9,25},{17,1},{25,9},{2,18},{10... | collective-permute-start | bytes 3981320 | tf_op jit(solution)/shard_map/ppermute | solution.py:507
  281.6 68.8 %collective-permute-start.26 = (bf16[4,24,6912]{2,1,0:T(8,128)(2,1)}, bf16[4,24,6912]{2,1,0:T(8,128)(2,1)}, u32[]{:S(2)}, u32[]{:S(2)}) collective-permute-start(bf16[4,24,6912]{2,1,0:T(8,128)(2,1)} %get-tuple-element.161), channel_id=1, source_target_pairs={{0,24},{8,16},{16,8},{24,0},{1,25},{9,17},{17,9},{25,1},{2,26},{10... | collective-permute-start | bytes 3981320 | tf_op jit(solution)/shard_map/ppermute | solution.py:507
  282.7 76.2 %all-to-all-start.5 = ((bf16[4,24,9216]{2,1,0:T(8,128)(2,1)}), bf16[4,24,9216]{2,1,0:T(8,128)(2,1)}, u32[]{:S(2)}, u32[]{:S(2)}) async-start(bf16[4,24,9216]{2,1,0:T(8,128)(2,1)} %cross_weight_grads.1), calls=%async_computation.5 | async-start | bytes 3538944 | tf_op jit(solution)/shard_map/all_to_all | solution.py:820
  370.7 38.9 %all-to-all-start.6 = ((bf16[4,24,6912]{2,1,0:T(8,128)(2,1)}), bf16[4,24,6912]{2,1,0:T(8,128)(2,1)S(1)}, u32[]{:S(2)}, u32[]{:S(2)}) async-start(bf16[4,24,6912]{2,1,0:T(8,128)(2,1)} %add_convert_fusion), calls=%async_computation.6 | async-start | bytes 2654208 | tf_op jit(solution)/shard_map/all_to_all | solution.py:573
  378.2 26.9 %collective-permute-start.31 = (bf16[4,24,2304]{2,1,0:T(8,128)(2,1)}, bf16[4,24,2304]{2,1,0:T(8,128)(2,1)}, u32[]{:S(2)}, u32[]{:S(2)}) collective-permute-start(bf16[4,24,2304]{2,1,0:T(8,128)(2,1)} %get-tuple-element.229), channel_id=1, source_target_pairs={{0,8},{8,0},{16,24},{24,16},{1,9},{9,1},{17,25},{25,17},{2,10},{10... | collective-permute-start | bytes 1327112 | tf_op jit(solution)/shard_map/ppermute | solution.py:507
  379.4 25.7 %collective-permute-start.32 = (bf16[4,24,2304]{2,1,0:T(8,128)(2,1)}, bf16[4,24,2304]{2,1,0:T(8,128)(2,1)}, u32[]{:S(2)}, u32[]{:S(2)}) collective-permute-start(bf16[4,24,2304]{2,1,0:T(8,128)(2,1)} %get-tuple-element.231), channel_id=1, source_target_pairs={{0,16},{8,24},{16,0},{24,8},{1,17},{9,25},{17,1},{25,9},{2,18},{10... | collective-permute-start | bytes 1327112 | tf_op jit(solution)/shard_map/ppermute | solution.py:507
  388.2 52.2 %collective-permute-start.37 = (bf16[24,9216]{1,0:T(8,128)(2,1)S(1)}, bf16[24,9216]{1,0:T(8,128)(2,1)}, u32[]{:S(2)}, u32[]{:S(2)}) collective-permute-start(bf16[24,9216]{1,0:T(8,128)(2,1)S(1)} %reduce_sum.38.refs_8_), channel_id=1, source_target_pairs={{0,8},{8,0},{16,24},{24,16},{1,9},{9,1},{17,25},{25,17},{2,10},{10... | collective-permute-start | bytes 1327112 | tf_op jit(solution)/shard_map/ppermute | solution.py:507
  409.6 32.7 %all-to-all-start.7 = ((bf16[4,24,2304]{2,1,0:T(8,128)(2,1)}), bf16[4,24,2304]{2,1,0:T(8,128)(2,1)S(1)}, u32[]{:S(2)}, u32[]{:S(2)}) async-start(bf16[4,24,2304]{2,1,0:T(8,128)(2,1)} %fusion.7), calls=%async_computation.7 | async-start | bytes 884736 | tf_op jit(solution)/shard_map/all_to_all | solution.py:573
  416.0 26.4 %collective-permute-start.38 = (bf16[24,9216]{1,0:T(8,128)(2,1)S(1)}, bf16[24,9216]{1,0:T(8,128)(2,1)S(1)}, u32[]{:S(2)}, u32[]{:S(2)}) collective-permute-start(bf16[24,9216]{1,0:T(8,128)(2,1)S(1)} %reduce_sum.38.refs_8_), channel_id=1, source_target_pairs={{0,16},{8,24},{16,0},{24,8},{1,17},{9,25},{17,1},{25,9},{2,18},{10... | collective-permute-start | bytes 1327112 | tf_op jit(solution)/shard_map/ppermute | solution.py:507
  416.8 26.6 %collective-permute-start.39 = (bf16[24,9216]{1,0:T(8,128)(2,1)S(1)}, bf16[24,9216]{1,0:T(8,128)(2,1)S(1)}, u32[]{:S(2)}, u32[]{:S(2)}) collective-permute-start(bf16[24,9216]{1,0:T(8,128)(2,1)S(1)} %reduce_sum.38.refs_8_), channel_id=1, source_target_pairs={{0,24},{8,16},{16,8},{24,0},{1,25},{9,17},{17,9},{25,1},{2,26},{10... | collective-permute-start | bytes 1327112 | tf_op jit(solution)/shard_map/ppermute | solution.py:507
  (51 other events, 693.9 us)

commit v3 on v2

--- a/solution.py
+++ b/solution.py
@@ -19,6 +19,7 @@
 ROOT_HALF = 0.7071067811865476
 PDF_AT_ZERO = 0.3989422804014327
 BLOCK = 256
+CHIP_GROUPS = [[0, 2, 4, 6], [1, 3, 5, 7]]
 VMEM_LIMIT = 60 * 1024 * 1024
 
 f32 = jnp.float32
@@ -152,14 +153,14 @@
     def scratch(self):
         return [item for matrix in self.matrices for item in matrix.scratch()]
 
-    def wrap(self, body, step_axis=0):
+    def wrap(self, body, with_place=False):
         many = sum(len(matrix.arrays) for matrix in self.matrices)
 
         def kernel(place_ref, *refs):
             given, rest = refs[:many], refs[many:]
             cut = len(rest) - 2 * len(self.matrices)
             rest, own = rest[:cut], rest[cut:]
-            first = pl.program_id(step_axis) == 0
+            first = pl.program_id(0) == 0
             views, copies = [], []
             for at, matrix in enumerate(self.matrices):
                 views.append(own[2 * at])
@@ -180,9 +181,16 @@
 
                 return views[at]
 
-            body(ready, *rest)
+            body(ready, *([place_ref] if with_place else []), *rest)
 
         return kernel
+
+
+def load_vec(small_ref, skip, own, vec_ref):
+    @pl.when(pl.program_id(0) == 0)
+    def _():
+        for part in range(small_ref.shape[0]):
+            vec_ref[0:12, part * own : (part + 1) * own] = small_ref[part, skip : skip + 12, :own].astype(f32)
 
 
 def qkv_bias(vec_ref):
@@ -190,8 +198,9 @@
     return jnp.concatenate([query, jnp.zeros_like(query), vec_ref[1:2, :]], 1)
 
 
-def attn_fwd_kernel(ready, x_ref, vec_ref, qkv_ref, mixed_ref, sum_ref):
+def attn_fwd_kernel(layout, ready, x_ref, small_ref, qkv_ref, mixed_ref, sum_ref, vec_ref):
     width = x_ref.shape[1]
+    load_vec(small_ref, *layout, vec_ref)
     w_ref = ready(0)
     rows = x_ref[...]
     qkv = dot_nn(rows, w_ref[:, : 3 * width]) + qkv_bias(vec_ref)
@@ -203,8 +212,9 @@
     sum_ref[...] = rows.astype(f32) + branch + vec_ref[2:3, :]
 
 
-def ffn_fwd_kernel(ready, sum_ref, vec_ref, norm_ref, act_ref, slope_ref, second_ref, tok_ref, cls_ref):
+def ffn_fwd_kernel(layout, ready, sum_ref, small_ref, norm_ref, act_ref, slope_ref, second_ref, tok_ref, cls_ref, vec_ref):
     width = sum_ref.shape[1]
+    load_vec(small_ref, *layout, vec_ref)
     up_ref = ready(0)
     down_ref = ready(1)
     unit, _ = normalise(sum_ref[...])
@@ -224,12 +234,22 @@
     unit, _ = normalise(total)
     result = unit * vec_ref[6:7, :] + vec_ref[7:8, :]
     tok_ref[...] = result.astype(bf16)
-    for index in range(sum_ref.shape[0] // SEG_LEN):
-        cls_ref[0, index : index + 1, :] = result[index * SEG_LEN : index * SEG_LEN + 1, :]
-
-
-def ffn_bwd_kernel(ready, cot_ref, cls_ref, second_ref, sum_ref, slope_ref, vec_ref, branch_ref, inner_ref, first_ref, low_ref, sums_ref):
+    per = sum_ref.shape[0] // SEG_LEN
+    for index in range(per):
+        row = jnp.broadcast_to(result[index * SEG_LEN : index * SEG_LEN + 1, :][None], (cls_ref.shape[0], 1, width))
+        cls_ref[:, pl.ds(pl.program_id(0) * per + index, 1), :] = row
+
+
+def ffn_bwd_kernel(
+    layout, ready, place_ref, cot_ref, cls_ref, second_ref, sum_ref, slope_ref, small_ref,
+    branch_ref, inner_ref, first_ref, low_ref, sums_ref, vec_ref,
+):
     width = sum_ref.shape[1]
+    load_vec(small_ref, *layout, vec_ref)
+    per = sum_ref.shape[0] // SEG_LEN
+    begin = pl.program_id(0) * per
+    if cls_ref.shape[0] > per * pl.num_programs(0):
+        begin = begin + (place_ref[0] * 2 + place_ref[1]) * (per * pl.num_programs(0))
 
     @pl.when(pl.program_id(0) == 0)
     def _():
@@ -239,7 +259,7 @@
     parts = []
     for index in range(sum_ref.shape[0] // SEG_LEN):
         rows = cot_ref[index * SEG_LEN : (index + 1) * SEG_LEN, :].astype(f32)
-        parts.append(rows + jnp.where(place, cls_ref[0, index : index + 1, :], 0.0))
+        parts.append(rows + jnp.where(place, cls_ref[pl.ds(begin + index, 1), :], 0.0))
     grad = jnp.concatenate(parts, 0)
     unit, inverse = normalise(second_ref[...])
     sums_ref[6:7, :] += column_sum(grad * unit)
@@ -287,11 +307,12 @@
 
 
 def cross_kernel(
-    ready, x_ref, cot_ref, key_own_ref, key_all_ref, vec_ref,
-    out_ref, x_grad_ref, low_in_ref, qkv_grad_ref, mixed_ref, attn_low_ref,
-    norm_ref, inner_ref, branch_ref, act_ref, sums_ref,
-    qkv_ref, mixed_grad, slope,
+    single, layout, ready, place_ref, x_ref, cot_ref, key_own_ref, key_all_ref, small_ref,
+    out_ref, x_grad_ref, grads_ref, sums_ref,
+    qkv_ref, qkv_grad_ref, mixed_ref, mixed_grad, slope, act_ref, inner_ref, vec_ref, grad_ref,
 ):
+    own = layout[1]
+    load_vec(small_ref, *layout, vec_ref)
     width = x_ref.shape[1]
     count = x_ref.shape[0]
     rows = pl.ds(0, count)
@@ -305,7 +326,6 @@
     mask = jnp.concatenate([same, same], 0)
     entry = x_ref[...]
     low_in = entry.astype(bf16)
-    low_in_ref[...] = low_in
     qkv = dot_nn(low_in, attn_ref[:, : 3 * width]) + qkv_bias(vec_ref)
     qkv_ref[...] = qkv.astype(bf16)
     for pair in range(PAIRS):
@@ -314,7 +334,6 @@
     unit_one, inverse_one = normalise(first_sum)
     normed = unit_one * vec_ref[3:4, :] + vec_ref[4:5, :]
     low = normed.astype(bf16)
-    norm_ref[...] = low
     up_ref = ready(1)
     down_ref = ready(2)
     total = normed + vec_ref[5:6, :]
@@ -329,12 +348,18 @@
     unit_two, inverse_two = normalise(total)
     out_ref[...] = (unit_two * vec_ref[6:7, :] + vec_ref[7:8, :]).astype(bf16)
 
-    grad = cot_ref[...].astype(f32)
+    if single:
+        for part in range(small_ref.shape[0]):
+            for at in range(width // 128):
+                tile = small_ref[part, at * 8 : (at + 1) * 8, :]
+                grad_ref[part * 8 : (part + 1) * 8, at * 128 : (at + 1) * 128] = tile.astype(f32)
+        grad = grad_ref[...]
+    else:
+        grad = cot_ref[...].astype(f32)
     sums_ref[6:7, :] += column_sum(grad * unit_two)
     sums_ref[7:8, :] += column_sum(grad)
     second_grad = norm_back(grad, unit_two, inverse_two, vec_ref[6:7, :])
     branch = second_grad.astype(bf16)
-    branch_ref[...] = branch
     sums_ref[5:6, :] += column_sum(branch.astype(f32))
     total = second_grad
     for part in range(4):
@@ -347,7 +372,6 @@
     sums_ref[4:5, :] += column_sum(total)
     first = norm_back(total, unit_one, inverse_one, vec_ref[3:4, :])
     attn_low = first.astype(bf16)
-    attn_low_ref[...] = attn_low
     sums_ref[2:3, :] += column_sum(attn_low.astype(f32))
     mixed_grad[...] = dot_nt(attn_low, attn_ref[:, 3 * width :]).astype(bf16)
     for pair in range(PAIRS):
@@ -357,6 +381,28 @@
     sums_ref[0:1, :] += column_sum(qkv_grad[:, :width].astype(f32))
     sums_ref[1:2, :] += column_sum(qkv_grad[:, 2 * width :].astype(f32))
 
+    begin = (place_ref[0] * 2 + place_ref[1]) * own
+    spot = lax.broadcasted_iota(jnp.int32, (width, own), 0) - lax.broadcasted_iota(jnp.int32, (width, own), 1)
+    chosen = (spot == begin).astype(f32).astype(bf16)
+    start = 0
+    for left, right in ((low_in, qkv_grad), (mixed_ref[...], attn_low), (low, inner_ref[...]), (branch, act_ref[...])):
+        cols = right.shape[1]
+        grad = dot_tn(dot_nn(left, chosen).astype(bf16), right)
+        if single:
+            grads_ref[:, start : start + cols] = grad.astype(bf16)
+        else:
+
+            @pl.when(pl.program_id(0) == 0)
+            def _(start=start, cols=cols):
+                grads_ref[:, start : start + cols] = jnp.zeros((own, cols), f32)
+
+            grads_ref[:, start : start + cols] += grad
+        start += cols
+    if single:
+        sums = sums_ref[0:12, :]
+        sums = jnp.concatenate([sums[:, : width // 2], sums[:, width // 2 :]], 0).astype(bf16)
+        grads_ref[:, start:] = jnp.concatenate([sums] * (own // 24), 0)
+
 
 def row_spec(width, block=BLOCK):
     return pl.BlockSpec((block, width), lambda i: (i, 0))
@@ -382,116 +428,122 @@
     return pl.CostEstimate(flops=int(flops), bytes_accessed=int(nbytes), transcendentals=int(trans))
 
 
-def attn_forward(flat, place, attn, vec):
+def attn_forward(flat, place, attn, small, layout):
     rows, width = flat.shape
     weights = Weights(attn)
     return pl.pallas_call(
-        weights.wrap(attn_fwd_kernel),
+        weights.wrap(partial(attn_fwd_kernel, layout)),
         grid=(rows // BLOCK,),
-        in_specs=weights.specs() + [row_spec(width), whole_spec(vec.shape)],
+        in_specs=weights.specs() + [row_spec(width), whole_spec(small.shape)],
         out_specs=[row_spec(3 * width), row_spec(width), row_spec(width)],
         out_shape=[shaped(rows, 3 * width), shaped(rows, width), shaped(rows, width, dtype=f32)],
-        scratch_shapes=weights.scratch(),
+        scratch_shapes=[pltpu.VMEM((16, width), f32)] + weights.scratch(),
         compiler_params=params(),
         cost_estimate=cost(2 * rows * width * (4 * width + 2 * SEG_LEN), rows * width * 14 + width * width * 8),
         name="seg_attn_fwd",
-    )(*weights.arrays(place), flat, vec)
-
-
-def ffn_forward(first_sum, place, up_proj, down_proj, vec):
+    )(*weights.arrays(place), flat, small)
+
+
+def ffn_forward(first_sum, place, up_proj, down_proj, small, layout, parts):
     rows, width = first_sum.shape
     inner = up_proj.shape[1]
-    per = BLOCK // SEG_LEN
     weights = Weights(up_proj, down_proj)
-    cls_spec = pl.BlockSpec((1, per, width), lambda i: (i, 0, 0))
+    cls_shape = (parts, rows // SEG_LEN, width)
+    cls_spec = fixed_spec(cls_shape)
     return pl.pallas_call(
-        weights.wrap(ffn_fwd_kernel),
+        weights.wrap(partial(ffn_fwd_kernel, layout)),
         grid=(rows // BLOCK,),
-        in_specs=weights.specs() + [row_spec(width), whole_spec(vec.shape)],
+        in_specs=weights.specs() + [row_spec(width), whole_spec(small.shape)],
         out_specs=[row_spec(width), row_spec(inner), row_spec(inner), row_spec(width), row_spec(width), cls_spec],
         out_shape=[
             shaped(rows, width), shaped(rows, inner), shaped(rows, inner), shaped(rows, width, dtype=f32),
-            shaped(rows, width), shaped(rows // BLOCK, per, width, dtype=f32),
+            shaped(rows, width), shaped(*cls_shape, dtype=f32),
         ],
-        scratch_shapes=weights.scratch(),
+        scratch_shapes=[pltpu.VMEM((16, width), f32)] + weights.scratch(),
         compiler_params=params(),
         cost_estimate=cost(4 * rows * width * inner, rows * (width * 12 + inner * 4) + width * inner * 4, 2 * rows * inner),
         name="seg_ffn_fwd",
-    )(*weights.arrays(place), first_sum, vec)
-
-
-def ffn_backward(cot, cls_grad, second_sum, first_sum, slope, place, up_proj, down_proj, vec):
+    )(*weights.arrays(place), first_sum, small)
+
+
+def ffn_backward(cot, cls_grad, second_sum, first_sum, slope, place, up_proj, down_proj, small, layout):
     rows, width = first_sum.shape
     inner = up_proj.shape[1]
-    per = BLOCK // SEG_LEN
     weights = Weights(up_proj, down_proj)
-    cls_spec = pl.BlockSpec((1, per, width), lambda i: (i, 0, 0))
+    cls_spec = whole_spec(cls_grad.shape)
     return pl.pallas_call(
-        weights.wrap(ffn_bwd_kernel),
+        weights.wrap(partial(ffn_bwd_kernel, layout), with_place=True),
         grid=(rows // BLOCK,),
         in_specs=weights.specs() + [
-            row_spec(width), cls_spec, row_spec(width), row_spec(width), row_spec(inner), whole_spec(vec.shape),
+            row_spec(width), cls_spec, row_spec(width), row_spec(width), row_spec(inner), whole_spec(small.shape),
         ],
-        out_specs=[row_spec(width), row_spec(inner), row_spec(width), row_spec(width), fixed_spec(vec.shape)],
+        out_specs=[row_spec(width), row_spec(inner), row_spec(width), row_spec(width), fixed_spec((16, width))],
         out_shape=[
             shaped(rows, width), shaped(rows, inner), shaped(rows, width, dtype=f32), shaped(rows, width),
-            shaped(*vec.shape, dtype=f32),
+            shaped(16, width, dtype=f32),
         ],
-        scratch_shapes=weights.scratch(),
+        scratch_shapes=[pltpu.VMEM((16, width), f32)] + weights.scratch(),
         compiler_params=params(),
         cost_estimate=cost(4 * rows * width * inner, rows * (width * 16 + inner * 4) + width * inner * 4),
         name="seg_ffn_bwd",
-    )(*weights.arrays(place), cot, cls_grad, second_sum, first_sum, slope, vec)
-
-
-def attn_backward(first_grad, attn_low, qkv, place, attn):
+    )(*weights.arrays(place), cot, cls_grad, second_sum, first_sum, slope, small)
+
+
+def attn_backward(first_grad, attn_low, qkv, place, attn, share, shares, before=()):
     rows, width = first_grad.shape
     weights = Weights(attn)
+    steps = rows // BLOCK // shares
+    spec = lambda cols: pl.BlockSpec((BLOCK, cols), lambda i: (i + share * steps, 0))
+    kept = len(before)
+    args = weights.arrays(place) + [first_grad, attn_low, qkv]
+
+    def body(ready, *refs):
+        attn_bwd_kernel(ready, *refs[:3], *refs[3 + kept :])
+
     return pl.pallas_call(
-        weights.wrap(attn_bwd_kernel),
-        grid=(rows // BLOCK,),
-        in_specs=weights.specs() + [row_spec(width), row_spec(width), row_spec(3 * width)],
-        out_specs=[row_spec(3 * width), row_spec(width), fixed_spec((8, width))],
+        weights.wrap(body),
+        grid=(steps,),
+        in_specs=weights.specs() + [spec(width), spec(width), spec(3 * width)] + [pl.BlockSpec(memory_space=pl.ANY)] * kept,
+        out_specs=[spec(3 * width), spec(width), fixed_spec((8, width))],
         out_shape=[shaped(rows, 3 * width), shaped(rows, width, dtype=f32), shaped(8, width, dtype=f32)],
+        input_output_aliases={len(args) + at: at for at in range(kept)},
         scratch_shapes=[pltpu.VMEM((BLOCK, width), bf16)] + weights.scratch(),
         compiler_params=params(),
-        cost_estimate=cost(2 * rows * width * (4 * width + 5 * SEG_LEN), rows * width * 22 + width * width * 8),
+        cost_estimate=cost(
+            2 * rows * width * (4 * width + 5 * SEG_LEN) // shares, rows * width * 22 // shares + width * width * 8
+        ),
         name="seg_attn_bwd",
-    )(*weights.arrays(place), first_grad, attn_low, qkv)
-
-
-def cross_layer(entry, cot, row_key, blocks, place, attn, up_proj, down_proj, vec):
+    )(*args, *before)
+
+
+def cross_layer(entry, cot, row_key, blocks, place, attn, up_proj, down_proj, small, layout):
     rows, width = entry.shape
     inner = up_proj.shape[1]
     block = rows // blocks
     spec = partial(row_spec, block=block)
     weights = Weights(attn, up_proj, down_proj)
+    own = layout[1]
+    wide = (own, 3 * inner + (width // 2 if by_links() else 0))
     return pl.pallas_call(
-        weights.wrap(cross_kernel),
+        weights.wrap(partial(cross_kernel, by_links(), layout), with_place=True),
         grid=(blocks,),
         in_specs=weights.specs() + [
-            spec(width), spec(width), spec(1), pl.BlockSpec((1, 1, block), lambda i: (i, 0, 0)), whole_spec(vec.shape),
+            spec(width), spec(width), spec(1), pl.BlockSpec((1, 1, block), lambda i: (i, 0, 0)), whole_spec(small.shape),
         ],
-        out_specs=[
-            spec(width), spec(width), spec(width), spec(3 * width), spec(width), spec(width),
-            spec(width), spec(inner), spec(width), spec(inner), fixed_spec(vec.shape),
-        ],
+        out_specs=[spec(width), spec(width), fixed_spec(wide), fixed_spec((16, width))],
         out_shape=[
-            shaped(rows, width), shaped(rows, width, dtype=f32), shaped(rows, width), shaped(rows, 3 * width),
-            shaped(rows, width), shaped(rows, width), shaped(rows, width), shaped(rows, inner),
-            shaped(rows, width), shaped(rows, inner), shaped(*vec.shape, dtype=f32),
+            shaped(rows, width), shaped(rows, width, dtype=f32), shaped(*wide, dtype=bf16 if by_links() else f32),
+            shaped(16, width, dtype=f32),
         ],
         scratch_shapes=[
-            pltpu.VMEM((block, 3 * width), bf16), pltpu.VMEM((block, width), bf16), pltpu.VMEM((block, inner), f32),
+            pltpu.VMEM((block, 3 * width), bf16), pltpu.VMEM((block, 3 * width), bf16), pltpu.VMEM((block, width), bf16),
+            pltpu.VMEM((block, width), bf16), pltpu.VMEM((block, inner), f32), pltpu.VMEM((block, inner), bf16),
+            pltpu.VMEM((block, inner), bf16), pltpu.VMEM((16, width), f32), pltpu.VMEM((block, width), f32),
         ] + weights.scratch(),
         compiler_params=params(),
         cost_estimate=cost(24 * rows * width * 4 * width, rows * width * 40 + width * inner * 6),
         name="cross_layer",
-    )(*weights.arrays(place), entry, cot, row_key.reshape(rows, 1), row_key.reshape(blocks, 1, block), vec)
-
-
-def spread_vec(columns):
-    return jnp.concatenate([columns.astype(f32), jnp.zeros((4, columns.shape[1]), f32)], 0)
+    )(*weights.arrays(place), entry, cot, row_key.reshape(rows, 1), row_key.reshape(blocks, 1, block), small)
 
 
 def hop_seg(value, hops):
@@ -523,37 +575,64 @@
         self.mine = jnp.concatenate(shards, 0) if self.many > 1 else shards[0]
         self.part = lax.dynamic_slice_in_dim(self.mine, lax.axis_index("batch") * self.quarter, self.quarter, 1)
 
-    def run_seg(self, direct):
-        if direct:
-            self.along = jnp.stack([hop_seg(self.part, hops) for hops in (3, 2, 1)])
+    def run_seg(self, how):
+        if how == "permute":
+            self.raw = [hop_seg(self.part, hops) for hops in (3, 2, 1)]
         else:
-            full = chips_exchange(jnp.broadcast_to(self.part, (4,) + self.part.shape))
-            self.along = lax.dynamic_slice_in_dim(jnp.concatenate([full, full[:3]], 0), lax.axis_index("seg") // 2 + 1, 3)
+            self.raw = [chips_exchange(jnp.broadcast_to(self.part, (4,) + self.part.shape))]
+
+    def run_own(self):
         self.mine_too = swap_core(self.mine)
 
-    def run_batch(self):
-        self.over = [swap_batch(self.along, flip) for flip in (1, 2, 3)]
-
-    def run_core(self):
-        self.over = jnp.stack([self.along] + self.over)
-        self.over_too = swap_core(self.over)
+    def sort_seg(self):
+        if len(self.raw) == 3:
+            self.along = jnp.stack(self.raw)
+        else:
+            full = jnp.concatenate([self.raw[0], self.raw[0][:3]], 0)
+            self.along = lax.dynamic_slice_in_dim(full, lax.axis_index("seg") // 2 + 1, 3)
+
+    def run_near(self):
+        self.near = [swap_batch(self.along, flip) for flip in (1, 2)]
+
+    def run_far(self):
+        half = self.mine.shape[0] // 2
+        self.far = [swap_batch(self.near[1][:, :half], 1), swap_batch(self.near[0][:, half:], 2)]
+
+    def run_core_near(self):
+        self.near = jnp.stack([self.along] + self.near)
+        self.near_too = swap_core(self.near)
+
+    def run_core_far(self):
+        self.far_too = [swap_core(array) for array in self.far]
 
     def pieces(self):
         own, cols, quarter = self.own, self.cols, self.quarter
-        arrays = [self.mine, self.over, self.mine_too, self.over_too]
+        half = self.mine.shape[0] // 2
+        arrays = [self.mine, self.near] + self.far + [self.mine_too, self.near_too] + self.far_too
         matrices = []
         for at in range(self.many):
-            lines = slice(at * own, (at + 1) * own)
+            first, last = at * own, (at + 1) * own
             blocks = []
             for core in (0, 1):
+
+                def chip(later, core=core):
+                    return lambda z, c: (((z + 1 + later) & 3) * 2 + (c ^ core)) * own
+
                 target = lambda z, c, q, core=core: ((z * 2 + (c ^ core)) * own, 0)
-                blocks.append((2 * core, (lines, slice(None)), (own, cols), target))
-                for flip in range(4):
-                    for later in range(3):
-                        target = lambda z, c, q, core=core, flip=flip, later=later: (
-                            (((z + 1 + later) & 3) * 2 + (c ^ core)) * own, (q ^ flip) * quarter
-                        )
-                        blocks.append((2 * core + 1, (flip, later, lines, slice(None)), (own, quarter), target))
+                blocks.append((4 * core, (slice(first, last), slice(None)), (own, cols), target))
+                for later in range(3):
+                    row = chip(later)
+                    for flip in range(3):
+                        target = lambda z, c, q, row=row, flip=flip: (row(z, c), (q ^ flip) * quarter)
+                        source = (flip, later, slice(first, last), slice(None))
+                        blocks.append((4 * core + 1, source, (own, quarter), target))
+                    for side in (0, 1):
+                        lo, hi = max(first, side * half), min(last, (side + 1) * half)
+                        if lo >= hi:
+                            continue
+                        target = lambda z, c, q, row=row, skip=lo - first: (row(z, c) + skip, (q ^ 3) * quarter)
+                        source = (later, slice(lo - side * half, hi - side * half), slice(None))
+                        blocks.append((4 * core + 2 + side, source, (hi - lo, quarter), target))
             matrices.append(Pieces((own * lax.axis_size("seg"), cols), arrays, blocks))
         return matrices
 
@@ -564,13 +643,8 @@
     return Pieces(full.shape, [full], [block])
 
 
-def swap_seg(value, flip):
-    return lax.ppermute(value, "seg", [(at, at ^ flip) for at in range(lax.axis_size("seg"))])
-
-
 def chips_exchange(value):
-    groups = [[0, 2, 4, 6], [1, 3, 5, 7]]
-    return lax.all_to_all(value, "seg", 0, 0, axis_index_groups=groups, tiled=True)
+    return lax.all_to_all(value, "seg", 0, 0, axis_index_groups=CHIP_GROUPS, tiled=True)
 
 
 def gather_seg(value):
@@ -626,33 +700,6 @@
     )(place, *[array for pair in pairs for array in pair])
 
 
-def cross_grad_kernel(*refs):
-    pairs, (out_ref,) = refs[:8], refs[8:]
-    size = out_ref.shape[1]
-    start = 0
-    for at in range(4):
-        cols = pairs[2 * at + 1].shape[1]
-        grad = dot_tn(pairs[2 * at][...], pairs[2 * at + 1][...]).astype(bf16)
-        for part in range(4):
-            out_ref[part, :, start : start + cols] = grad[part * size : (part + 1) * size]
-        start += cols
-
-
-def cross_grads(*pairs):
-    own = pairs[0][0].shape[1]
-    cols = sum(right.shape[1] for _, right in pairs)
-    vmem = pl.BlockSpec(memory_space=pltpu.VMEM)
-    return pl.pallas_call(
-        cross_grad_kernel,
-        in_specs=[vmem] * 8,
-        out_specs=vmem,
-        out_shape=shaped(4, own // 4, cols),
-        compiler_params=pltpu.CompilerParams(vmem_limit_bytes=VMEM_LIMIT),
-        cost_estimate=cost(2 * pairs[0][0].size * cols, own * cols * 2),
-        name="cross_weight_grads",
-    )(*[array for pair in pairs for array in pair])
-
-
 def wide_sum(first, *others):
     total = first.astype(f32)
     for other in others:
@@ -672,10 +719,6 @@
 
 def batch_swaps(parts):
     return [swap_batch(part, flip) for flip, part in zip((1, 2, 3), parts)]
-
-
-def chip_sum(value):
-    return jnp.sum(chips_exchange(value.astype(bf16)).astype(f32), 0)
 
 
 def place_kernel(plan, place_ref, *refs):
@@ -708,17 +751,6 @@
     return lax.psum_scatter(matrix.astype(bf16), "seg", scatter_dimension=0, tiled=True)
 
 
-def sum_everywhere(seg_sums, cross_sums):
-    if not by_links():
-        return lax.psum(seg_sums, ("batch", "seg")), lax.psum(cross_sums, "batch")
-    for flip in (1, 2, 4):
-        seg_sums = seg_sums + swap_seg(seg_sums, flip)
-    both = jnp.concatenate([seg_sums, cross_sums], 0)
-    for flip in (1, 2):
-        both = both + swap_batch(both, flip)
-    return both[: seg_sums.shape[0]], both[seg_sums.shape[0] :]
-
-
 def local(
     hidden, seg_doc, seg_attn, seg_up, seg_down, seg_vec,
     cross_attn, cross_up, cross_down, cross_vec, tok_cot, cls_cot,
@@ -732,41 +764,61 @@
     spot = jnp.stack([place // 2, place % 2, lax.axis_index("batch")]).astype(jnp.int32)
 
     flat = hidden.reshape(count * length, width)
-    small = jnp.concatenate([cls_cot.reshape(count * width), seg_vec.T.reshape(-1), cross_vec.T.reshape(-1)])
-
-    def spread_small(small):
-        cot_all = small[:, : count * width].reshape(total, width)
-        vecs = small[:, count * width :].reshape(parts, 24, own).transpose(1, 0, 2).reshape(24, width)
-        return cot_all, spread_vec(vecs[:12]), spread_vec(vecs[12:])
+    tiles = width // 128
+    vecs = jnp.pad(jnp.concatenate([seg_vec.T, cross_vec.T], 0), ((0, 0), (0, 128 - own)))
+    small = cls_cot.reshape(count, tiles, 128).transpose(1, 0, 2).reshape(count * tiles, 128)
+    small = jnp.concatenate([small, vecs], 0)
+    seg_layout, cross_layout = (count * tiles, own), (count * tiles + 12, own)
 
     if by_links():
         one, two, three, four = Gather(seg_attn), Gather(seg_up, seg_down), Gather(cross_attn, cross_up), Gather(cross_down)
-        one.run_seg(True)
+        one.run_seg("permute")
         small = gather_seg(small)
-        one.along, small, two.part, two.mine = fence(one.along, small, two.part, two.mine)
-        cot_all, seg_vec_full, cross_vec_full = spread_small(small)
-        one.run_batch()
-        two.run_seg(False)
-        one.over, two.along, three.part, three.mine = fence(one.over, two.along, three.part, three.mine)
-        one.run_core()
-        two.run_batch()
-        three.run_seg(False)
+        one.run_own()
+        one.raw, small, two.part, two.mine = fence(one.raw, small, two.part, two.mine)
+        one.sort_seg()
+        one.run_near()
+        two.run_seg("permute")
+        (one.near,) = fence(one.near)
+        one.run_far()
+        one.far, one.near, two.raw, three.part, three.mine = fence(one.far, one.near, two.raw, three.part, three.mine)
+        two.sort_seg()
+        one.run_core_near()
+        one.run_core_far()
+        two.run_near()
+        three.run_seg("exchange")
         (attn_full,) = one.pieces()
-        outs = attn_forward(flat, spot, attn_full, seg_vec_full)
-        (qkv, mixed, first_sum), two.over, three.along, four.part, four.mine = fence(
-            outs, two.over, three.along, four.part, four.mine
+        outs = attn_forward(flat, spot, attn_full, small, seg_layout)
+        (qkv, mixed, first_sum), two.near, two.mine, four.part, three.raw = fence(
+            outs, two.near, two.mine, four.part, three.raw
         )
-        two.run_core()
-        three.run_batch()
-        four.run_seg(False)
+        two.run_far()
+        two.run_core_near()
+        two.run_own()
+        two.far, three.raw, three.mine, four.mine = fence(two.far, three.raw, three.mine, four.mine)
+        three.sort_seg()
+        two.run_core_far()
+        three.run_near()
+        four.run_seg("exchange")
         up_full, down_full = two.pieces()
-        outs = ffn_forward(first_sum, spot, up_full, down_full, seg_vec_full)
-        (normed, act, slope, second_sum, tok, cls), three.over, four.along = fence(outs, three.over, four.along)
-        three.run_core()
-        four.run_batch()
-        entry = gather_seg(cls.reshape(count, width)).reshape(total, width)
-        entry, four.over = fence(entry, four.over)
-        four.run_core()
+        outs = ffn_forward(first_sum, spot, up_full, down_full, small, seg_layout, parts)
+        (normed, act, slope, second_sum, tok, cls), three.near, four.raw, three.mine, four.mine = fence(
+            outs, three.near, four.raw, three.mine, four.mine
+        )
+        four.sort_seg()
+        three.run_far()
+        entry = lax.all_to_all(cls, "seg", 0, 0, tiled=True).reshape(total, width)
+        cot_all = entry
+        three.run_core_near()
+        three.run_own()
+        four.run_near()
+        entry, three.far, four.near = fence(entry, three.far, four.near)
+        three.run_core_far()
+        four.run_far()
+        four.run_core_near()
+        four.run_own()
+        (four.far,) = fence(four.far)
+        four.run_core_far()
         cross_attn_full, cross_up_full = three.pieces()
         (cross_down_full,) = four.pieces()
     else:
@@ -774,10 +826,11 @@
         cross_attn_full, cross_up_full, cross_down_full = [
             gather_plain(shard) for shard in (cross_attn, cross_up, cross_down)
         ]
-        cot_all, seg_vec_full, cross_vec_full = spread_small(gather_seg(small))
-        qkv, mixed, first_sum = attn_forward(flat, spot, attn_full, seg_vec_full)
-        normed, act, slope, second_sum, tok, cls = ffn_forward(first_sum, spot, up_full, down_full, seg_vec_full)
-        entry = gather_seg(cls.reshape(count, width)).reshape(total, width)
+        small = gather_seg(small)
+        cot_all = small[:, : count * tiles].reshape(parts, tiles, count, 128).transpose(0, 2, 1, 3).reshape(total, width)
+        qkv, mixed, first_sum = attn_forward(flat, spot, attn_full, small, seg_layout)
+        normed, act, slope, second_sum, tok, cls = ffn_forward(first_sum, spot, up_full, down_full, small, seg_layout, parts)
+        entry = gather_seg(cls[0]).reshape(total, width)
 
     docs = seg_doc[:, 0].reshape(micro, segments, parts) + (1 << 16) * jnp.arange(micro, dtype=jnp.int32)[:, None, None]
     docs = docs.transpose(2, 0, 1)
@@ -789,62 +842,88 @@
     else:
         order = back = lambda rows: rows
         row_key = docs.reshape(total)
-    (
-        cls_out, cls_grad, x_low, x_qkv_grad, x_mixed, x_attn_low, x_norm, x_inner, x_branch, x_act, x_sums,
-    ) = cross_layer(
+    cls_out, cls_grad, x_grads, x_sums = cross_layer(
         order(entry), order(cot_all), row_key, blocks, spot,
-        cross_attn_full, cross_up_full, cross_down_full, cross_vec_full,
+        cross_attn_full, cross_up_full, cross_down_full, small, cross_layout,
     )
     own_cols = lambda rows: lax.dynamic_slice_in_dim(rows, place * own, own, 1)
     own_rows = lambda rows: lax.dynamic_slice_in_dim(back(rows), place * count, count, 0)
     cls_out = own_rows(cls_out)
-    cls_grad = own_rows(cls_grad)
-
-    branch, inner, first_grad, attn_low, ffn_sums = ffn_backward(
+    if not by_links():
+        cls_grad = own_rows(cls_grad)
+    outs = ffn_backward(
         tok_cot.reshape(count * length, width),
-        cls_grad.reshape(cls.shape), second_sum, first_sum, slope, spot, up_full, down_full, seg_vec_full,
+        cls_grad, second_sum, first_sum, slope, spot, up_full, down_full, small, seg_layout,
     )
-    cross_pairs = (
-        (own_cols(x_low), x_qkv_grad), (own_cols(x_mixed), x_attn_low),
-        (own_cols(x_norm), x_inner), (own_cols(x_branch), x_act),
-    )
 
     if by_links():
-        keep, send = weight_grads(spot, (branch, act), (normed, inner), (mixed, attn_low))
+        folded = lambda rows: jnp.concatenate([rows[:, : width // 2], rows[:, width // 2 :]], 0)
+        unfolded = lambda rows: jnp.concatenate([rows[:12], rows[12:]], 1)
+        x_came = lax.all_to_all(x_grads.reshape(4, own // 4, 3 * cols + width // 2), "batch", 0, 0, tiled=True)
+        (branch, inner, first_grad, attn_low, ffn_sums), x_came = fence(outs, x_came)
+        x_sum = jnp.sum(x_came.astype(f32), 0)
+        cross_sums = unfolded(x_sum[:, 3 * cols :])
+        keep_down, send = weight_grads(spot, (branch, act))
+        send, inner = fence(send, inner)
+        got_down = swap_core(send)
+        set_cross = batch_spread(x_sum[:, : 3 * cols])
+        keep_up, send_up = weight_grads(spot, (normed, inner), (mixed, attn_low))
+        got_down, keep_up, send_up = fence(got_down, keep_up, send_up)
+        stay_down, leave = core_sums(keep_down, got_down)
+        leave, send_up, attn_low = fence(leave, send_up, attn_low)
+        came_down = batch_swaps(leave)
+        got_up = swap_core(send_up)
+        outs = attn_backward(first_grad, attn_low, qkv, spot, attn_full, 0, 2)
+        outs, came_down, got_up = fence(outs, came_down, got_up)
+        total_down = wide_sum(stay_down, *came_down).astype(bf16)
+        stay_up, leave = core_sums(keep_up, got_up)
+        (qkv_grad, hidden_grad, sums_one), total_down, leave = fence(outs, total_down, leave)
+        raw_down = chips_exchange(total_down)
+        came_up = batch_swaps(leave)
+        outs = attn_backward(first_grad, attn_low, qkv, spot, attn_full, 1, 2, (qkv_grad, hidden_grad))
+        (qkv_grad, hidden_grad, sums_two), raw_down = fence(outs, raw_down)
+        sums = folded(jnp.concatenate([(sums_one + sums_two)[:2], ffn_sums[2:12]], 0))
+        sums_too = swap_core(sums)
+        keep, send = weight_grads(spot, (flat, qkv_grad))
+        keep, send, sums, sums_too, came_up = fence(keep, send, sums, sums_too, came_up)
         got = swap_core(send)
-        x_grads = cross_grads(*cross_pairs)
-        got, x_grads = fence(got, x_grads)
+        total_up = wide_sum(stay_up, *came_up).astype(bf16)
+        sums = jnp.broadcast_to(sums + sums_too, (4, 24, width // 2))
         stay, leave = core_sums(keep, got)
-        stay, leave, attn_low = fence(stay, leave, attn_low)
+        stay = jnp.concatenate([stay, sums], 2)
+        leave = [jnp.concatenate([part, sums.astype(bf16)], 2) for part in leave]
+        total_up, leave = fence(total_up, leave)
         came = batch_swaps(leave)
-        x_came = lax.all_to_all(x_grads, "batch", 0, 0, tiled=True)
-        outs = attn_backward(first_grad, attn_low, qkv, spot, attn_full)
-        (qkv_grad, hidden_grad, attn_sums), came, x_came = fence(outs, came, x_came)
-        total_one = wide_sum(stay, *came)
-        keep, send = weight_grads(spot, (flat, qkv_grad))
-        set_one = batch_spread(chip_sum(total_one))
-        set_cross = batch_spread(jnp.sum(x_came.astype(f32), 0))
-        stay, leave = core_sums(keep, swap_core(send))
-        set_two = batch_spread(chip_sum(wide_sum(stay, *batch_swaps(leave))))
-        plan = (
-            ((0, 2, 0, cols), (cols, 1, 0, cols), (2 * cols, 0, 3 * width, width)),
-            ((0, 0, 0, 3 * width),),
-            ((0, 3, 0, cols), (cols, 4, 0, cols), (2 * cols, 5, 0, cols)),
-        )
-        grads = place_outputs(spot, plan, (set_one, set_two, set_cross), 6, (own, cols))
+        raw_up = chips_exchange(total_up)
+        set_down = batch_spread(jnp.sum(raw_down.astype(f32), 0))
+        came, raw_up = fence(came, raw_up)
+        raw = chips_exchange(wide_sum(stay, *came).astype(bf16))
+        set_up = batch_spread(jnp.sum(raw_up.astype(f32), 0))
+        last = jnp.sum(raw.astype(f32), 0)
+        set_qkv = batch_spread(last[:, : 3 * width])
+        seg_sums = unfolded(last[:, 3 * width :])
+        shape = (own, cols)
+        x_plan = (((0, 0, 0, cols), (cols, 1, 0, cols), (2 * cols, 2, 0, cols)),)
+        x_placed = place_outputs(spot, x_plan, (set_cross,), 3, shape)
+        (down_placed,) = place_outputs(spot, (((0, 0, 0, cols),),), (set_down,), 1, shape)
+        (up_placed,) = place_outputs(spot, (((0, 0, 0, cols),),), (set_up,), 1, shape)
+        attn_plan = (((0, 0, 0, 3 * width),), ((cols, 0, 3 * width, width),))
+        (attn_placed,) = place_outputs(spot, attn_plan, (set_qkv, set_up), 1, shape)
+        grads = [attn_placed, up_placed, down_placed] + list(x_placed)
     else:
-        qkv_grad, hidden_grad, attn_sums = attn_backward(first_grad, attn_low, qkv, spot, attn_full)
-        wide = [dot_tn(left, right) for left, right in cross_pairs]
+        branch, inner, first_grad, attn_low, ffn_sums = outs
+        qkv_grad, hidden_grad, attn_sums = attn_backward(first_grad, attn_low, qkv, spot, attn_full, 0, 1)
+        x_grads = x_grads.astype(bf16)
         grads = [
             scatter_sum(jnp.concatenate([dot_tn(flat, qkv_grad), dot_tn(mixed, attn_low)], 1)),
             scatter_sum(dot_tn(normed, inner)), scatter_sum(dot_tn(branch, act)),
-            jnp.concatenate(wide[:2], 1).astype(bf16), wide[2].astype(bf16), wide[3].astype(bf16),
+            x_grads[:, :cols], x_grads[:, cols : 2 * cols], x_grads[:, 2 * cols :],
         ]
         grads = [grad.astype(f32) for grad in lax.psum(tuple(grads), "batch")]
-    sums = jnp.concatenate([attn_sums[:2], ffn_sums[2:12]], 0)
-    seg_sums, x_sums = sum_everywhere(sums, x_sums[:12])
+        seg_sums = lax.psum(jnp.concatenate([attn_sums[:2], ffn_sums[2:12]], 0), ("batch", "seg"))
+        cross_sums = lax.psum(x_sums[:12], "batch")
     seg_vec_grad = own_cols(seg_sums).T
-    cross_vec_grad = own_cols(x_sums).T
+    cross_vec_grad = own_cols(cross_sums).T
     return (
         tok.reshape(hidden.shape), cls_out.reshape(cls_cot.shape), hidden_grad.reshape(hidden.shape),
         grads[0], grads[1], grads[2], seg_vec_grad, grads[3], grads[4], grads[5], cross_vec_grad,

time: 473 us -> 425 us (0.90)
  waiting for transfers between devices: 145 us -> 95 us
  starting transfers between devices: 79.8 us -> 94 us
  blocking collectives: 13.2 us -> 0 us
  Pallas kernels: 152 us -> 162 us
    all_to_all x6 -> x7, waiting for transfers between devices: 63.5 us -> 11.2 us  [the longest x1 6.29 us: local(): entry = lax.all_to_all(cls, 'seg', 0, 0, tiled=True).reshape(total, width)]
    ppermute x3 -> x6, waiting for transfers between devices: 0.01 us -> 18.3 us  [hop_seg(): lax.ppermute(value, 'seg', [(at, (at + 2 * hops) % size) for at in range(...]
    all_to_all x1 -> x0, blocking collectives: 13.2 us -> none  [gather_seg(): return lax.all_to_all(copies, 'seg', 0, 0, tiled=True)]
    ppermute x3 -> x0, waiting for transfers between devices: 10.7 us -> none  [swap_seg(): lax.ppermute(value, 'seg', [(at, at ^ flip) for at in range(lax.axis_size...]
    ppermute x29 -> x37, starting transfers between devices: 35 us -> 43.3 us  [swap_batch(): lax.ppermute(value, 'batch', [(at, at ^ flip) for at in range(lax.axis_si...]
    unnamed x52 -> x97, local copies, waits for them, and re-layouts: 5.24 us -> 12.5 us
    all_to_all x6 -> x7, starting transfers between devices: 25.8 us -> 32.6 us  [the longest x5 23.2 us: chips_exchange(): lax.all_to_all(value, 'seg', 0, 0, axis_index_groups=CHIP_GROUPS, tiled=T...]
    ppermute x3 -> x0, starting transfers between devices: 6.69 us -> none  [swap_seg(): lax.ppermute(value, 'seg', [(at, at ^ flip) for at in range(lax.axis_size...]
  transfers between devices with their start and end apart: 52 -> 71, of which waited for: 19 -> 30; matrix products, arithmetic and copies ran while one was open for 12% -> 9% of each run, Pallas kernels for 17% -> 31%
where the time goes in v3:
time: 425 us; the launch traced here: 418 us
  Pallas kernels  162 us (38%)
  waiting for transfers between devices  95 us (22%)
  starting transfers between devices  94 us (22%)
  other arithmetic  34.7 us (8%)
  local copies, waits for them, and re-layouts  31 us (7%)
    ppermute x37, waiting for transfers between devices, swap_batch(): lax.ppermute(value, 'batch', [(at, at ^ flip) for at in range(lax.axis_si...  63.7 us
    ppermute x37, starting transfers between devices, swap_batch(): lax.ppermute(value, 'batch', [(at, at ^ flip) for at in range(lax.axis_si...  43.3 us
    pallas_call x2, Pallas kernels, attn_backward(): pl.pallas_call(weights.wrap(body), grid=(steps,), in_specs=weights.specs(...  41 us
    pallas_call x3, Pallas kernels, weight_grads(): pl.pallas_call(partial(weight_grad_kernel, steps), grid=(begin,), in_spec...  29.7 us
    all_to_all x5, starting transfers between devices, chips_exchange(): lax.all_to_all(value, 'seg', 0, 0, axis_index_groups=CHIP_GROUPS, tiled=T...  23.2 us
    pallas_call x1, Pallas kernels, ffn_forward(): pl.pallas_call(weights.wrap(partial(ffn_fwd_kernel, layout)), grid=(rows...  22.1 us
    pallas_call x1, Pallas kernels, ffn_backward(): pl.pallas_call(weights.wrap(partial(ffn_bwd_kernel, layout), with_place=T...  22.1 us
    pallas_call x1, Pallas kernels, cross_layer(): pl.pallas_call(weights.wrap(partial(cross_kernel, by_links(), layout), wi...  20.8 us
  transfers between devices with their start and end apart: 71, of which 30 were waited for; matrix products, arithmetic and copies ran while one was open for 9% of the time, Pallas kernels for 31%

profile of v3, /device:TPU:0, one launch (start us, length us, event | category | flops | bytes accessed | tf_op | source)
XLA Modules:
  0.0 418.2 jit_solution(5984170857004660185)
XLA Ops:
  1.6 5.1 %collective-permute-start = (bf16[96,768]{1,0:T(8,128)(2,1)S(1)}, bf16[96,768]{1,0:T(8,128)(2,1)S(1)}, u32[]{:S(2)}, u32[]{:S(2)}) collective-permute-start(bf16[96,768]{1,0:T(8,128)(2,1)S(1)} %constant_dynamic-slice_fusion.4), channel_id=1, source_target_pairs={{0,6},{1,7},{2,0},{3,1},{4,2},{5,3},{6,4},{7,5},{8,14},{9,15},{10,... | collective-permute-start | bytes 442376 | tf_op jit(solution)/shard_map/ppermute | solution.py:551
  9.9 4.1 all-to-all-start
  39.6 14.5 %collective-permute-done.8 = bf16[192,768]{1,0:T(8,128)(2,1)S(1)} collective-permute-done((bf16[192,768]{1,0:T(8,128)(2,1)S(1)}, bf16[192,768]{1,0:T(8,128)(2,1)S(1)}, u32[]{:S(2)}, u32[]{:S(2)}) %collective-permute-start.8) | collective-permute-done | bytes 294944 | tf_op jit(solution)/shard_map/ppermute | solution.py:551
  56.5 4.2 %all-to-all-start.1 = ((bf16[4,192,768]{2,1,0:T(8,128)(2,1)}), bf16[4,192,768]{2,1,0:T(8,128)(2,1)S(1)}, u32[]{:S(2)}, u32[]{:S(2)}) async-start(bf16[4,192,768]{2,1,0:T(8,128)(2,1)} %broadcast_in_dim.16), calls=%async_computation.1 | async-start | bytes 2359296 | tf_op jit(solution)/shard_map/all_to_all | solution.py:647
  66.9 15.8 %seg_attn_fwd.1 = (bf16[1024,2304]{1,0:T(8,128)(2,1)}, bf16[1024,768]{1,0:T(8,128)(2,1)}, f32[1024,768]{1,0:T(8,128)}) custom-call(s32[3]{0:T(128)} %pad_add_fusion.place_ref, bf16[96,3072]{1,0:T(8,128)(2,1)} %refs_0_.5, bf16[3,3,96,768]{3,2,1,0:T(8,128)(2,1)} %copy-done.1, bf16[3,48,768]{2,1,0:T(8,128)(2,1)} %copy-done.14, bf16[3,48,768]{2,1,0:T(8,128)(2,1)} %copy-done.15, ...), custom_call_target="tpu_custom_call" | custom-call | flops 5234491392 | bytes 15728640 | tf_op jit(solution)/shard_map/seg_attn_fwd/pallas_call | solution.py:434
  85.6 4.1 all-to-all-done.1
  96.6 11.0 %collective-permute-done.16.refs_2_.refs_10_ = bf16[3,96,768]{2,1,0:T(8,128)(2,1)S(1)} collective-permute-done((bf16[3,96,768]{2,1,0:T(8,128)(2,1)S(1)}, bf16[3,96,768]{2,1,0:T(8,128)(2,1)S(1)}, u32[]{:S(2)}, u32[]{:S(2)}) %collective-permute-start.16) | collective-permute-done | bytes 442400 | tf_op jit(solution)/shard_map/ppermute | solution.py:559
  116.5 22.1 %seg_ffn_fwd.1 = (bf16[1024,768]{1,0:T(8,128)(2,1)}, bf16[1024,3072]{1,0:T(8,128)(2,1)}, bf16[1024,3072]{1,0:T(8,128)(2,1)}, f32[1024,768]{1,0:T(8,128)}, bf16[1...) custom-call(s32[3]{0:T(128)} %pad_add_fusion.place_ref, bf16[192,3072]{1,0:T(8,128)(2,1)} %constant_dynamic-update-slice_fusion.refs_0_.refs_8_, ...), custom_call_target="tpu_custom_call" | custom-call | flops 9663676416 | bytes 31457280 | tf_op jit(solution)/shard_map/seg_ffn_fwd/pallas_call | solution.py:453
  148.5 5.6 %all-to-all-start.3 = ((f32[8,8,768]{2,1,0:T(8,128)}), f32[8,8,768]{2,1,0:T(8,128)S(1)}, u32[]{:S(2)}, u32[]{:S(2)}) async-start(f32[8,8,768]{2,1,0:T(8,128)} %get-tuple-element.181), calls=%async_computation.3 | async-start | bytes 393216 | tf_op jit(solution)/shard_map/all_to_all | solution.py:810
  156.2 6.3 %all-to-all-done.3 = f32[8,8,768]{2,1,0:T(8,128)S(1)} async-done(((f32[8,8,768]{2,1,0:T(8,128)}), f32[8,8,768]{2,1,0:T(8,128)S(1)}, u32[]{:S(2)}, u32[]{:S(2)}) %all-to-all-start.3) | async-done | bytes 196640 | tf_op jit(solution)/shard_map/all_to_all | solution.py:810
  184.4 20.8 %cross_layer.1 = (bf16[64,768]{1,0:T(8,128)(2,1)}, f32[64,768]{1,0:T(8,128)}, bf16[96,9600]{1,0:T(8,128)(2,1)}, f32[16,768]{1,0:T(8,128)}) custom-call(s32[3]{0:T(128)} %pad_add_fusion.place_ref, bf16[192,3072]{1,0:T(8,128)(2,1)} %constant_dynamic-update-slice_fusion.2.refs_0_.refs_8_, bf16[3,3,192,768]{3,2,1,0:T(8,128)(2,1)} %copy-done, ...), custom_call_target="tpu_custom_call" | custom-call | flops 3623878656 | bytes 16121856 | tf_op jit(solution)/shard_map/cross_layer/pallas_call | solution.py:527
  208.9 22.1 %seg_ffn_bwd.1 = (bf16[1024,768]{1,0:T(8,128)(2,1)}, bf16[1024,3072]{1,0:T(8,128)(2,1)}, f32[1024,768]{1,0:T(8,128)}, bf16[1024,768]{1,0:T(8,128)(2,1)}, f32[16,768]{1,0:T(8,128)}) custom-call(s32[3]{0:T(128)} %pad_add_fusion.place_ref, bf16[192,3072]{1,0:T(8,128)(2,1)} %constant_dynamic-update-slice_fusion.refs_0_.refs_8_, ...), custom_call_target="tpu_custom_call" | custom-call | flops 9663676416 | bytes 34603008 | tf_op jit(solution)/shard_map/seg_ffn_bwd/pallas_call | solution.py:474
  231.9 9.5 %weight_grads.3 = (bf16[4,4,24,3072]{3,2,1,0:T(8,128)(2,1)}, bf16[4,4,24,3072]{3,2,1,0:T(8,128)(2,1)}) custom-call(s32[3]{0:T(128)} %pad_add_fusion.place_ref, bf16[1024,768]{1,0:T(8,128)(2,1)} %get-tuple-element.202.refs_0_, bf16[1024,3072]{1,0:T(8,128)(2,1)} %get-tuple-element.203.refs_1_), custom_call_target="tpu_custom_call" | custom-call | flops 4831838208 | bytes 11010048 | tf_op jit(solution)/shard_map/weight_grads/pallas_call | solution.py:690
  241.4 12.2 %weight_grads.4 = (bf16[4,4,24,3840]{3,2,1,0:T(8,128)(2,1)}, bf16[4,4,24,3840]{3,2,1,0:T(8,128)(2,1)}) custom-call(s32[3]{0:T(128)} %pad_add_fusion.place_ref, bf16[1024,768]{1,0:T(8,128)(2,1)} %get-tuple-element.208.refs_0_, bf16[1024,3072]{1,0:T(8,128)(2,1)} %get-tuple-element.209.refs_1_, bf16[1024,768]{1,0:T(8,128)(2,1)} %get-tuple-element.210.refs_2_, ...), custom_call_target="tpu_custom_call" | custom-call | flops 6039797760 | bytes 13762560 | tf_op jit(solution)/shard_map/weight_grads/pallas_call | solution.py:690
  261.1 20.6 %seg_attn_bwd.2 = (bf16[1024,2304]{1,0:T(8,128)(2,1)}, f32[1024,768]{1,0:T(8,128)}, f32[8,768]{1,0:T(8,128)}) custom-call(s32[3]{0:T(128)} %pad_add_fusion.place_ref, bf16[96,3072]{1,0:T(8,128)(2,1)} %refs_0_.5, bf16[3,3,96,768]{3,2,1,0:T(8,128)(2,1)} %copy-done.1, bf16[3,48,768]{2,1,0:T(8,128)(2,1)} %copy-done.14, bf16[3,48,768]{2,1,0:T(8,128)(2,1)} %copy-done.15, ...), custom_call_target="tpu_custom_call" | custom-call | flops 2919235584 | bytes 13369344 | tf_op jit(solution)/shard_map/seg_attn_bwd/pallas_call | solution.py:503
  281.7 5.2 %collective-permute-done.40 = bf16[4,24,3072]{2,1,0:T(8,128)(2,1)S(1)} collective-permute-done((bf16[4,24,3072]{2,1,0:T(8,128)(2,1)}, bf16[4,24,3072]{2,1,0:T(8,128)(2,1)S(1)}, u32[]{:S(2)}, u32[]{:S(2)}) %collective-permute-start.40) | collective-permute-done | bytes 589856 | tf_op jit(solution)/shard_map/ppermute | solution.py:559
  287.7 3.9 fusion.12
  294.3 5.3 %all-to-all-start.5 = ((bf16[4,24,3072]{2,1,0:T(8,128)(2,1)}), bf16[4,24,3072]{2,1,0:T(8,128)(2,1)S(1)}, u32[]{:S(2)}, u32[]{:S(2)}) async-start(bf16[4,24,3072]{2,1,0:T(8,128)(2,1)} %fusion.5), calls=%async_computation.5 | async-start | bytes 1179648 | tf_op jit(solution)/shard_map/all_to_all | solution.py:647
  303.2 20.4 %seg_attn_bwd.3 = (bf16[1024,2304]{1,0:T(8,128)(2,1)}, f32[1024,768]{1,0:T(8,128)}, f32[8,768]{1,0:T(8,128)}) custom-call(s32[3]{0:T(128)} %pad_add_fusion.place_ref, bf16[96,3072]{1,0:T(8,128)(2,1)} %refs_0_.5, bf16[3,3,96,768]{3,2,1,0:T(8,128)(2,1)} %copy-done.1, bf16[3,48,768]{2,1,0:T(8,128)(2,1)} %copy-done.14, ...), custom_call_target="tpu_custom_call", output_to_operand_aliasing={{0}: (12, {}), {1}: (13, {})} | custom-call | flops 2919235584 | bytes 13369344 | tf_op jit(solution)/shard_map/seg_attn_bwd/pallas_call | solution.py:503
  324.6 8.0 %weight_grads.5 = (bf16[4,4,24,2304]{3,2,1,0:T(8,128)(2,1)}, bf16[4,4,24,2304]{3,2,1,0:T(8,128)(2,1)}) custom-call(s32[3]{0:T(128)} %pad_add_fusion.place_ref, bf16[1024,768]{1,0:T(8,128)(2,1)} %bitcast.103, bf16[1024,2304]{1,0:T(8,128)(2,1)} %get-tuple-element.240.refs_1_), custom_call_target="tpu_custom_call" | custom-call | flops 3623878656 | bytes 8257536 | tf_op jit(solution)/shard_map/weight_grads/pallas_call | solution.py:690
  338.7 4.8 %all-to-all-start.6 = ((bf16[4,24,3840]{2,1,0:T(8,128)(2,1)}), bf16[4,24,3840]{2,1,0:T(8,128)(2,1)S(1)}, u32[]{:S(2)}, u32[]{:S(2)}) async-start(bf16[4,24,3840]{2,1,0:T(8,128)(2,1)} %fusion.2), calls=%async_computation.6 | async-start | bytes 1474560 | tf_op jit(solution)/shard_map/all_to_all | solution.py:647
  349.3 9.1 %collective-permute-done.48 = bf16[4,24,2688]{2,1,0:T(8,128)(2,1)S(1)} collective-permute-done((bf16[4,24,2688]{2,1,0:T(8,128)(2,1)}, bf16[4,24,2688]{2,1,0:T(8,128)(2,1)S(1)}, u32[]{:S(2)}, u32[]{:S(2)}) %collective-permute-start.48) | collective-permute-done | bytes 516128 | tf_op jit(solution)/shard_map/ppermute | solution.py:559
  359.6 10.6 %collective-permute-done.49 = bf16[4,24,2688]{2,1,0:T(8,128)(2,1)S(1)} collective-permute-done((bf16[4,24,2688]{2,1,0:T(8,128)(2,1)}, bf16[4,24,2688]{2,1,0:T(8,128)(2,1)S(1)}, u32[]{:S(2)}, u32[]{:S(2)}) %collective-permute-start.49) | collective-permute-done | bytes 516128 | tf_op jit(solution)/shard_map/ppermute | solution.py:559
  373.5 5.1 %all-to-all-start.7 = ((bf16[4,24,2688]{2,1,0:T(8,128)(2,1)}), bf16[4,24,2688]{2,1,0:T(8,128)(2,1)S(1)}, u32[]{:S(2)}, u32[]{:S(2)}) async-start(bf16[4,24,2688]{2,1,0:T(8,128)(2,1)} %fusion.8), calls=%async_computation.7 | async-start | bytes 1032192 | tf_op jit(solution)/shard_map/all_to_all | solution.py:647
  (293 shorter events, 166.0 us)
Async XLA Ops:
  30.1 24.0 %collective-permute-start.8 = (bf16[192,768]{1,0:T(8,128)(2,1)S(1)}, bf16[192,768]{1,0:T(8,128)(2,1)S(1)}, u32[]{:S(2)}, u32[]{:S(2)}) collective-permute-start(bf16[192,768]{1,0:T(8,128)(2,1)S(1)} %constant_dynamic-slice_fusion.3), channel_id=1, source_target_pairs={{0,4},{1,5},{2,6},{3,7},{4,0},{5,1},{6,2},{7,3},{8,12},{9,13},{10,... | collective-permute-start | bytes 884744 | tf_op jit(solution)/shard_map/ppermute | solution.py:551
  30.1 24.0 %collective-permute-start.9 = (bf16[192,768]{1,0:T(8,128)(2,1)S(1)}, bf16[192,768]{1,0:T(8,128)(2,1)S(1)}, u32[]{:S(2)}, u32[]{:S(2)}) collective-permute-start(bf16[192,768]{1,0:T(8,128)(2,1)S(1)} %constant_dynamic-slice_fusion.3), channel_id=1, source_target_pairs={{0,2},{1,3},{2,4},{3,5},{4,6},{5,7},{6,0},{7,1},{8,10},{9,11},{10,... | collective-permute-start | bytes 884744 | tf_op jit(solution)/shard_map/ppermute | solution.py:551
  56.5 33.2 %all-to-all-start.1 = ((bf16[4,192,768]{2,1,0:T(8,128)(2,1)}), bf16[4,192,768]{2,1,0:T(8,128)(2,1)S(1)}, u32[]{:S(2)}, u32[]{:S(2)}) async-start(bf16[4,192,768]{2,1,0:T(8,128)(2,1)} %broadcast_in_dim.16), calls=%async_computation.1 | async-start | bytes 2359296 | tf_op jit(solution)/shard_map/all_to_all | solution.py:647
  92.9 23.6 %collective-permute-start.19 = (bf16[3,3,192,768]{3,2,1,0:T(8,128)(2,1)}, bf16[3,3,192,768]{3,2,1,0:T(8,128)(2,1)}, u32[]{:S(2)}, u32[]{:S(2)}) collective-permute-start(bf16[3,3,192,768]{3,2,1,0:T(8,128)(2,1)} %pad_maximum_fusion.refs_1_.refs_9_), channel_id=1, source_target_pairs={{0,1},{1,0},{2,3},{3,2},{4,5},{5,4},{6,7},{7,6},{8,9},{9,8},{10,11... | collective-permute-start | bytes 7962632 | tf_op jit(solution)/shard_map/ppermute | solution.py:555
  92.9 23.6 %collective-permute-start.18 = (bf16[192,3072]{1,0:T(8,128)(2,1)}, bf16[192,3072]{1,0:T(8,128)(2,1)}, u32[]{:S(2)}, u32[]{:S(2)}) collective-permute-start(bf16[192,3072]{1,0:T(8,128)(2,1)} %constant_dynamic-update-slice_fusion.refs_0_.refs_8_), channel_id=1, source_target_pairs={{0,1},{1,0},{2,3},{3,2},{4,5},{5,4},{6,7},{7,6},{8,9},{9,8},{10,11... | collective-permute-start | bytes 3538952 | tf_op jit(solution)/shard_map/ppermute | solution.py:555
  109.4 29.2 %all-to-all-start.2 = ((bf16[4,96,768]{2,1,0:T(8,128)(2,1)}), bf16[4,96,768]{2,1,0:T(8,128)(2,1)S(1)}, u32[]{:S(2)}, u32[]{:S(2)}) async-start(bf16[4,96,768]{2,1,0:T(8,128)(2,1)} %broadcast_in_dim.17), calls=%async_computation.2 | async-start | bytes 1179648 | tf_op jit(solution)/shard_map/all_to_all | solution.py:647
  114.5 24.1 %collective-permute-start.22 = (bf16[3,192,768]{2,1,0:T(8,128)(2,1)}, bf16[3,192,768]{2,1,0:T(8,128)(2,1)S(1)}, u32[]{:S(2)}, u32[]{:S(2)}) collective-permute-start(bf16[3,192,768]{2,1,0:T(8,128)(2,1)} %fusion.9), channel_id=1, source_target_pairs={{0,8},{8,0},{16,24},{24,16},{1,9},{9,1},{17,25},{25,17},{2,10},{10... | collective-permute-start | bytes 2654216 | tf_op jit(solution)/shard_map/ppermute | solution.py:559
  141.8 41.8 %collective-permute-start.29 = (bf16[3,3,192,768]{3,2,1,0:T(8,128)(2,1)S(1)}, bf16[3,3,192,768]{3,2,1,0:T(8,128)(2,1)}, u32[]{:S(2)}, u32[]{:S(2)}) collective-permute-start(bf16[3,3,192,768]{3,2,1,0:T(8,128)(2,1)S(1)} %pad_maximum_fusion.1.refs_1_.refs_9_), channel_id=1, source_target_pairs={{0,1},{1,0},{2,3},{3,2},{4,5},{5,4},{6,7},{7,6},{8,9},{9,8},{10,11... | collective-permute-start | bytes 7962632 | tf_op jit(solution)/shard_map/ppermute | solution.py:555
  205.2 26.7 %all-to-all-start.4 = ((bf16[4,24,9600]{2,1,0:T(8,128)(2,1)}), bf16[4,24,9600]{2,1,0:T(8,128)(2,1)S(1)}, u32[]{:S(2)}, u32[]{:S(2)}) async-start(bf16[4,24,9600]{2,1,0:T(8,128)(2,1)} %bitcast.86), calls=%async_computation.4 | async-start | bytes 3686400 | tf_op jit(solution)/shard_map/all_to_all | solution.py:862
  257.1 29.8 %collective-permute-start.42 = (bf16[4,4,24,3840]{3,2,1,0:T(8,128)(2,1)}, bf16[4,4,24,3840]{3,2,1,0:T(8,128)(2,1)}, u32[]{:S(2)}, u32[]{:S(2)}) collective-permute-start(bf16[4,4,24,3840]{3,2,1,0:T(8,128)(2,1)} %get-tuple-element.224), channel_id=1, source_target_pairs={{0,1},{1,0},{2,3},{3,2},{4,5},{5,4},{6,7},{7,6},{8,9},{9,8},{10,11... | collective-permute-start | bytes 8847368 | tf_op jit(solution)/shard_map/ppermute | solution.py:555
  257.6 24.1 %collective-permute-start.39 = (bf16[4,24,3072]{2,1,0:T(8,128)(2,1)}, bf16[4,24,3072]{2,1,0:T(8,128)(2,1)S(1)}, u32[]{:S(2)}, u32[]{:S(2)}) collective-permute-start(bf16[4,24,3072]{2,1,0:T(8,128)(2,1)} %get-tuple-element.221), channel_id=1, source_target_pairs={{0,8},{8,0},{16,24},{24,16},{1,9},{9,1},{17,25},{25,17},{2,10},{10... | collective-permute-start | bytes 1769480 | tf_op jit(solution)/shard_map/ppermute | solution.py:559
  259.0 27.8 %collective-permute-start.40 = (bf16[4,24,3072]{2,1,0:T(8,128)(2,1)}, bf16[4,24,3072]{2,1,0:T(8,128)(2,1)S(1)}, u32[]{:S(2)}, u32[]{:S(2)}) collective-permute-start(bf16[4,24,3072]{2,1,0:T(8,128)(2,1)} %get-tuple-element.222), channel_id=1, source_target_pairs={{0,16},{8,24},{16,0},{24,8},{1,17},{9,25},{17,1},{25,9},{2,18},{10... | collective-permute-start | bytes 1769480 | tf_op jit(solution)/shard_map/ppermute | solution.py:559
  260.3 26.6 %collective-permute-start.41 = (bf16[4,24,3072]{2,1,0:T(8,128)(2,1)}, bf16[4,24,3072]{2,1,0:T(8,128)(2,1)}, u32[]{:S(2)}, u32[]{:S(2)}) collective-permute-start(bf16[4,24,3072]{2,1,0:T(8,128)(2,1)} %get-tuple-element.223), channel_id=1, source_target_pairs={{0,24},{8,16},{16,8},{24,0},{1,25},{9,17},{17,9},{25,1},{2,26},{10... | collective-permute-start | bytes 1769480 | tf_op jit(solution)/shard_map/ppermute | solution.py:559
  294.3 29.3 %all-to-all-start.5 = ((bf16[4,24,3072]{2,1,0:T(8,128)(2,1)}), bf16[4,24,3072]{2,1,0:T(8,128)(2,1)S(1)}, u32[]{:S(2)}, u32[]{:S(2)}) async-start(bf16[4,24,3072]{2,1,0:T(8,128)(2,1)} %fusion.5), calls=%async_computation.5 | async-start | bytes 1179648 | tf_op jit(solution)/shard_map/all_to_all | solution.py:647
  299.7 32.9 %collective-permute-start.44 = (bf16[4,24,3840]{2,1,0:T(8,128)(2,1)}, bf16[4,24,3840]{2,1,0:T(8,128)(2,1)}, u32[]{:S(2)}, u32[]{:S(2)}) collective-permute-start(bf16[4,24,3840]{2,1,0:T(8,128)(2,1)} %get-tuple-element.246), channel_id=1, source_target_pairs={{0,8},{8,0},{16,24},{24,16},{1,9},{9,1},{17,25},{25,17},{2,10},{10... | collective-permute-start | bytes 2211848 | tf_op jit(solution)/shard_map/ppermute | solution.py:559
  300.0 33.2 %collective-permute-start.45 = (bf16[4,24,3840]{2,1,0:T(8,128)(2,1)}, bf16[4,24,3840]{2,1,0:T(8,128)(2,1)}, u32[]{:S(2)}, u32[]{:S(2)}) collective-permute-start(bf16[4,24,3840]{2,1,0:T(8,128)(2,1)} %get-tuple-element.247), channel_id=1, source_target_pairs={{0,16},{8,24},{16,0},{24,8},{1,17},{9,25},{17,1},{25,9},{2,18},{10... | collective-permute-start | bytes 2211848 | tf_op jit(solution)/shard_map/ppermute | solution.py:559
  301.8 31.5 %collective-permute-start.46 = (bf16[4,24,3840]{2,1,0:T(8,128)(2,1)S(1)}, bf16[4,24,3840]{2,1,0:T(8,128)(2,1)}, u32[]{:S(2)}, u32[]{:S(2)}) collective-permute-start(bf16[4,24,3840]{2,1,0:T(8,128)(2,1)S(1)} %get-tuple-element.248), channel_id=1, source_target_pairs={{0,24},{8,16},{16,8},{24,0},{1,25},{9,17},{17,9},{25,1},{2,26},{10... | collective-permute-start | bytes 2211848 | tf_op jit(solution)/shard_map/ppermute | solution.py:559
  338.7 32.3 %all-to-all-start.6 = ((bf16[4,24,3840]{2,1,0:T(8,128)(2,1)}), bf16[4,24,3840]{2,1,0:T(8,128)(2,1)S(1)}, u32[]{:S(2)}, u32[]{:S(2)}) async-start(bf16[4,24,3840]{2,1,0:T(8,128)(2,1)} %fusion.2), calls=%async_computation.6 | async-start | bytes 1474560 | tf_op jit(solution)/shard_map/all_to_all | solution.py:647
  344.3 25.9 %collective-permute-start.49 = (bf16[4,24,2688]{2,1,0:T(8,128)(2,1)}, bf16[4,24,2688]{2,1,0:T(8,128)(2,1)S(1)}, u32[]{:S(2)}, u32[]{:S(2)}) collective-permute-start(bf16[4,24,2688]{2,1,0:T(8,128)(2,1)} %get-tuple-element.257), channel_id=1, source_target_pairs={{0,16},{8,24},{16,0},{24,8},{1,17},{9,25},{17,1},{25,9},{2,18},{10... | collective-permute-start | bytes 1548296 | tf_op jit(solution)/shard_map/ppermute | solution.py:559
  345.4 25.7 %collective-permute-start.50 = (bf16[4,24,2688]{2,1,0:T(8,128)(2,1)}, bf16[4,24,2688]{2,1,0:T(8,128)(2,1)}, u32[]{:S(2)}, u32[]{:S(2)}) collective-permute-start(bf16[4,24,2688]{2,1,0:T(8,128)(2,1)} %get-tuple-element.258), channel_id=1, source_target_pairs={{0,24},{8,16},{16,8},{24,0},{1,25},{9,17},{17,9},{25,1},{2,26},{10... | collective-permute-start | bytes 1548296 | tf_op jit(solution)/shard_map/ppermute | solution.py:559
  347.4 35.3 %collective-permute-start.60 = (bf16[24,9216]{1,0:T(8,128)(2,1)S(1)}, bf16[24,9216]{1,0:T(8,128)(2,1)}, u32[]{:S(2)}, u32[]{:S(2)}) collective-permute-start(bf16[24,9216]{1,0:T(8,128)(2,1)S(1)} %slice.232.refs_0_), channel_id=1, source_target_pairs={{0,8},{8,0},{16,24},{24,16},{1,9},{9,1},{17,25},{25,17},{2,10},{10... | collective-permute-start | bytes 1327112 | tf_op jit(solution)/shard_map/ppermute | solution.py:559
  348.2 37.7 %collective-permute-start.61 = (bf16[24,9216]{1,0:T(8,128)(2,1)S(1)}, bf16[24,9216]{1,0:T(8,128)(2,1)}, u32[]{:S(2)}, u32[]{:S(2)}) collective-permute-start(bf16[24,9216]{1,0:T(8,128)(2,1)S(1)} %slice.232.refs_0_), channel_id=1, source_target_pairs={{0,16},{8,24},{16,0},{24,8},{1,17},{9,25},{17,1},{25,9},{2,18},{10... | collective-permute-start | bytes 1327112 | tf_op jit(solution)/shard_map/ppermute | solution.py:559
  358.4 30.7 %collective-permute-start.62 = (bf16[24,9216]{1,0:T(8,128)(2,1)S(1)}, bf16[24,9216]{1,0:T(8,128)(2,1)}, u32[]{:S(2)}, u32[]{:S(2)}) collective-permute-start(bf16[24,9216]{1,0:T(8,128)(2,1)S(1)} %slice.232.refs_0_), channel_id=1, source_target_pairs={{0,24},{8,16},{16,8},{24,0},{1,25},{9,17},{17,9},{25,1},{2,26},{10... | collective-permute-start | bytes 1327112 | tf_op jit(solution)/shard_map/ppermute | solution.py:559
  373.5 31.9 %all-to-all-start.7 = ((bf16[4,24,2688]{2,1,0:T(8,128)(2,1)}), bf16[4,24,2688]{2,1,0:T(8,128)(2,1)S(1)}, u32[]{:S(2)}, u32[]{:S(2)}) async-start(bf16[4,24,2688]{2,1,0:T(8,128)(2,1)} %fusion.8), calls=%async_computation.7 | async-start | bytes 1032192 | tf_op jit(solution)/shard_map/all_to_all | solution.py:647
  (94 other events, 858.1 us)
